TPU v7x, 32 devices: a whole 2x2x4 slice. The times are simulated.
32 devices in a mesh: rep: 2 (over x), seq: 8 (over z, core), chan: 2 (over y).
Axes of the slice: x: 2, y: 2, z: 4, core: 2. Of those that a mesh axis runs over, the one named last changes fastest.
Arguments:
- inputs: bfloat16 [2, 8192, 256], P('rep', 'seq', 'chan'), may hold values from -6 to 6
- cotangent: bfloat16 [2, 8192, 256], P('rep', 'seq', 'chan'), may hold values from -0.046875 to 0.046875
- filter_taps: bfloat16 [8192, 256], P('seq', 'chan'), may hold values from -6 to 6
- out_proj: bfloat16 [256, 256], P('chan'), may hold values from -0.375 to 0.375
Outputs:
- grad_input: bfloat16 [2, 8192, 256], P('rep', 'seq', 'chan')
- grad_filter: float32 [8192, 256], P('seq', 'chan')
All inputs are finite; a program needn't handle non-finite values.
Results may differ from a plain program's by a relative error of at most 0.0049.
Values may be sent and summed in bfloat16 or wider, within the bound.
No kernel may reach another device: no remote copies, remote signals or barrier semaphores. Data moves between devices by JAX's collectives and lax.ppermute only.
A program may use at most 128 MiB of HBM per device.

v0:
```python
import math

import jax
import jax.numpy as jnp
import numpy as np
from jax import lax
from jax.experimental import pallas as pl
from jax.experimental.pallas import tpu as pltpu
from jax.sharding import PartitionSpec as P


LANES = 128
F32 = jnp.float32
BF16 = jnp.bfloat16
VMEM_LIMIT = 48 * 1024 * 1024
CORES = 2
MAX_DIRECT = 4


def split(values):
    high = values.astype(BF16)
    low = (values - high.astype(F32)).astype(BF16)
    return high, low


def split_table(table):
    table = np.asarray(table, np.float32)
    high = table.astype(BF16)
    low = (table - high.astype(np.float32)).astype(BF16)
    return np.stack([high, low])


def phase(numerator, modulus):
    angle = 2.0 * math.pi * np.mod(numerator, modulus) / modulus
    return np.cos(angle), np.sin(angle)


def tables(devices, groups, narrow, tok_rows):
    length = devices * tok_rows
    tiles = tok_rows // LANES
    rows = groups * devices * narrow
    dev = np.arange(devices)
    quarter = 4 * dev + 1
    cos_d, sin_d = phase(quarter[:, None] * dev[None, :], 4 * devices)
    eye_g, eye_c = np.eye(groups), np.eye(narrow)

    def expand(square):
        return np.einsum("gh,jd,ce->gjchde", eye_g, square, eye_c).reshape(rows, rows)

    cos_d, sin_d = expand(cos_d), expand(sin_d)
    first = split_table(np.concatenate([cos_d, -sin_d], axis=0))
    last = split_table(np.concatenate([cos_d.T, -sin_d.T], axis=1) / length)
    local = np.arange(tok_rows)
    cos_r, sin_r = phase(quarter[:, None] * local[None, :], 4 * length)

    def widen(block):
        block = np.broadcast_to(block[None, :, None, :], (groups, devices, narrow, tok_rows))
        return block.reshape(rows, tok_rows)

    turn = np.stack([widen(cos_r), widen(sin_r)]).astype(np.float32)
    lane = np.arange(LANES)
    step = np.arange(tiles)
    cos_s, sin_s = phase(step[:, None] * lane[None, :], tok_rows)
    small = np.stack([cos_s, sin_s]).astype(np.float32)
    cos_b, sin_b = phase(lane[:, None] * lane[None, :], LANES)
    forward = split_table(np.block([[cos_b, -sin_b], [sin_b, cos_b]]))
    inverse = split_table(np.block([[cos_b, sin_b], [-sin_b, cos_b]]))
    return first, last, turn, small, forward, inverse


def butterflies(real_parts, imag_parts, sign):
    size = len(real_parts)
    if size == 1:
        return real_parts, imag_parts
    even_re, even_im = butterflies(real_parts[0::2], imag_parts[0::2], sign)
    odd_re, odd_im = butterflies(real_parts[1::2], imag_parts[1::2], sign)
    low_re, low_im, high_re, high_im = [], [], [], []
    for index in range(size // 2):
        re, im = odd_re[index], odd_im[index]
        if index == 0:
            turned = (re, im)
        elif 4 * index == size:
            turned = (-im, re) if sign > 0 else (im, -re)
        else:
            angle = sign * 2.0 * math.pi * index / size
            c, s = math.cos(angle), math.sin(angle)
            if 8 * index == size:
                turned = ((re - im) * c, (re + im) * c) if sign > 0 else ((re + im) * c, (im - re) * c)
            else:
                turned = (re * c - im * s, re * s + im * c)
        low_re.append(even_re[index] + turned[0])
        low_im.append(even_im[index] + turned[1])
        high_re.append(even_re[index] - turned[0])
        high_im.append(even_im[index] - turned[1])
    return low_re + high_re, low_im + high_im


def dot(lhs, rhs):
    return jnp.dot(lhs, rhs, preferred_element_type=F32)


CHUNK = 16


def transform(block, first, turn, small, forward, stage, high, low, spectrum, rows, all_rows):
    tiles = block.shape[1] // LANES
    if rows == all_rows:
        stage[...] = dot(first[0], block) + dot(first[1], block)
    else:
        for part in range(2):
            pick = pl.ds(part * all_rows, rows)
            stage[part * rows : (part + 1) * rows, :] = dot(first[0, pick, :rows], block) + dot(
                first[1, pick, :rows], block
            )

    def body(index, carry):
        start = pl.multiple_of(index * CHUNK, CHUNK)
        res, ims = [], []
        for tile in range(tiles):
            lanes = pl.ds(tile * LANES, LANES)
            re = stage[pl.ds(start, CHUNK), lanes]
            im = stage[pl.ds(rows + start, CHUNK), lanes]
            c = turn[0, pl.ds(start, CHUNK), lanes]
            s = turn[1, pl.ds(start, CHUNK), lanes]
            res.append(re * c + im * s)
            ims.append(im * c - re * s)
        res, ims = butterflies(res, ims, -1.0)
        for tile in range(tiles):
            re, im = res[tile], ims[tile]
            if tile > 0:
                c, s = small[0, tile : tile + 1, :], small[1, tile : tile + 1, :]
                re, im = re * c + im * s, im * c - re * s
            at = pl.ds(tile * rows + start, CHUNK)
            for part, lanes in ((re, pl.ds(0, LANES)), (im, pl.ds(LANES, LANES))):
                part_high, part_low = split(part)
                high[at, lanes] = part_high
                low[at, lanes] = part_low
        return carry

    lax.fori_loop(0, rows // CHUNK, body, 0)
    count = tiles * rows
    wide = high[:count, :]
    spectrum[...] = dot(wide, forward[0]) + (dot(wide, forward[1]) + dot(low[:count, :], forward[0]))


def untransform(last, turn, small, inverse, stage, high, low, back_high, back_low, rows, all_rows, tiles):
    count = tiles * rows
    wide = high[:count, :]
    stage[:count, :] = dot(wide, inverse[0]) + (dot(wide, inverse[1]) + dot(low[:count, :], inverse[0]))

    def body(index, carry):
        start = pl.multiple_of(index * CHUNK, CHUNK)
        res, ims = [], []
        for tile in range(tiles):
            at = pl.ds(tile * rows + start, CHUNK)
            re = stage[at, pl.ds(0, LANES)]
            im = stage[at, pl.ds(LANES, LANES)]
            if tile > 0:
                c, s = small[0, tile : tile + 1, :], small[1, tile : tile + 1, :]
                re, im = re * c - im * s, im * c + re * s
            res.append(re)
            ims.append(im)
        res, ims = butterflies(res, ims, 1.0)
        for tile in range(tiles):
            lanes = pl.ds(tile * LANES, LANES)
            c = turn[0, pl.ds(start, CHUNK), lanes]
            s = turn[1, pl.ds(start, CHUNK), lanes]
            re, im = res[tile], ims[tile]
            for part, at in ((re * c - im * s, start), (im * c + re * s, rows + start)):
                part_high, part_low = split(part)
                back_high[pl.ds(at, CHUNK), lanes] = part_high
                back_low[pl.ds(at, CHUNK), lanes] = part_low
        return carry

    lax.fori_loop(0, rows // CHUNK, body, 0)
    if rows == all_rows:
        table_high, table_low = last[0], last[1]
    else:
        table_high, table_low = (
            jnp.concatenate([last[k, :rows, :rows], last[k, :rows, all_rows : all_rows + rows]], axis=1)
            for k in range(2)
        )
    right = back_high[: 2 * rows, :]
    return dot(table_high, right) + (dot(table_low, right) + dot(table_high, back_low[: 2 * rows, :]))


def identity(size, dtype):
    row = lax.broadcasted_iota(jnp.int32, (size, size), 0)
    col = lax.broadcasted_iota(jnp.int32, (size, size), 1)
    return (row == col).astype(dtype)


def flipped(left, right):
    return lax.dot_general(left, right, (((1,), (1,)), ((), ())), preferred_element_type=F32)


def per_device_wide(inputs, cotangent, filter_taps, out_proj):
    devices = lax.axis_size("seq")
    groups = lax.axis_size("rep")
    chans = lax.axis_size("chan")
    tok_rows, chan_width = inputs.shape[1:]
    tiles = tok_rows // LANES
    narrow = chan_width // devices
    rows = chan_width
    first, last, turn, small, forward, inverse = (
        jnp.asarray(t) for t in tables(devices, 1, narrow, tok_rows)
    )
    shape = jax.ShapeDtypeStruct

    def call(kernel, out_shape, scratch=(), cost=3 * 10**6):
        return pl.pallas_call(
            kernel,
            out_shape=out_shape,
            scratch_shapes=scratch,
            compiler_params=pltpu.CompilerParams(vmem_limit_bytes=VMEM_LIMIT),
            cost_estimate=pl.CostEstimate(flops=10**8, bytes_accessed=cost, transcendentals=0),
        )

    def pieces(width):
        return (shape((devices, narrow, width), BF16),)

    def put(out_refs, source, lanes):
        out_refs[0][:, :, lanes] = source[...].reshape(devices, narrow, tok_rows).astype(BF16)

    def take(in_refs, lanes, block):
        block[...] = in_refs[0][:, :, lanes].astype(F32).reshape(rows, tok_rows).astype(BF16)

    def exchange(sent):
        return (lax.all_to_all(sent[0], "seq", split_axis=0, concat_axis=0, tiled=True),)

    count = 1
    front, behind = pl.ds(0, tok_rows), pl.ds(tok_rows, tok_rows)
    flat = pltpu.VMEM((rows, tok_rows), F32)
    block_scratch = pltpu.VMEM((rows, tok_rows), BF16)
    half_pair = [
        pltpu.VMEM((tiles * rows, 2 * LANES), BF16),
        pltpu.VMEM((tiles * rows, 2 * LANES), BF16),
    ]
    back_pair = [
        pltpu.VMEM((2 * rows, tok_rows), BF16),
        pltpu.VMEM((2 * rows, tok_rows), BF16),
    ]
    stage_scratch = pltpu.VMEM((2 * rows, tok_rows), F32)
    spec_shape = shape((tiles * rows, 2 * LANES), F32)
    spec_scratch = pltpu.VMEM((tiles * rows, 2 * LANES), F32)

    def pack_kernel(input_ref, taps_ref, *refs):
        *out_refs, wide = refs
        eye = identity(chan_width, BF16)
        wide[...] = flipped(eye, input_ref[...])
        put(out_refs, wide, front)
        wide[...] = flipped(eye, taps_ref[...])
        put(out_refs, wide, behind)

    def mix_kernel(own_ref, other_ref, proj_ref, *refs):
        *out_refs, wide = refs
        chan = lax.axis_index("chan")
        own = pl.ds(pl.multiple_of(chan * chan_width, chan_width), chan_width)
        other = pl.ds(pl.multiple_of((1 - chan) * chan_width, chan_width), chan_width)
        wide[...] = flipped(proj_ref[:, own], own_ref[...]) + flipped(proj_ref[:, other], other_ref[...])
        put(out_refs, wide, front)

    def early_kernel(*refs):
        recv, (first, turn, small, forward, input_ref, taps_ref, block, stage, high, low) = (
            refs[:count], refs[count:],
        )
        for lanes, spectrum in ((front, input_ref), (behind, taps_ref)):
            take(recv, lanes, block)
            transform(block[...], first, turn, small, forward, stage, high, low, spectrum, rows, rows)

    real, imag = pl.ds(0, LANES), pl.ds(LANES, LANES)

    def multiply(grad, other, high, low):
        def body(tile, carry):
            at = pl.ds(pl.multiple_of(tile * rows, rows), rows)
            gr, gi = grad[at, real], grad[at, imag]
            kr, ki = other[at, real], other[at, imag]
            for part, lanes in ((gr * kr + gi * ki, real), (gi * kr - gr * ki, imag)):
                part_high, part_low = split(part)
                high[at, lanes] = part_high
                low[at, lanes] = part_low
            return carry

        lax.fori_loop(0, tiles, body, 0)

    def filter_kernel(*refs):
        recv, rest = refs[:count], refs[count:]
        (input_ref, first, last, turn, small, forward, inverse, grad, out_ref,
         block, stage, high, low, back, back_high, back_low) = rest
        take(recv, front, block)
        transform(block[...], first, turn, small, forward, stage, high, low, grad, rows, rows)
        multiply(grad, input_ref, high, low)
        value = untransform(
            last, turn, small, inverse, back, high, low, back_high, back_low, rows, rows, tiles
        )
        out_ref[...] = value.astype(BF16)

    def input_kernel(grad, taps_ref, last, turn, small, inverse, *refs):
        *out_refs, high, low, back, back_high, back_low, wide = refs
        multiply(grad, taps_ref, high, low)
        wide[...] = untransform(
            last, turn, small, inverse, back, high, low, back_high, back_low, rows, rows, tiles
        )
        put(out_refs, wide, front)

    def sum_kernel(own_ref, other_ref, *refs):
        *out_refs, wide = refs
        wide[...] = own_ref[...].astype(F32) + other_ref[...].astype(F32)
        put(out_refs, wide, front)

    def final_kernel(*refs):
        *recv, out_ref, block = refs
        take(recv, front, block)
        moved = lax.dot_general(
            block[...], identity(chan_width, BF16), (((0,), (0,)), ((), ())), preferred_element_type=F32
        )
        out_ref[...] = moved.astype(out_ref.dtype)

    own = cotangent.reshape(tok_rows, chan_width)
    other = lax.ppermute(own, "chan", [(k, (k + 1) % chans) for k in range(chans)])
    early = exchange(
        call(pack_kernel, pieces(2 * tok_rows), [flat])(inputs.reshape(tok_rows, chan_width), filter_taps)
    )
    late = exchange(call(mix_kernel, pieces(tok_rows), [flat])(own, other, out_proj))
    input_spec, taps_spec = call(
        early_kernel, (spec_shape, spec_shape), [block_scratch, stage_scratch] + half_pair, 9 * 10**6
    )(*early, first, turn, small, forward)
    grad_spec, partial = call(
        filter_kernel,
        (spec_shape, shape((rows, tok_rows), BF16)),
        [block_scratch, stage_scratch] + half_pair + [spec_scratch] + back_pair,
        9 * 10**6,
    )(*late, input_spec, first, last, turn, small, forward, inverse)
    partial_other = lax.ppermute(partial, "rep", [(k, (k + 1) % groups) for k in range(groups)])
    input_back = exchange(
        call(input_kernel, pieces(tok_rows), half_pair + [spec_scratch] + back_pair + [flat], 6 * 10**6)(
            grad_spec, taps_spec, last, turn, small, inverse
        )
    )
    filter_back = exchange(call(sum_kernel, pieces(tok_rows), [flat])(partial, partial_other))
    grad_input = call(final_kernel, shape((tok_rows, chan_width), BF16), [block_scratch])(*input_back)
    grad_filter = call(final_kernel, shape((tok_rows, chan_width), F32), [block_scratch])(*filter_back)
    return grad_input.reshape(1, tok_rows, chan_width), grad_filter


def per_device_near(inputs, cotangent, filter_taps, out_proj):
    devices = lax.axis_size("seq")
    tok_rows, chan_width = inputs.shape[1:]
    tiles = tok_rows // LANES
    narrow = chan_width // devices
    rows = chan_width
    chips = devices // CORES
    wide_rows = CORES * narrow
    half = chips * narrow
    first, last, turn, small, forward, inverse = (
        jnp.asarray(t) for t in tables(devices, 1, narrow, tok_rows)
    )
    shape = jax.ShapeDtypeStruct
    swap_pairs = [(k, k ^ 1) for k in range(devices)]

    def call(kernel, out_shape, scratch=(), cost=3 * 10**6):
        return pl.pallas_call(
            kernel,
            out_shape=out_shape,
            scratch_shapes=scratch,
            compiler_params=pltpu.CompilerParams(vmem_limit_bytes=VMEM_LIMIT),
            cost_estimate=pl.CostEstimate(flops=10**8, bytes_accessed=cost, transcendentals=0),
        )

    def swap(value):
        return lax.ppermute(value, "seq", swap_pairs)

    def cross(value, axis):
        size = lax.axis_size(axis)
        return lax.ppermute(value, axis, [(k, (k + 1) % size) for k in range(size)])

    def exchange(sent):
        got = [sent[0]]
        for offset in range(1, chips):
            pairs = [(k, k ^ (offset * CORES)) for k in range(devices)]
            got.append(lax.ppermute(sent[offset], "seq", pairs))
        return tuple(got)

    def place():
        at = lax.axis_index("seq")
        return at // CORES, at % CORES

    def pieces(width):
        return tuple(shape((CORES, narrow, width), BF16) for _ in range(chips))

    front, behind = pl.ds(0, tok_rows), pl.ds(tok_rows, tok_rows)
    block_scratch = pltpu.VMEM((rows, tok_rows), BF16)
    half_pair = [
        pltpu.VMEM((tiles * rows, 2 * LANES), BF16),
        pltpu.VMEM((tiles * rows, 2 * LANES), BF16),
    ]
    back_pair = [
        pltpu.VMEM((2 * rows, tok_rows), BF16),
        pltpu.VMEM((2 * rows, tok_rows), BF16),
    ]
    stage_scratch = pltpu.VMEM((2 * rows, tok_rows), F32)
    spec_shape = shape((tiles * rows, 2 * LANES), F32)
    spec_scratch = pltpu.VMEM((tiles * rows, 2 * LANES), F32)
    flat = pltpu.VMEM((rows, tok_rows), F32)
    half_scratch = pltpu.VMEM((half, tok_rows), F32)
    halves = (shape((chips, narrow, tok_rows), BF16), shape((chips, narrow, tok_rows), BF16))

    def put(out_refs, source, side, lanes):
        chip, _ = place()
        for offset in range(chips):
            at = pl.multiple_of((chip ^ offset) * narrow, narrow)
            out_refs[offset][pl.ds(side, 1), :, lanes] = (
                source[pl.ds(at, narrow), :].reshape(1, narrow, tok_rows).astype(BF16)
            )

    def take(in_refs, lanes, block):
        chip, _ = place()
        for offset in range(chips):
            at = pl.multiple_of((chip ^ offset) * wide_rows, wide_rows)
            for core in range(CORES):
                block[pl.ds(at + core * narrow, narrow), :] = in_refs[offset][core, :, lanes]

    def cut(source, mine_ref, theirs_ref):
        _, core = place()
        for chip in range(chips):
            for ref, side in ((mine_ref, core), (theirs_ref, 1 - core)):
                at = pl.multiple_of(chip * wide_rows + side * narrow, narrow)
                ref[chip] = source[pl.ds(at, narrow), :].astype(BF16)

    def chosen(core):
        row = lax.broadcasted_iota(jnp.int32, (half, chan_width), 0)
        col = lax.broadcasted_iota(jnp.int32, (half, chan_width), 1)
        pick = (row // narrow) * wide_rows + core * narrow + row % narrow
        return (pick == col).astype(F32).astype(BF16)

    def pack_kernel(input_ref, input_near, taps_ref, taps_near, *refs):
        *out_refs, wide = refs
        _, core = place()
        pick = chosen(core)
        for own_ref, near_ref, lanes in ((input_ref, input_near, front), (taps_ref, taps_near, behind)):
            for ref, side in ((own_ref, core), (near_ref, 1 - core)):
                wide[...] = flipped(pick, ref[...])
                put(out_refs, wide, side, lanes)

    def own_kernel(own_ref, near_ref, proj_ref, part_ref, part_near, other_ref):
        chan = lax.axis_index("chan")
        _, core = place()
        picked = [
            proj_ref[pl.ds(pl.multiple_of(chip * wide_rows + core * narrow, narrow), narrow), :]
            for chip in range(chips)
        ]
        held = jnp.concatenate(picked, axis=0)
        swapped = jnp.concatenate([held[:, chan_width:], held[:, :chan_width]], axis=1)
        held = jnp.where(chan == 0, held, swapped)
        part_ref[...] = flipped(held[:, :chan_width], own_ref[...])
        part_near[...] = flipped(held[:, :chan_width], near_ref[...])
        other_ref[...] = held[:, chan_width:]

    def mix_kernel(part_ref, part_near, proj_ref, other_ref, other_near, *refs):
        *out_refs, wide = refs
        _, core = place()
        for part, ref, side in ((part_ref, other_ref, core), (part_near, other_near, 1 - core)):
            wide[...] = part[...] + flipped(proj_ref[...], ref[...])
            put(out_refs, wide, side, front)

    def early_kernel(*refs):
        recv, rest = refs[:chips], refs[chips:]
        first, turn, small, forward, input_ref, taps_ref, block, stage, high, low = rest
        for lanes, spectrum in ((front, input_ref), (behind, taps_ref)):
            take(recv, lanes, block)
            transform(block[...], first, turn, small, forward, stage, high, low, spectrum, rows, rows)

    real, imag = pl.ds(0, LANES), pl.ds(LANES, LANES)

    def multiply(grad, other, high, low):
        def body(tile, carry):
            at = pl.ds(pl.multiple_of(tile * rows, rows), rows)
            gr, gi = grad[at, real], grad[at, imag]
            kr, ki = other[at, real], other[at, imag]
            for part, lanes in ((gr * kr + gi * ki, real), (gi * kr - gr * ki, imag)):
                part_high, part_low = split(part)
                high[at, lanes] = part_high
                low[at, lanes] = part_low
            return carry

        lax.fori_loop(0, tiles, body, 0)

    def filter_kernel(*refs):
        recv, rest = refs[:chips], refs[chips:]
        (input_ref, first, last, turn, small, forward, inverse, grad, mine_ref, theirs_ref,
         block, stage, high, low, back, back_high, back_low, wide) = rest
        take(recv, front, block)
        transform(block[...], first, turn, small, forward, stage, high, low, grad, rows, rows)
        multiply(grad, input_ref, high, low)
        wide[...] = untransform(
            last, turn, small, inverse, back, high, low, back_high, back_low, rows, rows, tiles
        )
        cut(wide, mine_ref, theirs_ref)

    def input_kernel(grad, taps_ref, last, turn, small, inverse, mine_ref, theirs_ref, *scratch):
        high, low, back, back_high, back_low, wide = scratch
        multiply(grad, taps_ref, high, low)
        wide[...] = untransform(
            last, turn, small, inverse, back, high, low, back_high, back_low, rows, rows, tiles
        )
        cut(wide, mine_ref, theirs_ref)

    def join_kernel(mine_ref, near_ref, *out_refs):
        chip, core = place()
        for offset in range(chips):
            for ref, side in ((mine_ref, core), (near_ref, 1 - core)):
                out_refs[offset][pl.ds(side, 1)] = ref[pl.ds(chip ^ offset, 1)]

    def sum_kernel(mine_ref, mine_other, near_ref, near_other, *out_refs):
        chip, core = place()
        for offset in range(chips):
            at = pl.ds(chip ^ offset, 1)
            for ref, other, side in ((mine_ref, mine_other, core), (near_ref, near_other, 1 - core)):
                total = ref[at].astype(F32) + other[at].astype(F32)
                out_refs[offset][pl.ds(side, 1)] = total.astype(BF16)

    def final_kernel(*refs):
        *recv, out_ref, block = refs
        take(recv, front, block)
        moved = lax.dot_general(
            block[...], identity(chan_width, BF16), (((0,), (0,)), ((), ())), preferred_element_type=F32
        )
        out_ref[...] = moved.astype(out_ref.dtype)

    signal = inputs.reshape(tok_rows, chan_width)
    own = cotangent.reshape(tok_rows, chan_width)
    signal_near = swap(signal)
    taps_near = swap(filter_taps)
    other = cross(own, "chan")
    own_near = swap(own)
    early = exchange(
        call(pack_kernel, pieces(2 * tok_rows), [half_scratch])(signal, signal_near, filter_taps, taps_near),
    )
    part_shape = shape((half, tok_rows), F32)
    part, part_near, proj_other = call(
        own_kernel, (part_shape, part_shape, shape((half, chan_width), BF16))
    )(own, own_near, out_proj)
    other_near = swap(other)
    late = exchange(call(mix_kernel, pieces(tok_rows), [half_scratch])(part, part_near, proj_other, other, other_near))
    input_spec, taps_spec = call(
        early_kernel, (spec_shape, spec_shape), [block_scratch, stage_scratch] + half_pair, 9 * 10**6
    )(*early, first, turn, small, forward)
    grad_spec, mine, theirs = call(
        filter_kernel,
        (spec_shape,) + halves,
        [block_scratch, stage_scratch] + half_pair + [spec_scratch] + back_pair + [flat],
        9 * 10**6,
    )(*late, input_spec, first, last, turn, small, forward, inverse)
    mine_other = cross(mine, "rep")
    near = swap(theirs)
    near_other = cross(near, "rep")
    input_mine, input_theirs = call(
        input_kernel, halves, half_pair + [spec_scratch] + back_pair + [flat], 6 * 10**6
    )(grad_spec, taps_spec, last, turn, small, inverse)
    input_near = swap(input_theirs)
    input_back = exchange(call(join_kernel, pieces(tok_rows))(input_mine, input_near))
    filter_back = exchange(call(sum_kernel, pieces(tok_rows))(mine, mine_other, near, near_other))
    grad_input = call(final_kernel, shape((tok_rows, chan_width), BF16), [block_scratch])(*input_back)
    grad_filter = call(final_kernel, shape((tok_rows, chan_width), F32), [block_scratch])(*filter_back)
    return grad_input.reshape(1, tok_rows, chan_width), grad_filter


def solution(mesh):
    few = mesh.shape["seq"] == CORES * MAX_DIRECT
    body = per_device_near if few else per_device_wide

    return jax.shard_map(
        body,
        mesh=mesh,
        in_specs=(
            P("rep", "seq", "chan"),
            P("rep", "seq", "chan"),
            P("seq", "chan"),
            P("chan", None),
        ),
        out_specs=(P("rep", "seq", "chan"), P("seq", "chan")),
        check_vma=False,
    )
```

profile of v0, /device:TPU:0, one launch (start us, length us, event | category | flops | bytes accessed | tf_op | source)
XLA Modules:
  0.0 61.0 jit_solution(7605387348833023560)
XLA Ops:
  0.6 3.1 %collective-permute-start.1 = (bf16[1024,128]{1,0:T(8,128)(2,1)}, bf16[1024,128]{1,0:T(8,128)(2,1)S(1)}, u32[]{:S(2)}, u32[]{:S(2)}) collective-permute-start(bf16[1024,128]{1,0:T(8,128)(2,1)} %bitcast.3), channel_id=1, source_target_pairs={{0,1},{1,0},{2,3},{3,2},{4,5},{5,4},{6,7},{7,6},{8,9},{9,8},{10,11... | collective-permute-start | bytes 786440 | tf_op jit(solution)/shard_map/ppermute | solution.py:375
  3.7 0.0 collective-permute-start.6
  3.7 0.5 collective-permute-start.7
  4.2 0.0 collective-permute-start
  4.2 6.0 %collective-permute-done.1.other_ref = bf16[1024,128]{1,0:T(8,128)(2,1)S(1)} collective-permute-done((bf16[1024,128]{1,0:T(8,128)(2,1)}, bf16[1024,128]{1,0:T(8,128)(2,1)S(1)}, u32[]{:S(2)}, u32[]{:S(2)}) %collective-permute-start.1) | collective-permute-done | bytes 262176 | tf_op jit(solution)/shard_map/ppermute | solution.py:375
  10.2 0.0 collective-permute-start.2
  10.2 0.0 collective-permute-done.6.input_near
  10.2 0.0 collective-permute-done.7.taps_near
  10.2 0.9 %copy-done.6 = bf16[1,1024,128]{2,1,0:T(8,128)(2,1)S(1)} copy-done((bf16[1,1024,128]{2,1,0:T(8,128)(2,1)S(1)}, bf16[1,1024,128]{2,1,0:T(8,128)(2,1)}, u32[]{:S(2)}) %copy-start.6) | copy-done | bytes 262168
  11.2 0.9 %copy-done.7 = bf16[1024,128]{1,0:T(8,128)(2,1)S(1)} copy-done((bf16[1024,128]{1,0:T(8,128)(2,1)S(1)}, bf16[1024,128]{1,0:T(8,128)(2,1)}, u32[]{:S(2)}) %copy-start.7) | copy-done | bytes 262168
  12.1 0.5 shard_map.115
  12.6 0.0 copy-start
  12.6 1.9 %collective-permute-start.8 = (bf16[2,16,2048]{2,1,0:T(8,128)(2,1)S(1)}, bf16[2,16,2048]{2,1,0:T(8,128)(2,1)S(1)}, u32[]{:S(2)}, u32[]{:S(2)}) collective-permute-start(bf16[2,16,2048]{2,1,0:T(8,128)(2,1)S(1)} %get-tuple-element.36), channel_id=1, source_target_pairs={{0,4},{2,6},{4,0},{6,2},{8,12},{10,14},{12,8},{14,10},{1,5},{3,7},... | collective-permute-start | bytes 393224 | tf_op jit(solution)/shard_map/ppermute | solution.py:381
  14.5 2.6 %collective-permute-start.9 = (bf16[2,16,2048]{2,1,0:T(8,128)(2,1)S(1)}, bf16[2,16,2048]{2,1,0:T(8,128)(2,1)S(1)}, u32[]{:S(2)}, u32[]{:S(2)}) collective-permute-start(bf16[2,16,2048]{2,1,0:T(8,128)(2,1)S(1)} %get-tuple-element.37), channel_id=1, source_target_pairs={{0,8},{2,10},{4,12},{6,14},{8,0},{10,2},{12,4},{14,6},{1,9},{3,11}... | collective-permute-start | bytes 393224 | tf_op jit(solution)/shard_map/ppermute | solution.py:381
  17.1 0.3 shard_map.113
  17.4 0.0 collective-permute-done.2.other_near
  17.4 0.0 copy-start.2
  17.4 0.0 copy-start.4
  17.5 0.0 copy-start.8
  17.5 0.3 shard_map.114
  17.8 0.9 %collective-permute-start.3 = (bf16[2,16,1024]{2,1,0:T(8,128)(2,1)S(1)}, bf16[2,16,1024]{2,1,0:T(8,128)(2,1)S(1)}, u32[]{:S(2)}, u32[]{:S(2)}) collective-permute-start(bf16[2,16,1024]{2,1,0:T(8,128)(2,1)S(1)} %get-tuple-element.32), channel_id=1, source_target_pairs={{0,4},{2,6},{4,0},{6,2},{8,12},{10,14},{12,8},{14,10},{1,5},{3,7},... | collective-permute-start | bytes 196616 | tf_op jit(solution)/shard_map/ppermute | solution.py:381
  18.7 3.5 %collective-permute-start.4 = (bf16[2,16,1024]{2,1,0:T(8,128)(2,1)S(1)}, bf16[2,16,1024]{2,1,0:T(8,128)(2,1)S(1)}, u32[]{:S(2)}, u32[]{:S(2)}) collective-permute-start(bf16[2,16,1024]{2,1,0:T(8,128)(2,1)S(1)} %get-tuple-element.33), channel_id=1, source_target_pairs={{0,8},{2,10},{4,12},{6,14},{8,0},{10,2},{12,4},{14,6},{1,9},{3,11}... | collective-permute-start | bytes 196616 | tf_op jit(solution)/shard_map/ppermute | solution.py:381
  22.2 0.0 collective-permute-done.8.refs_1_
  22.2 1.8 %collective-permute-start.5 = (bf16[2,16,1024]{2,1,0:T(8,128)(2,1)S(1)}, bf16[2,16,1024]{2,1,0:T(8,128)(2,1)S(1)}, u32[]{:S(2)}, u32[]{:S(2)}) collective-permute-start(bf16[2,16,1024]{2,1,0:T(8,128)(2,1)S(1)} %get-tuple-element.34), channel_id=1, source_target_pairs={{0,12},{2,14},{4,8},{6,10},{8,4},{10,6},{12,0},{14,2},{1,13},{3,15... | collective-permute-start | bytes 196616 | tf_op jit(solution)/shard_map/ppermute | solution.py:381
  24.1 3.4 %collective-permute-done.9.refs_2_ = bf16[2,16,2048]{2,1,0:T(8,128)(2,1)S(1)} collective-permute-done((bf16[2,16,2048]{2,1,0:T(8,128)(2,1)S(1)}, bf16[2,16,2048]{2,1,0:T(8,128)(2,1)S(1)}, u32[]{:S(2)}, u32[]{:S(2)}) %collective-permute-start.9) | collective-permute-done | bytes 131104 | tf_op jit(solution)/shard_map/ppermute | solution.py:381
  27.4 0.0 collective-permute-done.10.refs_3_
  27.5 0.0 copy-start.1
  27.5 0.0 copy-start.3
  27.5 3.3 %shard_map.116 = (f32[1024,256]{1,0:T(8,128)S(1)}, f32[1024,256]{1,0:T(8,128)S(1)}) custom-call(bf16[2,16,2048]{2,1,0:T(8,128)(2,1)S(1)} %get-tuple-element.35.refs_0_, bf16[2,16,2048]{2,1,0:T(8,128)(2,1)S(1)} %collective-permute-done.8.refs_1_, bf16[2,16,2048]{2,1,0:T(8,128)(2,1)S(1)} %collective-permute-done.9.refs_2_, ...), custom_call_target="tpu_custom_call" | custom-call | flops 100000000 | bytes 9000000 | tf_op jit(solution)/shard_map/pallas_call | solution.py:545
  30.8 0.0 collective-permute-done.3.refs_1_
  30.8 3.6 %collective-permute-done.4.refs_2_ = bf16[2,16,1024]{2,1,0:T(8,128)(2,1)S(1)} collective-permute-done((bf16[2,16,1024]{2,1,0:T(8,128)(2,1)S(1)}, bf16[2,16,1024]{2,1,0:T(8,128)(2,1)S(1)}, u32[]{:S(2)}, u32[]{:S(2)}) %collective-permute-start.4) | collective-permute-done | bytes 65568 | tf_op jit(solution)/shard_map/ppermute | solution.py:381
  34.4 4.3 %shard_map.117 = (f32[1024,256]{1,0:T(8,128)S(1)}, bf16[4,16,1024]{2,1,0:T(8,128)(2,1)S(1)}, bf16[4,16,1024]{2,1,0:T(8,128)(2,1)S(1)}) custom-call(bf16[2,16,1024]{2,1,0:T(8,128)(2,1)S(1)} %get-tuple-element.31.refs_0_, bf16[2,16,1024]{2,1,0:T(8,128)(2,1)S(1)} %collective-permute-done.3.refs_1_, bf16[2,16,1024]{2,1,0:T(8,128)(2,1)S(1)} %collective-permute-done.4.refs_2_, ...), custom_call_target="tpu_custom_call" | custom-call | flops 100000000 | bytes 9000000 | tf_op jit(solution)/shard_map/pallas_call | solution.py:548
  38.7 0.1 collective-permute-start.16
  38.8 2.3 %shard_map.118 = (bf16[4,16,1024]{2,1,0:T(8,128)(2,1)S(1)}, bf16[4,16,1024]{2,1,0:T(8,128)(2,1)S(1)}) custom-call(f32[1024,256]{1,0:T(8,128)S(1)} %get-tuple-element.40.grad, f32[1024,256]{1,0:T(8,128)S(1)} %get-tuple-element.41.taps_ref, bf16[2,128,256]{2,1,0:T(8,128)(2,1)S(1)} %copy-done.3, f32[2,128,1024]{2,1,0:T(8,128)S(1)} %copy-done, ...), custom_call_target="tpu_custom_call" | custom-call | flops 100000000 | bytes 6000000 | tf_op jit(solution)/shard_map/pallas_call | solution.py:557
  41.1 0.5 collective-permute-start.11
  41.6 1.5 %collective-permute-start.15 = (bf16[4,16,1024]{2,1,0:T(8,128)(2,1)S(1)}, bf16[4,16,1024]{2,1,0:T(8,128)(2,1)S(1)}, u32[]{:S(2)}, u32[]{:S(2)}) collective-permute-start(bf16[4,16,1024]{2,1,0:T(8,128)(2,1)S(1)} %get-tuple-element.48.mine_ref), channel_id=1, source_target_pairs={{0,16},{16,0},{1,17},{17,1},{2,18},{18,2},{3,19},{19,3},{4,20},{20... | collective-permute-start | bytes 393224 | tf_op jit(solution)/shard_map/ppermute | solution.py:375
  43.1 0.5 collective-permute-start.17
  43.7 2.6 %collective-permute-start.12 = (bf16[2,16,1024]{2,1,0:T(8,128)(2,1)S(1)}, bf16[2,16,1024]{2,1,0:T(8,128)(2,1)S(1)}, u32[]{:S(2)}, u32[]{:S(2)}) collective-permute-start(bf16[2,16,1024]{2,1,0:T(8,128)(2,1)S(1)} %get-tuple-element.45), channel_id=1, source_target_pairs={{0,4},{2,6},{4,0},{6,2},{8,12},{10,14},{12,8},{14,10},{1,5},{3,7},... | collective-permute-start | bytes 196616 | tf_op jit(solution)/shard_map/ppermute | solution.py:381
  46.3 1.1 %collective-permute-start.13 = (bf16[2,16,1024]{2,1,0:T(8,128)(2,1)S(1)}, bf16[2,16,1024]{2,1,0:T(8,128)(2,1)S(1)}, u32[]{:S(2)}, u32[]{:S(2)}) collective-permute-start(bf16[2,16,1024]{2,1,0:T(8,128)(2,1)S(1)} %get-tuple-element.46), channel_id=1, source_target_pairs={{0,8},{2,10},{4,12},{6,14},{8,0},{10,2},{12,4},{14,6},{1,9},{3,11}... | collective-permute-start | bytes 196616 | tf_op jit(solution)/shard_map/ppermute | solution.py:381
  47.4 1.4 %collective-permute-start.14 = (bf16[2,16,1024]{2,1,0:T(8,128)(2,1)S(1)}, bf16[2,16,1024]{2,1,0:T(8,128)(2,1)S(1)}, u32[]{:S(2)}, u32[]{:S(2)}) collective-permute-start(bf16[2,16,1024]{2,1,0:T(8,128)(2,1)S(1)} %get-tuple-element.47), channel_id=1, source_target_pairs={{0,12},{2,14},{4,8},{6,10},{8,4},{10,6},{12,0},{14,2},{1,13},{3,15... | collective-permute-start | bytes 196616 | tf_op jit(solution)/shard_map/ppermute | solution.py:381
  48.8 1.1 %collective-permute-done.17.near_other = bf16[4,16,1024]{2,1,0:T(8,128)(2,1)S(1)} collective-permute-done((bf16[4,16,1024]{2,1,0:T(8,128)(2,1)S(1)}, bf16[4,16,1024]{2,1,0:T(8,128)(2,1)S(1)}, u32[]{:S(2)}, u32[]{:S(2)}) %collective-permute-start.17) | collective-permute-done | bytes 131104 | tf_op jit(solution)/shard_map/ppermute | solution.py:375
  49.9 0.1 shard_map.121
  50.0 2.6 %collective-permute-start.18 = (bf16[2,16,1024]{2,1,0:T(8,128)(2,1)S(1)}, bf16[2,16,1024]{2,1,0:T(8,128)(2,1)S(1)}, u32[]{:S(2)}, u32[]{:S(2)}) collective-permute-start(bf16[2,16,1024]{2,1,0:T(8,128)(2,1)S(1)} %get-tuple-element.51), channel_id=1, source_target_pairs={{0,4},{2,6},{4,0},{6,2},{8,12},{10,14},{12,8},{14,10},{1,5},{3,7},... | collective-permute-start | bytes 196616 | tf_op jit(solution)/shard_map/ppermute | solution.py:381
  52.6 1.1 %collective-permute-start.19 = (bf16[2,16,1024]{2,1,0:T(8,128)(2,1)S(1)}, bf16[2,16,1024]{2,1,0:T(8,128)(2,1)S(1)}, u32[]{:S(2)}, u32[]{:S(2)}) collective-permute-start(bf16[2,16,1024]{2,1,0:T(8,128)(2,1)S(1)} %get-tuple-element.52), channel_id=1, source_target_pairs={{0,8},{2,10},{4,12},{6,14},{8,0},{10,2},{12,4},{14,6},{1,9},{3,11}... | collective-permute-start | bytes 196616 | tf_op jit(solution)/shard_map/ppermute | solution.py:381
  53.7 1.4 %collective-permute-start.20 = (bf16[2,16,1024]{2,1,0:T(8,128)(2,1)S(1)}, bf16[2,16,1024]{2,1,0:T(8,128)(2,1)S(1)}, u32[]{:S(2)}, u32[]{:S(2)}) collective-permute-start(bf16[2,16,1024]{2,1,0:T(8,128)(2,1)S(1)} %get-tuple-element.53), channel_id=1, source_target_pairs={{0,12},{2,14},{4,8},{6,10},{8,4},{10,6},{12,0},{14,2},{1,13},{3,15... | collective-permute-start | bytes 196616 | tf_op jit(solution)/shard_map/ppermute | solution.py:381
  55.1 1.0 %shard_map.120 = bf16[1024,128]{1,0:T(8,128)(2,1)} custom-call(bf16[2,16,1024]{2,1,0:T(8,128)(2,1)S(1)} %get-tuple-element.44.refs_0_, bf16[2,16,1024]{2,1,0:T(8,128)(2,1)S(1)} %collective-permute-done.12.refs_1_, bf16[2,16,1024]{2,1,0:T(8,128)(2,1)S(1)} %collective-permute-done.13.refs_2_, bf16[2,16,1024]{2,1,0:T(8,128)(2,1)S(1)} %collective-permute-done.14.refs_3_), custom_call_target="tpu_custom_call" | custom-call | flops 100000000 | bytes 3000000 | tf_op jit(solution)/shard_map/pallas_call | solution.py:563
  56.1 3.8 %collective-permute-done.19.refs_2_ = bf16[2,16,1024]{2,1,0:T(8,128)(2,1)S(1)} collective-permute-done((bf16[2,16,1024]{2,1,0:T(8,128)(2,1)S(1)}, bf16[2,16,1024]{2,1,0:T(8,128)(2,1)S(1)}, u32[]{:S(2)}, u32[]{:S(2)}) %collective-permute-start.19) | collective-permute-done | bytes 65568 | tf_op jit(solution)/shard_map/ppermute | solution.py:381
  60.0 1.1 %shard_map.122 = f32[1024,128]{1,0:T(8,128)} custom-call(bf16[2,16,1024]{2,1,0:T(8,128)(2,1)S(1)} %get-tuple-element.50.refs_0_, bf16[2,16,1024]{2,1,0:T(8,128)(2,1)S(1)} %collective-permute-done.18.refs_1_, bf16[2,16,1024]{2,1,0:T(8,128)(2,1)S(1)} %collective-permute-done.19.refs_2_, bf16[2,16,1024]{2,1,0:T(8,128)(2,1)S(1)} %collective-permute-done.20.refs_3_), custom_call_target="tpu_custom_call" | custom-call | flops 100000000 | bytes 3000000 | tf_op jit(solution)/shard_map/pallas_call | solution.py:564
  (24 shorter events, 0.1 us)
Async XLA Ops:
  0.6 9.6 %collective-permute-start.1 = (bf16[1024,128]{1,0:T(8,128)(2,1)}, bf16[1024,128]{1,0:T(8,128)(2,1)S(1)}, u32[]{:S(2)}, u32[]{:S(2)}) collective-permute-start(bf16[1024,128]{1,0:T(8,128)(2,1)} %bitcast.3), channel_id=1, source_target_pairs={{0,1},{1,0},{2,3},{3,2},{4,5},{5,4},{6,7},{7,6},{8,9},{9,8},{10,11... | collective-permute-start | bytes 786440 | tf_op jit(solution)/shard_map/ppermute | solution.py:375
  3.7 13.4 %copy-start.5 = (bf16[1,1024,128]{2,1,0:T(8,128)(2,1)S(1)}, bf16[1,1024,128]{2,1,0:T(8,128)(2,1)}, u32[]{:S(2)}) copy-start(bf16[1,1024,128]{2,1,0:T(8,128)(2,1)} %param.11) | copy-start | bytes 786436
  3.7 6.5 %collective-permute-start.6 = (bf16[1024,128]{1,0:T(8,128)(2,1)}, bf16[1024,128]{1,0:T(8,128)(2,1)S(1)}, u32[]{:S(2)}, u32[]{:S(2)}) collective-permute-start(bf16[1024,128]{1,0:T(8,128)(2,1)} %bitcast.6), channel_id=1, source_target_pairs={{0,2},{2,0},{4,6},{6,4},{8,10},{10,8},{12,14},{14,12},{1,3},{3,1},... | collective-permute-start | bytes 786440 | tf_op jit(solution)/shard_map/ppermute | solution.py:371
  3.7 6.5 %collective-permute-start.7 = (bf16[1024,128]{1,0:T(8,128)(2,1)}, bf16[1024,128]{1,0:T(8,128)(2,1)S(1)}, u32[]{:S(2)}, u32[]{:S(2)}) collective-permute-start(bf16[1024,128]{1,0:T(8,128)(2,1)} %taps_ref.1), channel_id=1, source_target_pairs={{0,2},{2,0},{4,6},{6,4},{8,10},{10,8},{12,14},{14,12},{1,3},{3,1},... | collective-permute-start | bytes 786440 | tf_op jit(solution)/shard_map/ppermute | solution.py:371
  4.2 12.9 %collective-permute-start = (bf16[1024,128]{1,0:T(8,128)(2,1)}, bf16[1024,128]{1,0:T(8,128)(2,1)S(1)}, u32[]{:S(2)}, u32[]{:S(2)}) collective-permute-start(bf16[1024,128]{1,0:T(8,128)(2,1)} %bitcast.4), channel_id=1, source_target_pairs={{0,2},{2,0},{4,6},{6,4},{8,10},{10,8},{12,14},{14,12},{1,3},{3,1},... | collective-permute-start | bytes 786440 | tf_op jit(solution)/shard_map/ppermute | solution.py:371
  10.2 7.2 %collective-permute-start.2 = (bf16[1024,128]{1,0:T(8,128)(2,1)S(1)}, bf16[1024,128]{1,0:T(8,128)(2,1)S(1)}, u32[]{:S(2)}, u32[]{:S(2)}) collective-permute-start(bf16[1024,128]{1,0:T(8,128)(2,1)S(1)} %collective-permute-done.1.other_ref), channel_id=1, source_target_pairs={{0,2},{2,0},{4,6},{6,4},{8,10},{10,8},{12,14},{14,12},{1,3},{3,1},... | collective-permute-start | bytes 786440 | tf_op jit(solution)/shard_map/ppermute | solution.py:371
  10.2 1.0 %copy-start.6 = (bf16[1,1024,128]{2,1,0:T(8,128)(2,1)S(1)}, bf16[1,1024,128]{2,1,0:T(8,128)(2,1)}, u32[]{:S(2)}) copy-start(bf16[1,1024,128]{2,1,0:T(8,128)(2,1)} %param.10) | copy-start | bytes 786436
  11.2 0.9 %copy-start.7 = (bf16[1024,128]{1,0:T(8,128)(2,1)S(1)}, bf16[1024,128]{1,0:T(8,128)(2,1)}, u32[]{:S(2)}) copy-start(bf16[1024,128]{1,0:T(8,128)(2,1)} %taps_ref.1) | copy-start | bytes 786436
  12.1 5.0 %copy-start.9 = (bf16[128,256]{1,0:T(8,128)(2,1)S(1)}, bf16[128,256]{1,0:T(8,128)(2,1)}, u32[]{:S(2)}) copy-start(bf16[128,256]{1,0:T(8,128)(2,1)} %proj_ref.1) | copy-start | bytes 196612
  12.6 14.8 %copy-start = (f32[2,128,1024]{2,1,0:T(8,128)S(1)}, f32[2,128,1024]{2,1,0:T(8,128)}, u32[]{:S(2)}) copy-start(f32[2,128,1024]{2,1,0:T(8,128)} %constant.14.clone.refs_5_.refs_7_.turn) | copy-start | bytes 3145732
  12.6 9.6 %collective-permute-start.8 = (bf16[2,16,2048]{2,1,0:T(8,128)(2,1)S(1)}, bf16[2,16,2048]{2,1,0:T(8,128)(2,1)S(1)}, u32[]{:S(2)}, u32[]{:S(2)}) collective-permute-start(bf16[2,16,2048]{2,1,0:T(8,128)(2,1)S(1)} %get-tuple-element.36), channel_id=1, source_target_pairs={{0,4},{2,6},{4,0},{6,2},{8,12},{10,14},{12,8},{14,10},{1,5},{3,7},... | collective-permute-start | bytes 393224 | tf_op jit(solution)/shard_map/ppermute | solution.py:381
  14.5 12.9 %collective-permute-start.9 = (bf16[2,16,2048]{2,1,0:T(8,128)(2,1)S(1)}, bf16[2,16,2048]{2,1,0:T(8,128)(2,1)S(1)}, u32[]{:S(2)}, u32[]{:S(2)}) collective-permute-start(bf16[2,16,2048]{2,1,0:T(8,128)(2,1)S(1)} %get-tuple-element.37), channel_id=1, source_target_pairs={{0,8},{2,10},{4,12},{6,14},{8,0},{10,2},{12,4},{14,6},{1,9},{3,11}... | collective-permute-start | bytes 393224 | tf_op jit(solution)/shard_map/ppermute | solution.py:381
  17.1 10.3 %collective-permute-start.10 = (bf16[2,16,2048]{2,1,0:T(8,128)(2,1)S(1)}, bf16[2,16,2048]{2,1,0:T(8,128)(2,1)S(1)}, u32[]{:S(2)}, u32[]{:S(2)}) collective-permute-start(bf16[2,16,2048]{2,1,0:T(8,128)(2,1)S(1)} %get-tuple-element.38), channel_id=1, source_target_pairs={{0,12},{2,14},{4,8},{6,10},{8,4},{10,6},{12,0},{14,2},{1,13},{3,15... | collective-permute-start | bytes 393224 | tf_op jit(solution)/shard_map/ppermute | solution.py:381
  17.4 10.0 %copy-start.2 = (bf16[2,256,256]{2,1,0:T(8,128)(2,1)S(1)}, bf16[2,256,256]{2,1,0:T(8,128)(2,1)}, u32[]{:S(2)}) copy-start(bf16[2,256,256]{2,1,0:T(8,128)(2,1)} %constant.16.clone.refs_7_.refs_9_) | copy-start | bytes 786436
  17.4 10.0 %copy-start.4 = (bf16[2,256,128]{2,1,0:T(8,128)(2,1)S(1)}, bf16[2,256,128]{2,1,0:T(8,128)(2,1)}, u32[]{:S(2)}) copy-start(bf16[2,256,128]{2,1,0:T(8,128)(2,1)} %constant.12.clone.refs_4_.refs_5_) | copy-start | bytes 393220
  17.5 10.0 %copy-start.8 = (f32[2,8,128]{2,1,0:T(8,128)S(1)}, f32[2,8,128]{2,1,0:T(8,128)}, u32[]{:S(2)}) copy-start(f32[2,8,128]{2,1,0:T(8,128)} %constant.15.clone.refs_6_.refs_8_.small) | copy-start | bytes 24580
  17.8 13.0 %collective-permute-start.3 = (bf16[2,16,1024]{2,1,0:T(8,128)(2,1)S(1)}, bf16[2,16,1024]{2,1,0:T(8,128)(2,1)S(1)}, u32[]{:S(2)}, u32[]{:S(2)}) collective-permute-start(bf16[2,16,1024]{2,1,0:T(8,128)(2,1)S(1)} %get-tuple-element.32), channel_id=1, source_target_pairs={{0,4},{2,6},{4,0},{6,2},{8,12},{10,14},{12,8},{14,10},{1,5},{3,7},... | collective-permute-start | bytes 196616 | tf_op jit(solution)/shard_map/ppermute | solution.py:381
  18.7 15.7 %collective-permute-start.4 = (bf16[2,16,1024]{2,1,0:T(8,128)(2,1)S(1)}, bf16[2,16,1024]{2,1,0:T(8,128)(2,1)S(1)}, u32[]{:S(2)}, u32[]{:S(2)}) collective-permute-start(bf16[2,16,1024]{2,1,0:T(8,128)(2,1)S(1)} %get-tuple-element.33), channel_id=1, source_target_pairs={{0,8},{2,10},{4,12},{6,14},{8,0},{10,2},{12,4},{14,6},{1,9},{3,11}... | collective-permute-start | bytes 196616 | tf_op jit(solution)/shard_map/ppermute | solution.py:381
  22.2 12.2 %collective-permute-start.5 = (bf16[2,16,1024]{2,1,0:T(8,128)(2,1)S(1)}, bf16[2,16,1024]{2,1,0:T(8,128)(2,1)S(1)}, u32[]{:S(2)}, u32[]{:S(2)}) collective-permute-start(bf16[2,16,1024]{2,1,0:T(8,128)(2,1)S(1)} %get-tuple-element.34), channel_id=1, source_target_pairs={{0,12},{2,14},{4,8},{6,10},{8,4},{10,6},{12,0},{14,2},{1,13},{3,15... | collective-permute-start | bytes 196616 | tf_op jit(solution)/shard_map/ppermute | solution.py:381
  27.5 7.0 %copy-start.1 = (bf16[2,256,256]{2,1,0:T(8,128)(2,1)S(1)}, bf16[2,256,256]{2,1,0:T(8,128)(2,1)}, u32[]{:S(2)}) copy-start(bf16[2,256,256]{2,1,0:T(8,128)(2,1)} %constant.17.clone.refs_10_.inverse) | copy-start | bytes 786436
  27.5 6.9 %copy-start.3 = (bf16[2,128,256]{2,1,0:T(8,128)(2,1)S(1)}, bf16[2,128,256]{2,1,0:T(8,128)(2,1)}, u32[]{:S(2)}) copy-start(bf16[2,128,256]{2,1,0:T(8,128)(2,1)} %constant.13.clone.refs_6_.last) | copy-start | bytes 393220
  38.7 4.4 %collective-permute-start.16 = (bf16[4,16,1024]{2,1,0:T(8,128)(2,1)S(1)}, bf16[4,16,1024]{2,1,0:T(8,128)(2,1)S(1)}, u32[]{:S(2)}, u32[]{:S(2)}) collective-permute-start(bf16[4,16,1024]{2,1,0:T(8,128)(2,1)S(1)} %get-tuple-element.49), channel_id=1, source_target_pairs={{0,2},{2,0},{4,6},{6,4},{8,10},{10,8},{12,14},{14,12},{1,3},{3,1},... | collective-permute-start | bytes 393224 | tf_op jit(solution)/shard_map/ppermute | solution.py:371
  41.1 2.6 %collective-permute-start.11 = (bf16[4,16,1024]{2,1,0:T(8,128)(2,1)S(1)}, bf16[4,16,1024]{2,1,0:T(8,128)(2,1)S(1)}, u32[]{:S(2)}, u32[]{:S(2)}) collective-permute-start(bf16[4,16,1024]{2,1,0:T(8,128)(2,1)S(1)} %get-tuple-element.43), channel_id=1, source_target_pairs={{0,2},{2,0},{4,6},{6,4},{8,10},{10,8},{12,14},{14,12},{1,3},{3,1},... | collective-permute-start | bytes 393224 | tf_op jit(solution)/shard_map/ppermute | solution.py:371
  41.6 7.2 %collective-permute-start.15 = (bf16[4,16,1024]{2,1,0:T(8,128)(2,1)S(1)}, bf16[4,16,1024]{2,1,0:T(8,128)(2,1)S(1)}, u32[]{:S(2)}, u32[]{:S(2)}) collective-permute-start(bf16[4,16,1024]{2,1,0:T(8,128)(2,1)S(1)} %get-tuple-element.48.mine_ref), channel_id=1, source_target_pairs={{0,16},{16,0},{1,17},{17,1},{2,18},{18,2},{3,19},{19,3},{4,20},{20... | collective-permute-start | bytes 393224 | tf_op jit(solution)/shard_map/ppermute | solution.py:375
  43.1 6.8 %collective-permute-start.17 = (bf16[4,16,1024]{2,1,0:T(8,128)(2,1)S(1)}, bf16[4,16,1024]{2,1,0:T(8,128)(2,1)S(1)}, u32[]{:S(2)}, u32[]{:S(2)}) collective-permute-start(bf16[4,16,1024]{2,1,0:T(8,128)(2,1)S(1)} %collective-permute-done.16.near_ref), channel_id=1, source_target_pairs={{0,16},{16,0},{1,17},{17,1},{2,18},{18,2},{3,19},{19,3},{4,20},{20... | collective-permute-start | bytes 393224 | tf_op jit(solution)/shard_map/ppermute | solution.py:375
  43.7 10.1 %collective-permute-start.12 = (bf16[2,16,1024]{2,1,0:T(8,128)(2,1)S(1)}, bf16[2,16,1024]{2,1,0:T(8,128)(2,1)S(1)}, u32[]{:S(2)}, u32[]{:S(2)}) collective-permute-start(bf16[2,16,1024]{2,1,0:T(8,128)(2,1)S(1)} %get-tuple-element.45), channel_id=1, source_target_pairs={{0,4},{2,6},{4,0},{6,2},{8,12},{10,14},{12,8},{14,10},{1,5},{3,7},... | collective-permute-start | bytes 196616 | tf_op jit(solution)/shard_map/ppermute | solution.py:381
  46.3 8.8 %collective-permute-start.13 = (bf16[2,16,1024]{2,1,0:T(8,128)(2,1)S(1)}, bf16[2,16,1024]{2,1,0:T(8,128)(2,1)S(1)}, u32[]{:S(2)}, u32[]{:S(2)}) collective-permute-start(bf16[2,16,1024]{2,1,0:T(8,128)(2,1)S(1)} %get-tuple-element.46), channel_id=1, source_target_pairs={{0,8},{2,10},{4,12},{6,14},{8,0},{10,2},{12,4},{14,6},{1,9},{3,11}... | collective-permute-start | bytes 196616 | tf_op jit(solution)/shard_map/ppermute | solution.py:381
  47.4 7.7 %collective-permute-start.14 = (bf16[2,16,1024]{2,1,0:T(8,128)(2,1)S(1)}, bf16[2,16,1024]{2,1,0:T(8,128)(2,1)S(1)}, u32[]{:S(2)}, u32[]{:S(2)}) collective-permute-start(bf16[2,16,1024]{2,1,0:T(8,128)(2,1)S(1)} %get-tuple-element.47), channel_id=1, source_target_pairs={{0,12},{2,14},{4,8},{6,10},{8,4},{10,6},{12,0},{14,2},{1,13},{3,15... | collective-permute-start | bytes 196616 | tf_op jit(solution)/shard_map/ppermute | solution.py:381
  50.0 6.2 %collective-permute-start.18 = (bf16[2,16,1024]{2,1,0:T(8,128)(2,1)S(1)}, bf16[2,16,1024]{2,1,0:T(8,128)(2,1)S(1)}, u32[]{:S(2)}, u32[]{:S(2)}) collective-permute-start(bf16[2,16,1024]{2,1,0:T(8,128)(2,1)S(1)} %get-tuple-element.51), channel_id=1, source_target_pairs={{0,4},{2,6},{4,0},{6,2},{8,12},{10,14},{12,8},{14,10},{1,5},{3,7},... | collective-permute-start | bytes 196616 | tf_op jit(solution)/shard_map/ppermute | solution.py:381
  52.6 7.3 %collective-permute-start.19 = (bf16[2,16,1024]{2,1,0:T(8,128)(2,1)S(1)}, bf16[2,16,1024]{2,1,0:T(8,128)(2,1)S(1)}, u32[]{:S(2)}, u32[]{:S(2)}) collective-permute-start(bf16[2,16,1024]{2,1,0:T(8,128)(2,1)S(1)} %get-tuple-element.52), channel_id=1, source_target_pairs={{0,8},{2,10},{4,12},{6,14},{8,0},{10,2},{12,4},{14,6},{1,9},{3,11}... | collective-permute-start | bytes 196616 | tf_op jit(solution)/shard_map/ppermute | solution.py:381
  53.7 6.2 %collective-permute-start.20 = (bf16[2,16,1024]{2,1,0:T(8,128)(2,1)S(1)}, bf16[2,16,1024]{2,1,0:T(8,128)(2,1)S(1)}, u32[]{:S(2)}, u32[]{:S(2)}) collective-permute-start(bf16[2,16,1024]{2,1,0:T(8,128)(2,1)S(1)} %get-tuple-element.53), channel_id=1, source_target_pairs={{0,12},{2,14},{4,8},{6,10},{8,4},{10,6},{12,0},{14,2},{1,13},{3,15... | collective-permute-start | bytes 196616 | tf_op jit(solution)/shard_map/ppermute | solution.py:381
where the time goes:
time: 61.2 us; the launch traced here: 61 us
  starting transfers between devices  27.3 us (45%)
  waiting for transfers between devices  17.9 us (29%)
  Pallas kernels  13.1 us (21%)
  local copies, waits for them, and re-layouts  1.94 us (3%)
  between operations  0.82 us (1%)
    ppermute x12, starting transfers between devices, exchange(): got.append(lax.ppermute(sent[offset], 'seq', pairs))  21 us
    ppermute x12, waiting for transfers between devices, exchange(): got.append(lax.ppermute(sent[offset], 'seq', pairs))  10.8 us
    ppermute x3, waiting for transfers between devices, cross(): return lax.ppermute(value, axis, [(k, (k + 1) % size) for k in range(size)])  7.08 us
    ppermute x3, starting transfers between devices, cross(): return lax.ppermute(value, axis, [(k, (k + 1) % size) for k in range(size)])  5.09 us
    pallas_call x1, Pallas kernels, per_device_near(): call(filter_kernel, (spec_shape,) + halves, [block_scratch, stage_scratch...  4.29 us
    pallas_call x1, Pallas kernels, per_device_near(): call(early_kernel, (spec_shape, spec_shape), [block_scratch, stage_scratc...  3.27 us
    pallas_call x1, Pallas kernels, per_device_near(): call(input_kernel, halves, half_pair + [spec_scratch] + back_pair + [flat...  2.27 us
    unnamed x20, local copies, waits for them, and re-layouts  1.94 us
  transfers between devices with their start and end apart: 21, of which 5 were waited for; matrix products, arithmetic and copies ran while one was open for 0% of the time, Pallas kernels for 13%

commit v1 on v0

--- a/solution.py
+++ b/solution.py
@@ -102,16 +102,10 @@
 CHUNK = 16
 
 
-def transform(block, first, turn, small, forward, stage, high, low, spectrum, rows, all_rows):
+def transform(block, first, turn, small, forward, stage, high, low, spectrum, rows):
     tiles = block.shape[1] // LANES
-    if rows == all_rows:
-        stage[...] = dot(first[0], block) + dot(first[1], block)
-    else:
-        for part in range(2):
-            pick = pl.ds(part * all_rows, rows)
-            stage[part * rows : (part + 1) * rows, :] = dot(first[0, pick, :rows], block) + dot(
-                first[1, pick, :rows], block
-            )
+    table = jnp.concatenate([first[0], first[1]], axis=1)
+    stage[...] = dot(table, jnp.concatenate([block, block], axis=0))
 
     def body(index, carry):
         start = pl.multiple_of(index * CHUNK, CHUNK)
@@ -138,15 +132,17 @@
         return carry
 
     lax.fori_loop(0, rows // CHUNK, body, 0)
-    count = tiles * rows
-    wide = high[:count, :]
-    spectrum[...] = dot(wide, forward[0]) + (dot(wide, forward[1]) + dot(low[:count, :], forward[0]))
-
-
-def untransform(last, turn, small, inverse, stage, high, low, back_high, back_low, rows, all_rows, tiles):
-    count = tiles * rows
-    wide = high[:count, :]
-    stage[:count, :] = dot(wide, inverse[0]) + (dot(wide, inverse[1]) + dot(low[:count, :], inverse[0]))
+    spectrum[...] = dot(
+        jnp.concatenate([high[...], low[...], high[...]], axis=1),
+        jnp.concatenate([forward[0], forward[0], forward[1]], axis=0),
+    )
+
+
+def untransform(last, turn, small, inverse, stage, high, back_high, rows, tiles):
+    stage[...] = dot(
+        jnp.concatenate([high[...], high[...]], axis=1),
+        jnp.concatenate([inverse[0], inverse[1]], axis=0),
+    )
 
     def body(index, carry):
         start = pl.multiple_of(index * CHUNK, CHUNK)
@@ -166,22 +162,16 @@
             c = turn[0, pl.ds(start, CHUNK), lanes]
             s = turn[1, pl.ds(start, CHUNK), lanes]
             re, im = res[tile], ims[tile]
-            for part, at in ((re * c - im * s, start), (im * c + re * s, rows + start)):
-                part_high, part_low = split(part)
-                back_high[pl.ds(at, CHUNK), lanes] = part_high
-                back_low[pl.ds(at, CHUNK), lanes] = part_low
+            back_high[pl.ds(start, CHUNK), lanes] = (re * c - im * s).astype(BF16)
+            back_high[pl.ds(rows + start, CHUNK), lanes] = (im * c + re * s).astype(BF16)
         return carry
 
     lax.fori_loop(0, rows // CHUNK, body, 0)
-    if rows == all_rows:
-        table_high, table_low = last[0], last[1]
-    else:
-        table_high, table_low = (
-            jnp.concatenate([last[k, :rows, :rows], last[k, :rows, all_rows : all_rows + rows]], axis=1)
-            for k in range(2)
-        )
-    right = back_high[: 2 * rows, :]
-    return dot(table_high, right) + (dot(table_low, right) + dot(table_high, back_low[: 2 * rows, :]))
+    right = back_high[...]
+    return dot(
+        jnp.concatenate([last[0], last[1]], axis=1),
+        jnp.concatenate([right, right], axis=0),
+    )
 
 
 def identity(size, dtype):
@@ -236,10 +226,7 @@
         pltpu.VMEM((tiles * rows, 2 * LANES), BF16),
         pltpu.VMEM((tiles * rows, 2 * LANES), BF16),
     ]
-    back_pair = [
-        pltpu.VMEM((2 * rows, tok_rows), BF16),
-        pltpu.VMEM((2 * rows, tok_rows), BF16),
-    ]
+    back_one = [pltpu.VMEM((2 * rows, tok_rows), BF16)]
     stage_scratch = pltpu.VMEM((2 * rows, tok_rows), F32)
     spec_shape = shape((tiles * rows, 2 * LANES), F32)
     spec_scratch = pltpu.VMEM((tiles * rows, 2 * LANES), F32)
@@ -266,19 +253,17 @@
         )
         for lanes, spectrum in ((front, input_ref), (behind, taps_ref)):
             take(recv, lanes, block)
-            transform(block[...], first, turn, small, forward, stage, high, low, spectrum, rows, rows)
+            transform(block[...], first, turn, small, forward, stage, high, low, spectrum, rows)
 
     real, imag = pl.ds(0, LANES), pl.ds(LANES, LANES)
 
-    def multiply(grad, other, high, low):
+    def multiply(grad, other, high):
         def body(tile, carry):
             at = pl.ds(pl.multiple_of(tile * rows, rows), rows)
             gr, gi = grad[at, real], grad[at, imag]
             kr, ki = other[at, real], other[at, imag]
-            for part, lanes in ((gr * kr + gi * ki, real), (gi * kr - gr * ki, imag)):
-                part_high, part_low = split(part)
-                high[at, lanes] = part_high
-                low[at, lanes] = part_low
+            high[at, real] = (gr * kr + gi * ki).astype(BF16)
+            high[at, imag] = (gi * kr - gr * ki).astype(BF16)
             return carry
 
         lax.fori_loop(0, tiles, body, 0)
@@ -286,20 +271,20 @@
     def filter_kernel(*refs):
         recv, rest = refs[:count], refs[count:]
         (input_ref, first, last, turn, small, forward, inverse, grad, out_ref,
-         block, stage, high, low, back, back_high, back_low) = rest
+         block, stage, high, low, back, back_high) = rest
         take(recv, front, block)
-        transform(block[...], first, turn, small, forward, stage, high, low, grad, rows, rows)
-        multiply(grad, input_ref, high, low)
+        transform(block[...], first, turn, small, forward, stage, high, low, grad, rows)
+        multiply(grad, input_ref, high)
         value = untransform(
-            last, turn, small, inverse, back, high, low, back_high, back_low, rows, rows, tiles
+            last, turn, small, inverse, back, high, back_high, rows, tiles
         )
         out_ref[...] = value.astype(BF16)
 
     def input_kernel(grad, taps_ref, last, turn, small, inverse, *refs):
-        *out_refs, high, low, back, back_high, back_low, wide = refs
-        multiply(grad, taps_ref, high, low)
+        *out_refs, high, low, back, back_high, wide = refs
+        multiply(grad, taps_ref, high)
         wide[...] = untransform(
-            last, turn, small, inverse, back, high, low, back_high, back_low, rows, rows, tiles
+            last, turn, small, inverse, back, high, back_high, rows, tiles
         )
         put(out_refs, wide, front)
 
@@ -328,12 +313,12 @@
     grad_spec, partial = call(
         filter_kernel,
         (spec_shape, shape((rows, tok_rows), BF16)),
-        [block_scratch, stage_scratch] + half_pair + [spec_scratch] + back_pair,
+        [block_scratch, stage_scratch] + half_pair + [spec_scratch] + back_one,
         9 * 10**6,
     )(*late, input_spec, first, last, turn, small, forward, inverse)
     partial_other = lax.ppermute(partial, "rep", [(k, (k + 1) % groups) for k in range(groups)])
     input_back = exchange(
-        call(input_kernel, pieces(tok_rows), half_pair + [spec_scratch] + back_pair + [flat], 6 * 10**6)(
+        call(input_kernel, pieces(tok_rows), half_pair + [spec_scratch] + back_one + [flat], 6 * 10**6)(
             grad_spec, taps_spec, last, turn, small, inverse
         )
     )
@@ -345,6 +330,7 @@
 
 def per_device_near(inputs, cotangent, filter_taps, out_proj):
     devices = lax.axis_size("seq")
+    groups = lax.axis_size("rep")
     tok_rows, chan_width = inputs.shape[1:]
     tiles = tok_rows // LANES
     narrow = chan_width // devices
@@ -388,16 +374,14 @@
     def pieces(width):
         return tuple(shape((CORES, narrow, width), BF16) for _ in range(chips))
 
-    front, behind = pl.ds(0, tok_rows), pl.ds(tok_rows, tok_rows)
+    part_rows = tok_rows // groups
+    front, behind = pl.ds(0, tok_rows), pl.ds(tok_rows, part_rows)
     block_scratch = pltpu.VMEM((rows, tok_rows), BF16)
     half_pair = [
         pltpu.VMEM((tiles * rows, 2 * LANES), BF16),
         pltpu.VMEM((tiles * rows, 2 * LANES), BF16),
     ]
-    back_pair = [
-        pltpu.VMEM((2 * rows, tok_rows), BF16),
-        pltpu.VMEM((2 * rows, tok_rows), BF16),
-    ]
+    back_one = [pltpu.VMEM((2 * rows, tok_rows), BF16)]
     stage_scratch = pltpu.VMEM((2 * rows, tok_rows), F32)
     spec_shape = shape((tiles * rows, 2 * LANES), F32)
     spec_scratch = pltpu.VMEM((tiles * rows, 2 * LANES), F32)
@@ -405,12 +389,12 @@
     half_scratch = pltpu.VMEM((half, tok_rows), F32)
     halves = (shape((chips, narrow, tok_rows), BF16), shape((chips, narrow, tok_rows), BF16))
 
-    def put(out_refs, source, side, lanes):
+    def put(out_refs, source, side, lanes, part=slice(None)):
         chip, _ = place()
         for offset in range(chips):
             at = pl.multiple_of((chip ^ offset) * narrow, narrow)
             out_refs[offset][pl.ds(side, 1), :, lanes] = (
-                source[pl.ds(at, narrow), :].reshape(1, narrow, tok_rows).astype(BF16)
+                source[pl.ds(at, narrow), part][None].astype(BF16)
             )
 
     def take(in_refs, lanes, block):
@@ -433,16 +417,26 @@
         pick = (row // narrow) * wide_rows + core * narrow + row % narrow
         return (pick == col).astype(F32).astype(BF16)
 
-    def pack_kernel(input_ref, input_near, taps_ref, taps_near, *refs):
+    def pack_kernel(held_ref, input_near, taps_near, *refs):
         *out_refs, wide = refs
         _, core = place()
         pick = chosen(core)
-        for own_ref, near_ref, lanes in ((input_ref, input_near, front), (taps_ref, taps_near, behind)):
-            for ref, side in ((own_ref, core), (near_ref, 1 - core)):
-                wide[...] = flipped(pick, ref[...])
-                put(out_refs, wide, side, lanes)
-
-    def own_kernel(own_ref, near_ref, proj_ref, part_ref, part_near, other_ref):
+        start = pl.multiple_of(lax.axis_index("rep") * part_rows, part_rows)
+        wide[...] = flipped(pick, held_ref[:tok_rows, :])
+        put(out_refs, wide, core, front)
+        wide[...] = flipped(pick, input_near[...])
+        put(out_refs, wide, 1 - core, front)
+        part = pl.ds(0, part_rows)
+        wide[:, part] = flipped(pick, held_ref[tok_rows:, :])
+        put(out_refs, wide, core, behind, part)
+        wide[:, part] = flipped(pick, taps_near[pl.ds(start, part_rows), :])
+        put(out_refs, wide, 1 - core, behind, part)
+
+    def taps_kernel(gate_ref, *refs):
+        *recv, out_ref = refs
+        take(recv, behind, out_ref)
+
+    def own_kernel(own_ref, proj_ref, near_ref, part_ref, part_near, other_ref):
         chan = lax.axis_index("chan")
         _, core = place()
         picked = [
@@ -463,24 +457,26 @@
             wide[...] = part[...] + flipped(proj_ref[...], ref[...])
             put(out_refs, wide, side, front)
 
-    def early_kernel(*refs):
-        recv, rest = refs[:chips], refs[chips:]
-        first, turn, small, forward, input_ref, taps_ref, block, stage, high, low = rest
-        for lanes, spectrum in ((front, input_ref), (behind, taps_ref)):
-            take(recv, lanes, block)
-            transform(block[...], first, turn, small, forward, stage, high, low, spectrum, rows, rows)
+    def signal_kernel(*refs):
+        recv, (first, turn, small, forward, spectrum, block, stage, high, low) = refs[:chips], refs[chips:]
+        take(recv, front, block)
+        transform(block[...], first, turn, small, forward, stage, high, low, spectrum, rows)
+
+    def taps_spec_kernel(own_ref, other_ref, first, turn, small, forward, spectrum, block, stage, high, low):
+        index = lax.axis_index("rep")
+        for ref, at in ((own_ref, index), (other_ref, 1 - index)):
+            block[:, pl.ds(pl.multiple_of(at * part_rows, part_rows), part_rows)] = ref[...]
+        transform(block[...], first, turn, small, forward, stage, high, low, spectrum, rows)
 
     real, imag = pl.ds(0, LANES), pl.ds(LANES, LANES)
 
-    def multiply(grad, other, high, low):
+    def multiply(grad, other, high):
         def body(tile, carry):
             at = pl.ds(pl.multiple_of(tile * rows, rows), rows)
             gr, gi = grad[at, real], grad[at, imag]
             kr, ki = other[at, real], other[at, imag]
-            for part, lanes in ((gr * kr + gi * ki, real), (gi * kr - gr * ki, imag)):
-                part_high, part_low = split(part)
-                high[at, lanes] = part_high
-                low[at, lanes] = part_low
+            high[at, real] = (gr * kr + gi * ki).astype(BF16)
+            high[at, imag] = (gi * kr - gr * ki).astype(BF16)
             return carry
 
         lax.fori_loop(0, tiles, body, 0)
@@ -488,28 +484,26 @@
     def filter_kernel(*refs):
         recv, rest = refs[:chips], refs[chips:]
         (input_ref, first, last, turn, small, forward, inverse, grad, mine_ref, theirs_ref,
-         block, stage, high, low, back, back_high, back_low, wide) = rest
+         block, stage, high, low, back, back_high, wide) = rest
         take(recv, front, block)
-        transform(block[...], first, turn, small, forward, stage, high, low, grad, rows, rows)
-        multiply(grad, input_ref, high, low)
-        wide[...] = untransform(
-            last, turn, small, inverse, back, high, low, back_high, back_low, rows, rows, tiles
-        )
+        transform(block[...], first, turn, small, forward, stage, high, low, grad, rows)
+        multiply(grad, input_ref, high)
+        wide[...] = untransform(last, turn, small, inverse, back, high, back_high, rows, tiles)
         cut(wide, mine_ref, theirs_ref)
 
-    def input_kernel(grad, taps_ref, last, turn, small, inverse, mine_ref, theirs_ref, *scratch):
-        high, low, back, back_high, back_low, wide = scratch
-        multiply(grad, taps_ref, high, low)
-        wide[...] = untransform(
-            last, turn, small, inverse, back, high, low, back_high, back_low, rows, rows, tiles
-        )
-        cut(wide, mine_ref, theirs_ref)
-
-    def join_kernel(mine_ref, near_ref, *out_refs):
-        chip, core = place()
+    def input_kernel(grad, taps_ref, last, turn, small, inverse, *refs):
+        *out_refs, high, back, back_high, wide = refs
+        multiply(grad, taps_ref, high)
+        wide[...] = untransform(last, turn, small, inverse, back, high, back_high, rows, tiles)
+        chip, _ = place()
         for offset in range(chips):
-            for ref, side in ((mine_ref, core), (near_ref, 1 - core)):
-                out_refs[offset][pl.ds(side, 1)] = ref[pl.ds(chip ^ offset, 1)]
+            at = pl.multiple_of((chip ^ offset) * wide_rows, wide_rows)
+            out_refs[offset][...] = (
+                wide[pl.ds(at, wide_rows), :].reshape(CORES, narrow, tok_rows).astype(BF16)
+            )
+
+    def gate_kernel(value_ref, out_ref):
+        out_ref[...] = value_ref[:16, :]
 
     def sum_kernel(mine_ref, mine_other, near_ref, near_other, *out_refs):
         chip, core = place()
@@ -521,7 +515,14 @@
 
     def final_kernel(*refs):
         *recv, out_ref, block = refs
-        take(recv, front, block)
+        if len(recv) == chips:
+            take(recv, front, block)
+        else:
+            chip, core = place()
+            for offset in range(chips):
+                for flip in range(CORES):
+                    at = pl.multiple_of((chip ^ offset) * wide_rows + (core ^ flip) * narrow, narrow)
+                    block[pl.ds(at, narrow), :] = recv[flip * chips + offset][core]
         moved = lax.dot_general(
             block[...], identity(chan_width, BF16), (((0,), (0,)), ((), ())), preferred_element_type=F32
         )
@@ -533,32 +534,46 @@
     taps_near = swap(filter_taps)
     other = cross(own, "chan")
     own_near = swap(own)
+    taps_part = lax.dynamic_slice_in_dim(filter_taps, lax.axis_index("rep") * part_rows, part_rows, 0)
+    held = jnp.concatenate([signal, taps_part], axis=0)
     early = exchange(
-        call(pack_kernel, pieces(2 * tok_rows), [half_scratch])(signal, signal_near, filter_taps, taps_near),
+        call(
+            pack_kernel,
+            pieces(tok_rows + part_rows),
+            [half_scratch],
+        )(held, signal_near, taps_near),
     )
     part_shape = shape((half, tok_rows), F32)
     part, part_near, proj_other = call(
-        own_kernel, (part_shape, part_shape, shape((half, chan_width), BF16))
-    )(own, own_near, out_proj)
+        own_kernel,
+        (part_shape, part_shape, shape((half, chan_width), BF16)),
+    )(own, out_proj, own_near)
     other_near = swap(other)
     late = exchange(call(mix_kernel, pieces(tok_rows), [half_scratch])(part, part_near, proj_other, other, other_near))
-    input_spec, taps_spec = call(
-        early_kernel, (spec_shape, spec_shape), [block_scratch, stage_scratch] + half_pair, 9 * 10**6
-    )(*early, first, turn, small, forward)
+    gate = call(gate_kernel, shape((16, chan_width), BF16), (), 10**4)(proj_other)
+    own_taps = call(taps_kernel, shape((rows, part_rows), BF16))(gate, *early)
+    other_taps = cross(own_taps, "rep")
+    transform_scratch = [block_scratch, stage_scratch] + half_pair
+    input_spec = call(signal_kernel, spec_shape, transform_scratch, 6 * 10**6)(
+        *early, first, turn, small, forward
+    )
     grad_spec, mine, theirs = call(
         filter_kernel,
         (spec_shape,) + halves,
-        [block_scratch, stage_scratch] + half_pair + [spec_scratch] + back_pair + [flat],
-        9 * 10**6,
+        [block_scratch, stage_scratch] + half_pair + [spec_scratch] + back_one + [flat],
+        12 * 10**6,
     )(*late, input_spec, first, last, turn, small, forward, inverse)
     mine_other = cross(mine, "rep")
     near = swap(theirs)
     near_other = cross(near, "rep")
-    input_mine, input_theirs = call(
-        input_kernel, halves, half_pair + [spec_scratch] + back_pair + [flat], 6 * 10**6
+    taps_spec = call(taps_spec_kernel, spec_shape, transform_scratch, 6 * 10**6)(
+        own_taps, other_taps, first, turn, small, forward
+    )
+    input_sent = call(
+        input_kernel, pieces(tok_rows), half_pair[:1] + [spec_scratch] + back_one + [flat], 6 * 10**6
     )(grad_spec, taps_spec, last, turn, small, inverse)
-    input_near = swap(input_theirs)
-    input_back = exchange(call(join_kernel, pieces(tok_rows))(input_mine, input_near))
+    input_back = exchange(input_sent)
+    input_back += tuple(swap(piece) for piece in input_back)
     filter_back = exchange(call(sum_kernel, pieces(tok_rows))(mine, mine_other, near, near_other))
     grad_input = call(final_kernel, shape((tok_rows, chan_width), BF16), [block_scratch])(*input_back)
     grad_filter = call(final_kernel, shape((tok_rows, chan_width), F32), [block_scratch])(*filter_back)

time: 61.2 us -> 60.7 us (level)
  waiting for transfers between devices: 17.9 us -> 20.5 us
  Pallas kernels: 13.1 us -> 11.4 us
  local copies, waits for them, and re-layouts: 1.94 us -> 0.96 us
    ppermute x12, waiting for transfers between devices: 10.8 us -> 15.3 us  [exchange(): got.append(lax.ppermute(sent[offset], 'seq', pairs))]
    ppermute x12, starting transfers between devices: 21 us -> 18.9 us  [exchange(): got.append(lax.ppermute(sent[offset], 'seq', pairs))]
    ppermute x3 -> x4, waiting for transfers between devices: 7.08 us -> 5.1 us  [cross(): return lax.ppermute(value, axis, [(k, (k + 1) % size) for k in range(size)])]
    unnamed x20 -> x18, local copies, waits for them, and re-layouts: 1.94 us -> 0.05 us
    ppermute x3 -> x4, starting transfers between devices: 5.09 us -> 6.72 us  [cross(): return lax.ppermute(value, axis, [(k, (k + 1) % size) for k in range(size)])]
    pallas_call x4 -> x6, Pallas kernels: 6.04 us -> 5.02 us  [the longest x1 1.62 us: per_device_near(): call(input_kernel, pieces(tok_rows), half_pair[:1] + [spec_scratch] + bac...]
    dynamic_slice x0 -> x1, local copies, waits for them, and re-layouts: none -> 0.91 us  [per_device_near(): lax.dynamic_slice_in_dim(filter_taps, lax.axis_index('rep') * part_rows,...]
    pallas_call x1, Pallas kernels: 4.29 us -> 3.65 us  [per_device_near(): call(filter_kernel, (spec_shape,) + halves, [block_scratch, stage_scratch...]
  transfers between devices with their start and end apart: 21 -> 25, of which waited for: 5 -> 5; matrix products, arithmetic and copies ran while one was open for 0% -> 2% of each run, Pallas kernels for 13% -> 17%
where the time goes in v1:
time: 60.7 us; the launch traced here: 60.6 us
  starting transfers between devices  26.8 us (44%)
  waiting for transfers between devices  20.5 us (34%)
  Pallas kernels  11.4 us (19%)
  local copies, waits for them, and re-layouts  0.96 us (2%)
  between operations  0.83 us (1%)
    ppermute x12, starting transfers between devices, exchange(): got.append(lax.ppermute(sent[offset], 'seq', pairs))  18.9 us
    ppermute x12, waiting for transfers between devices, exchange(): got.append(lax.ppermute(sent[offset], 'seq', pairs))  15.3 us
    ppermute x4, starting transfers between devices, cross(): return lax.ppermute(value, axis, [(k, (k + 1) % size) for k in range(size)])  6.72 us
    ppermute x4, waiting for transfers between devices, cross(): return lax.ppermute(value, axis, [(k, (k + 1) % size) for k in range(size)])  5.1 us
    pallas_call x1, Pallas kernels, per_device_near(): call(filter_kernel, (spec_shape,) + halves, [block_scratch, stage_scratch...  3.65 us
    pallas_call x1, Pallas kernels, per_device_near(): call(input_kernel, pieces(tok_rows), half_pair[:1] + [spec_scratch] + bac...  1.62 us
    pallas_call x1, Pallas kernels, per_device_near(): call(taps_spec_kernel, spec_shape, transform_scratch, 6 * 10 ** 6)  1.49 us
    pallas_call x1, Pallas kernels, per_device_near(): call(signal_kernel, spec_shape, transform_scratch, 6 * 10 ** 6)  1.48 us
  transfers between devices with their start and end apart: 25, of which 5 were waited for; matrix products, arithmetic and copies ran while one was open for 2% of the time, Pallas kernels for 17%

profile of v1, /device:TPU:0, one launch (start us, length us, event | category | flops | bytes accessed | tf_op | source)
XLA Modules:
  0.0 60.6 jit_solution(10183060364437500121)
XLA Ops:
  0.6 3.1 %collective-permute-start.1 = (bf16[1024,128]{1,0:T(8,128)(2,1)}, bf16[1024,128]{1,0:T(8,128)(2,1)S(1)}, u32[]{:S(2)}, u32[]{:S(2)}) collective-permute-start(bf16[1024,128]{1,0:T(8,128)(2,1)} %bitcast.3), channel_id=1, source_target_pairs={{0,1},{1,0},{2,3},{3,2},{4,5},{5,4},{6,7},{7,6},{8,9},{9,8},{10,11... | collective-permute-start | bytes 786440 | tf_op jit(solution)/shard_map/ppermute | solution.py:361
  3.7 0.0 collective-permute-start
  3.7 0.5 collective-permute-start.6
  4.2 0.9 %constant_dynamic-slice_fusion = bf16[512,128]{1,0:T(8,128)(2,1)S(1)} fusion(bf16[1024,128]{1,0:T(8,128)(2,1)} %param.12, s32[]{:T(128)S(6)} %select_n.3), kind=kLoop, calls=%fused_computation.1 | loop fusion | bytes 262148 | tf_op jit(solution)/shard_map/dynamic_slice | solution.py:537
  5.1 5.1 %collective-permute-done.1.other_ref = bf16[1024,128]{1,0:T(8,128)(2,1)S(1)} collective-permute-done((bf16[1024,128]{1,0:T(8,128)(2,1)}, bf16[1024,128]{1,0:T(8,128)(2,1)S(1)}, u32[]{:S(2)}, u32[]{:S(2)}) %collective-permute-start.1) | collective-permute-done | bytes 262176 | tf_op jit(solution)/shard_map/ppermute | solution.py:361
  10.2 0.0 collective-permute-start.2
  10.3 0.0 copy-start.5
  10.3 0.0 copy-start.7
  10.3 0.0 collective-permute-done.7.taps_near
  10.3 0.4 shard_map.115
  10.7 1.8 %collective-permute-start.8 = (bf16[2,16,1536]{2,1,0:T(8,128)(2,1)S(1)}, bf16[2,16,1536]{2,1,0:T(8,128)(2,1)S(1)}, u32[]{:S(2)}, u32[]{:S(2)}) collective-permute-start(bf16[2,16,1536]{2,1,0:T(8,128)(2,1)S(1)} %get-tuple-element.32), channel_id=1, source_target_pairs={{0,4},{2,6},{4,0},{6,2},{8,12},{10,14},{12,8},{14,10},{1,5},{3,7},... | collective-permute-start | bytes 294920 | tf_op jit(solution)/shard_map/ppermute | solution.py:367
  12.6 2.6 %collective-permute-start.9 = (bf16[2,16,1536]{2,1,0:T(8,128)(2,1)S(1)}, bf16[2,16,1536]{2,1,0:T(8,128)(2,1)S(1)}, u32[]{:S(2)}, u32[]{:S(2)}) collective-permute-start(bf16[2,16,1536]{2,1,0:T(8,128)(2,1)S(1)} %get-tuple-element.33), channel_id=1, source_target_pairs={{0,8},{2,10},{4,12},{6,14},{8,0},{10,2},{12,4},{14,6},{1,9},{3,11}... | collective-permute-start | bytes 294920 | tf_op jit(solution)/shard_map/ppermute | solution.py:367
  15.2 0.0 collective-permute-start.10
  15.2 0.0 collective-permute-done.near_ref
  15.2 0.3 shard_map.113
  15.5 0.0 copy-start
  15.5 0.0 collective-permute-done.2.other_near
  15.5 0.3 shard_map.114
  15.8 0.9 %collective-permute-start.3 = (bf16[2,16,1024]{2,1,0:T(8,128)(2,1)S(1)}, bf16[2,16,1024]{2,1,0:T(8,128)(2,1)S(1)}, u32[]{:S(2)}, u32[]{:S(2)}) collective-permute-start(bf16[2,16,1024]{2,1,0:T(8,128)(2,1)S(1)} %get-tuple-element.28), channel_id=1, source_target_pairs={{0,4},{2,6},{4,0},{6,2},{8,12},{10,14},{12,8},{14,10},{1,5},{3,7},... | collective-permute-start | bytes 196616 | tf_op jit(solution)/shard_map/ppermute | solution.py:367
  16.8 3.5 %collective-permute-start.4 = (bf16[2,16,1024]{2,1,0:T(8,128)(2,1)S(1)}, bf16[2,16,1024]{2,1,0:T(8,128)(2,1)S(1)}, u32[]{:S(2)}, u32[]{:S(2)}) collective-permute-start(bf16[2,16,1024]{2,1,0:T(8,128)(2,1)S(1)} %get-tuple-element.29), channel_id=1, source_target_pairs={{0,8},{2,10},{4,12},{6,14},{8,0},{10,2},{12,4},{14,6},{1,9},{3,11}... | collective-permute-start | bytes 196616 | tf_op jit(solution)/shard_map/ppermute | solution.py:367
  20.3 0.6 %collective-permute-start.5 = (bf16[2,16,1024]{2,1,0:T(8,128)(2,1)S(1)}, bf16[2,16,1024]{2,1,0:T(8,128)(2,1)S(1)}, u32[]{:S(2)}, u32[]{:S(2)}) collective-permute-start(bf16[2,16,1024]{2,1,0:T(8,128)(2,1)S(1)} %get-tuple-element.30), channel_id=1, source_target_pairs={{0,12},{2,14},{4,8},{6,10},{8,4},{10,6},{12,0},{14,2},{1,13},{3,15... | collective-permute-start | bytes 196616 | tf_op jit(solution)/shard_map/ppermute | solution.py:367
  20.9 2.5 %collective-permute-done.9.refs_2_ = bf16[2,16,1536]{2,1,0:T(8,128)(2,1)S(1)} collective-permute-done((bf16[2,16,1536]{2,1,0:T(8,128)(2,1)S(1)}, bf16[2,16,1536]{2,1,0:T(8,128)(2,1)S(1)}, u32[]{:S(2)}, u32[]{:S(2)}) %collective-permute-start.9) | collective-permute-done | bytes 98336 | tf_op jit(solution)/shard_map/ppermute | solution.py:367
  23.4 0.0 copy-start.3
  23.4 0.0 copy-start.4
  23.4 1.6 %collective-permute-start.11 = (bf16[128,512]{1,0:T(8,128)(2,1)S(1)}, bf16[128,512]{1,0:T(8,128)(2,1)S(1)}, u32[]{:S(2)}, u32[]{:S(2)}) collective-permute-start(bf16[128,512]{1,0:T(8,128)(2,1)S(1)} %shard_map.119.own_ref), channel_id=1, source_target_pairs={{0,16},{16,0},{1,17},{17,1},{2,18},{18,2},{3,19},{19,3},{4,20},{20... | collective-permute-start | bytes 393224 | tf_op jit(solution)/shard_map/ppermute | solution.py:361
  25.0 1.5 %shard_map.116.refs_4_ = f32[1024,256]{1,0:T(8,128)S(1)} custom-call(bf16[2,16,1536]{2,1,0:T(8,128)(2,1)S(1)} %get-tuple-element.31.refs_0_, bf16[2,16,1536]{2,1,0:T(8,128)(2,1)S(1)} %collective-permute-done.8.refs_1_, bf16[2,16,1536]{2,1,0:T(8,128)(2,1)S(1)} %collective-permute-done.9.refs_2_, bf16[2,16,1536]{2,1,0:T(8,128)(2,1)S(1)} %collective-permute-done.10.refs_3_, ...), custom_call_target="tpu_custom_call" | custom-call | flops 100000000 | bytes 6000000 | tf_op jit(solution)/shard_map/pallas_call | solution.py:557
  26.5 3.1 %collective-permute-done.4.refs_2_ = bf16[2,16,1024]{2,1,0:T(8,128)(2,1)S(1)} collective-permute-done((bf16[2,16,1024]{2,1,0:T(8,128)(2,1)S(1)}, bf16[2,16,1024]{2,1,0:T(8,128)(2,1)S(1)}, u32[]{:S(2)}, u32[]{:S(2)}) %collective-permute-start.4) | collective-permute-done | bytes 65568 | tf_op jit(solution)/shard_map/ppermute | solution.py:367
  29.6 3.6 %shard_map.117 = (f32[1024,256]{1,0:T(8,128)S(1)}, bf16[4,16,1024]{2,1,0:T(8,128)(2,1)S(1)}, bf16[4,16,1024]{2,1,0:T(8,128)(2,1)S(1)}) custom-call(bf16[2,16,1024]{2,1,0:T(8,128)(2,1)S(1)} %get-tuple-element.27.refs_0_, bf16[2,16,1024]{2,1,0:T(8,128)(2,1)S(1)} %collective-permute-done.3.refs_1_, bf16[2,16,1024]{2,1,0:T(8,128)(2,1)S(1)} %collective-permute-done.4.refs_2_, ...), custom_call_target="tpu_custom_call" | custom-call | flops 100000000 | bytes 12000000 | tf_op jit(solution)/shard_map/pallas_call | solution.py:560
  33.3 0.1 collective-permute-start.20
  33.4 1.5 %shard_map.120.taps_ref = f32[1024,256]{1,0:T(8,128)S(1)} custom-call(bf16[128,512]{1,0:T(8,128)(2,1)S(1)} %shard_map.119.own_ref, bf16[128,512]{1,0:T(8,128)(2,1)S(1)} %collective-permute-done.11.other_ref, bf16[2,256,128]{2,1,0:T(8,128)(2,1)S(1)} %copy-done.2, f32[2,128,1024]{2,1,0:T(8,128)S(1)} %copy-done, f32[2,8,128]{2,1,0:T(8,128)S(1)} %copy-done.6, ...), custom_call_target="tpu_custom_call" | custom-call | flops 100000000 | bytes 6000000 | tf_op jit(solution)/shard_map/pallas_call | solution.py:569
  34.9 1.6 %collective-permute-start.19 = (bf16[4,16,1024]{2,1,0:T(8,128)(2,1)S(1)}, bf16[4,16,1024]{2,1,0:T(8,128)(2,1)S(1)}, u32[]{:S(2)}, u32[]{:S(2)}) collective-permute-start(bf16[4,16,1024]{2,1,0:T(8,128)(2,1)S(1)} %get-tuple-element.40.mine_ref), channel_id=1, source_target_pairs={{0,16},{16,0},{1,17},{17,1},{2,18},{18,2},{3,19},{19,3},{4,20},{20... | collective-permute-start | bytes 393224 | tf_op jit(solution)/shard_map/ppermute | solution.py:361
  36.4 0.0 collective-permute-done.20.near_ref
  36.4 0.5 collective-permute-start.21
  37.0 1.6 %shard_map.121 = (bf16[2,16,1024]{2,1,0:T(8,128)(2,1)S(1)}, bf16[2,16,1024]{2,1,0:T(8,128)(2,1)S(1)}, bf16[2,16,1024]{2,1,0:T(8,128)(2,1)S(1)}, bf16[2,16,1024]{2,1,0:T(8,128)(2,1)S(1)}) custom-call(f32[1024,256]{1,0:T(8,128)S(1)} %get-tuple-element.35.grad, f32[1024,256]{1,0:T(8,128)S(1)} %shard_map.120.taps_ref, bf16[2,128,256]{2,1,0:T(8,128)(2,1)S(1)} %copy-done.4, ...), custom_call_target="tpu_custom_call" | custom-call | flops 100000000 | bytes 6000000 | tf_op jit(solution)/shard_map/pallas_call | solution.py:572
  38.6 2.4 %collective-permute-start.12 = (bf16[2,16,1024]{2,1,0:T(8,128)(2,1)S(1)}, bf16[2,16,1024]{2,1,0:T(8,128)(2,1)S(1)}, u32[]{:S(2)}, u32[]{:S(2)}) collective-permute-start(bf16[2,16,1024]{2,1,0:T(8,128)(2,1)S(1)} %get-tuple-element.37), channel_id=1, source_target_pairs={{0,4},{2,6},{4,0},{6,2},{8,12},{10,14},{12,8},{14,10},{1,5},{3,7},... | collective-permute-start | bytes 196616 | tf_op jit(solution)/shard_map/ppermute | solution.py:367
  41.0 1.2 %collective-permute-start.13 = (bf16[2,16,1024]{2,1,0:T(8,128)(2,1)S(1)}, bf16[2,16,1024]{2,1,0:T(8,128)(2,1)S(1)}, u32[]{:S(2)}, u32[]{:S(2)}) collective-permute-start(bf16[2,16,1024]{2,1,0:T(8,128)(2,1)S(1)} %get-tuple-element.38), channel_id=1, source_target_pairs={{0,8},{2,10},{4,12},{6,14},{8,0},{10,2},{12,4},{14,6},{1,9},{3,11}... | collective-permute-start | bytes 196616 | tf_op jit(solution)/shard_map/ppermute | solution.py:367
  42.2 1.4 %collective-permute-start.14 = (bf16[2,16,1024]{2,1,0:T(8,128)(2,1)S(1)}, bf16[2,16,1024]{2,1,0:T(8,128)(2,1)S(1)}, u32[]{:S(2)}, u32[]{:S(2)}) collective-permute-start(bf16[2,16,1024]{2,1,0:T(8,128)(2,1)S(1)} %get-tuple-element.39), channel_id=1, source_target_pairs={{0,12},{2,14},{4,8},{6,10},{8,4},{10,6},{12,0},{14,2},{1,13},{3,15... | collective-permute-start | bytes 196616 | tf_op jit(solution)/shard_map/ppermute | solution.py:367
  43.6 5.5 %collective-permute-done.13.refs_2_ = bf16[2,16,1024]{2,1,0:T(8,128)(2,1)S(1)} collective-permute-done((bf16[2,16,1024]{2,1,0:T(8,128)(2,1)S(1)}, bf16[2,16,1024]{2,1,0:T(8,128)(2,1)S(1)}, u32[]{:S(2)}, u32[]{:S(2)}) %collective-permute-start.13) | collective-permute-done | bytes 65568 | tf_op jit(solution)/shard_map/ppermute | solution.py:367
  49.1 0.5 collective-permute-start.17
  49.7 0.1 collective-permute-start.18
  49.7 0.1 shard_map.123
  49.8 1.3 %collective-permute-start.22 = (bf16[2,16,1024]{2,1,0:T(8,128)(2,1)S(1)}, bf16[2,16,1024]{2,1,0:T(8,128)(2,1)S(1)}, u32[]{:S(2)}, u32[]{:S(2)}) collective-permute-start(bf16[2,16,1024]{2,1,0:T(8,128)(2,1)S(1)} %get-tuple-element.43), channel_id=1, source_target_pairs={{0,4},{2,6},{4,0},{6,2},{8,12},{10,14},{12,8},{14,10},{1,5},{3,7},... | collective-permute-start | bytes 196616 | tf_op jit(solution)/shard_map/ppermute | solution.py:367
  51.1 1.6 %collective-permute-start.23 = (bf16[2,16,1024]{2,1,0:T(8,128)(2,1)S(1)}, bf16[2,16,1024]{2,1,0:T(8,128)(2,1)S(1)}, u32[]{:S(2)}, u32[]{:S(2)}) collective-permute-start(bf16[2,16,1024]{2,1,0:T(8,128)(2,1)S(1)} %get-tuple-element.44), channel_id=1, source_target_pairs={{0,8},{2,10},{4,12},{6,14},{8,0},{10,2},{12,4},{14,6},{1,9},{3,11}... | collective-permute-start | bytes 196616 | tf_op jit(solution)/shard_map/ppermute | solution.py:367
  52.7 0.0 collective-permute-done.16.refs_5_
  52.7 1.6 %collective-permute-start.24 = (bf16[2,16,1024]{2,1,0:T(8,128)(2,1)S(1)}, bf16[2,16,1024]{2,1,0:T(8,128)(2,1)S(1)}, u32[]{:S(2)}, u32[]{:S(2)}) collective-permute-start(bf16[2,16,1024]{2,1,0:T(8,128)(2,1)S(1)} %get-tuple-element.45), channel_id=1, source_target_pairs={{0,12},{2,14},{4,8},{6,10},{8,4},{10,6},{12,0},{14,2},{1,13},{3,15... | collective-permute-start | bytes 196616 | tf_op jit(solution)/shard_map/ppermute | solution.py:367
  54.3 1.0 %shard_map.122 = bf16[1024,128]{1,0:T(8,128)(2,1)} custom-call(bf16[2,16,1024]{2,1,0:T(8,128)(2,1)S(1)} %get-tuple-element.36.refs_0_, bf16[2,16,1024]{2,1,0:T(8,128)(2,1)S(1)} %collective-permute-done.12.refs_1_, bf16[2,16,1024]{2,1,0:T(8,128)(2,1)S(1)} %collective-permute-done.13.refs_2_, bf16[2,16,1024]{2,1,0:T(8,128)(2,1)S(1)} %collective-permute-done.14.refs_3_, ...), custom_call_target="tpu_custom_call" | custom-call | flops 100000000 | bytes 3000000 | tf_op jit(solution)/shard_map/pallas_call | solution.py:578
  55.3 4.2 %collective-permute-done.23.refs_2_ = bf16[2,16,1024]{2,1,0:T(8,128)(2,1)S(1)} collective-permute-done((bf16[2,16,1024]{2,1,0:T(8,128)(2,1)S(1)}, bf16[2,16,1024]{2,1,0:T(8,128)(2,1)S(1)}, u32[]{:S(2)}, u32[]{:S(2)}) %collective-permute-start.23) | collective-permute-done | bytes 65568 | tf_op jit(solution)/shard_map/ppermute | solution.py:367
  59.5 1.1 %shard_map.124 = f32[1024,128]{1,0:T(8,128)} custom-call(bf16[2,16,1024]{2,1,0:T(8,128)(2,1)S(1)} %get-tuple-element.42.refs_0_, bf16[2,16,1024]{2,1,0:T(8,128)(2,1)S(1)} %collective-permute-done.22.refs_1_, bf16[2,16,1024]{2,1,0:T(8,128)(2,1)S(1)} %collective-permute-done.23.refs_2_, bf16[2,16,1024]{2,1,0:T(8,128)(2,1)S(1)} %collective-permute-done.24.refs_3_), custom_call_target="tpu_custom_call" | custom-call | flops 100000000 | bytes 3000000 | tf_op jit(solution)/shard_map/pallas_call | solution.py:579
  (34 shorter events, 0.1 us)
Async XLA Ops:
  0.6 9.6 %copy-start.8 = (bf16[1,1024,128]{2,1,0:T(8,128)(2,1)S(1)}, bf16[1,1024,128]{2,1,0:T(8,128)(2,1)}, u32[]{:S(2)}) copy-start(bf16[1,1024,128]{2,1,0:T(8,128)(2,1)} %param.10) | copy-start | bytes 786436
  0.6 9.6 %collective-permute-start.1 = (bf16[1024,128]{1,0:T(8,128)(2,1)}, bf16[1024,128]{1,0:T(8,128)(2,1)S(1)}, u32[]{:S(2)}, u32[]{:S(2)}) collective-permute-start(bf16[1024,128]{1,0:T(8,128)(2,1)} %bitcast.3), channel_id=1, source_target_pairs={{0,1},{1,0},{2,3},{3,2},{4,5},{5,4},{6,7},{7,6},{8,9},{9,8},{10,11... | collective-permute-start | bytes 786440 | tf_op jit(solution)/shard_map/ppermute | solution.py:361
  3.7 11.5 %collective-permute-start = (bf16[1024,128]{1,0:T(8,128)(2,1)}, bf16[1024,128]{1,0:T(8,128)(2,1)S(1)}, u32[]{:S(2)}, u32[]{:S(2)}) collective-permute-start(bf16[1024,128]{1,0:T(8,128)(2,1)} %bitcast.4), channel_id=1, source_target_pairs={{0,2},{2,0},{4,6},{6,4},{8,10},{10,8},{12,14},{14,12},{1,3},{3,1},... | collective-permute-start | bytes 786440 | tf_op jit(solution)/shard_map/ppermute | solution.py:357
  3.7 6.6 %collective-permute-start.6 = (bf16[1024,128]{1,0:T(8,128)(2,1)}, bf16[1024,128]{1,0:T(8,128)(2,1)S(1)}, u32[]{:S(2)}, u32[]{:S(2)}) collective-permute-start(bf16[1024,128]{1,0:T(8,128)(2,1)} %bitcast.6), channel_id=1, source_target_pairs={{0,2},{2,0},{4,6},{6,4},{8,10},{10,8},{12,14},{14,12},{1,3},{3,1},... | collective-permute-start | bytes 786440 | tf_op jit(solution)/shard_map/ppermute | solution.py:357
  4.2 6.1 %collective-permute-start.7 = (bf16[1024,128]{1,0:T(8,128)(2,1)}, bf16[1024,128]{1,0:T(8,128)(2,1)S(1)}, u32[]{:S(2)}, u32[]{:S(2)}) collective-permute-start(bf16[1024,128]{1,0:T(8,128)(2,1)} %param.12), channel_id=1, source_target_pairs={{0,2},{2,0},{4,6},{6,4},{8,10},{10,8},{12,14},{14,12},{1,3},{3,1},... | collective-permute-start | bytes 786440 | tf_op jit(solution)/shard_map/ppermute | solution.py:357
  10.2 5.3 %collective-permute-start.2 = (bf16[1024,128]{1,0:T(8,128)(2,1)S(1)}, bf16[1024,128]{1,0:T(8,128)(2,1)S(1)}, u32[]{:S(2)}, u32[]{:S(2)}) collective-permute-start(bf16[1024,128]{1,0:T(8,128)(2,1)S(1)} %collective-permute-done.1.other_ref), channel_id=1, source_target_pairs={{0,2},{2,0},{4,6},{6,4},{8,10},{10,8},{12,14},{14,12},{1,3},{3,1},... | collective-permute-start | bytes 786440 | tf_op jit(solution)/shard_map/ppermute | solution.py:357
  10.3 4.9 %copy-start.5 = (bf16[1,1024,128]{2,1,0:T(8,128)(2,1)S(1)}, bf16[1,1024,128]{2,1,0:T(8,128)(2,1)}, u32[]{:S(2)}) copy-start(bf16[1,1024,128]{2,1,0:T(8,128)(2,1)} %param.11) | copy-start | bytes 786436
  10.3 4.9 %copy-start.7 = (bf16[128,256]{1,0:T(8,128)(2,1)S(1)}, bf16[128,256]{1,0:T(8,128)(2,1)}, u32[]{:S(2)}) copy-start(bf16[128,256]{1,0:T(8,128)(2,1)} %proj_ref.1) | copy-start | bytes 196612
  10.7 9.6 %collective-permute-start.8 = (bf16[2,16,1536]{2,1,0:T(8,128)(2,1)S(1)}, bf16[2,16,1536]{2,1,0:T(8,128)(2,1)S(1)}, u32[]{:S(2)}, u32[]{:S(2)}) collective-permute-start(bf16[2,16,1536]{2,1,0:T(8,128)(2,1)S(1)} %get-tuple-element.32), channel_id=1, source_target_pairs={{0,4},{2,6},{4,0},{6,2},{8,12},{10,14},{12,8},{14,10},{1,5},{3,7},... | collective-permute-start | bytes 294920 | tf_op jit(solution)/shard_map/ppermute | solution.py:367
  12.6 10.8 %collective-permute-start.9 = (bf16[2,16,1536]{2,1,0:T(8,128)(2,1)S(1)}, bf16[2,16,1536]{2,1,0:T(8,128)(2,1)S(1)}, u32[]{:S(2)}, u32[]{:S(2)}) collective-permute-start(bf16[2,16,1536]{2,1,0:T(8,128)(2,1)S(1)} %get-tuple-element.33), channel_id=1, source_target_pairs={{0,8},{2,10},{4,12},{6,14},{8,0},{10,2},{12,4},{14,6},{1,9},{3,11}... | collective-permute-start | bytes 294920 | tf_op jit(solution)/shard_map/ppermute | solution.py:367
  15.2 8.2 %collective-permute-start.10 = (bf16[2,16,1536]{2,1,0:T(8,128)(2,1)S(1)}, bf16[2,16,1536]{2,1,0:T(8,128)(2,1)S(1)}, u32[]{:S(2)}, u32[]{:S(2)}) collective-permute-start(bf16[2,16,1536]{2,1,0:T(8,128)(2,1)S(1)} %get-tuple-element.34), channel_id=1, source_target_pairs={{0,12},{2,14},{4,8},{6,10},{8,4},{10,6},{12,0},{14,2},{1,13},{3,15... | collective-permute-start | bytes 294920 | tf_op jit(solution)/shard_map/ppermute | solution.py:367
  15.5 9.5 %copy-start = (f32[2,128,1024]{2,1,0:T(8,128)S(1)}, f32[2,128,1024]{2,1,0:T(8,128)}, u32[]{:S(2)}) copy-start(f32[2,128,1024]{2,1,0:T(8,128)} %constant.26.clone.refs_5_.refs_7_.turn) | copy-start | bytes 3145732
  15.8 10.7 %collective-permute-start.3 = (bf16[2,16,1024]{2,1,0:T(8,128)(2,1)S(1)}, bf16[2,16,1024]{2,1,0:T(8,128)(2,1)S(1)}, u32[]{:S(2)}, u32[]{:S(2)}) collective-permute-start(bf16[2,16,1024]{2,1,0:T(8,128)(2,1)S(1)} %get-tuple-element.28), channel_id=1, source_target_pairs={{0,4},{2,6},{4,0},{6,2},{8,12},{10,14},{12,8},{14,10},{1,5},{3,7},... | collective-permute-start | bytes 196616 | tf_op jit(solution)/shard_map/ppermute | solution.py:367
  16.8 12.8 %collective-permute-start.4 = (bf16[2,16,1024]{2,1,0:T(8,128)(2,1)S(1)}, bf16[2,16,1024]{2,1,0:T(8,128)(2,1)S(1)}, u32[]{:S(2)}, u32[]{:S(2)}) collective-permute-start(bf16[2,16,1024]{2,1,0:T(8,128)(2,1)S(1)} %get-tuple-element.29), channel_id=1, source_target_pairs={{0,8},{2,10},{4,12},{6,14},{8,0},{10,2},{12,4},{14,6},{1,9},{3,11}... | collective-permute-start | bytes 196616 | tf_op jit(solution)/shard_map/ppermute | solution.py:367
  20.3 9.4 %collective-permute-start.5 = (bf16[2,16,1024]{2,1,0:T(8,128)(2,1)S(1)}, bf16[2,16,1024]{2,1,0:T(8,128)(2,1)S(1)}, u32[]{:S(2)}, u32[]{:S(2)}) collective-permute-start(bf16[2,16,1024]{2,1,0:T(8,128)(2,1)S(1)} %get-tuple-element.30), channel_id=1, source_target_pairs={{0,12},{2,14},{4,8},{6,10},{8,4},{10,6},{12,0},{14,2},{1,13},{3,15... | collective-permute-start | bytes 196616 | tf_op jit(solution)/shard_map/ppermute | solution.py:367
  23.3 1.6 %copy-start.1 = (bf16[2,256,256]{2,1,0:T(8,128)(2,1)S(1)}, bf16[2,256,256]{2,1,0:T(8,128)(2,1)}, u32[]{:S(2)}) copy-start(bf16[2,256,256]{2,1,0:T(8,128)(2,1)} %constant.28.clone.refs_7_.refs_9_.forward) | copy-start | bytes 786436
  23.3 1.6 %copy-start.2 = (bf16[2,256,128]{2,1,0:T(8,128)(2,1)S(1)}, bf16[2,256,128]{2,1,0:T(8,128)(2,1)}, u32[]{:S(2)}) copy-start(bf16[2,256,128]{2,1,0:T(8,128)(2,1)} %constant.24.clone.refs_4_.refs_5_.first) | copy-start | bytes 393220
  23.3 1.6 %copy-start.6 = (f32[2,8,128]{2,1,0:T(8,128)S(1)}, f32[2,8,128]{2,1,0:T(8,128)}, u32[]{:S(2)}) copy-start(f32[2,8,128]{2,1,0:T(8,128)} %constant.27.clone.refs_6_.refs_8_.small) | copy-start | bytes 24580
  23.4 6.2 %copy-start.3 = (bf16[2,256,256]{2,1,0:T(8,128)(2,1)S(1)}, bf16[2,256,256]{2,1,0:T(8,128)(2,1)}, u32[]{:S(2)}) copy-start(bf16[2,256,256]{2,1,0:T(8,128)(2,1)} %constant.29.clone.refs_10_.inverse) | copy-start | bytes 786436
  23.4 6.2 %copy-start.4 = (bf16[2,128,256]{2,1,0:T(8,128)(2,1)S(1)}, bf16[2,128,256]{2,1,0:T(8,128)(2,1)}, u32[]{:S(2)}) copy-start(bf16[2,128,256]{2,1,0:T(8,128)(2,1)} %constant.25.clone.refs_6_.last) | copy-start | bytes 393220
  23.4 10.0 %collective-permute-start.11 = (bf16[128,512]{1,0:T(8,128)(2,1)S(1)}, bf16[128,512]{1,0:T(8,128)(2,1)S(1)}, u32[]{:S(2)}, u32[]{:S(2)}) collective-permute-start(bf16[128,512]{1,0:T(8,128)(2,1)S(1)} %shard_map.119.own_ref), channel_id=1, source_target_pairs={{0,16},{16,0},{1,17},{17,1},{2,18},{18,2},{3,19},{19,3},{4,20},{20... | collective-permute-start | bytes 393224 | tf_op jit(solution)/shard_map/ppermute | solution.py:361
  33.3 3.1 %collective-permute-start.20 = (bf16[4,16,1024]{2,1,0:T(8,128)(2,1)S(1)}, bf16[4,16,1024]{2,1,0:T(8,128)(2,1)S(1)}, u32[]{:S(2)}, u32[]{:S(2)}) collective-permute-start(bf16[4,16,1024]{2,1,0:T(8,128)(2,1)S(1)} %get-tuple-element.41), channel_id=1, source_target_pairs={{0,2},{2,0},{4,6},{6,4},{8,10},{10,8},{12,14},{14,12},{1,3},{3,1},... | collective-permute-start | bytes 393224 | tf_op jit(solution)/shard_map/ppermute | solution.py:357
  34.9 14.8 %collective-permute-start.19 = (bf16[4,16,1024]{2,1,0:T(8,128)(2,1)S(1)}, bf16[4,16,1024]{2,1,0:T(8,128)(2,1)S(1)}, u32[]{:S(2)}, u32[]{:S(2)}) collective-permute-start(bf16[4,16,1024]{2,1,0:T(8,128)(2,1)S(1)} %get-tuple-element.40.mine_ref), channel_id=1, source_target_pairs={{0,16},{16,0},{1,17},{17,1},{2,18},{18,2},{3,19},{19,3},{4,20},{20... | collective-permute-start | bytes 393224 | tf_op jit(solution)/shard_map/ppermute | solution.py:361
  36.4 13.3 %collective-permute-start.21 = (bf16[4,16,1024]{2,1,0:T(8,128)(2,1)S(1)}, bf16[4,16,1024]{2,1,0:T(8,128)(2,1)S(1)}, u32[]{:S(2)}, u32[]{:S(2)}) collective-permute-start(bf16[4,16,1024]{2,1,0:T(8,128)(2,1)S(1)} %collective-permute-done.20.near_ref), channel_id=1, source_target_pairs={{0,16},{16,0},{1,17},{17,1},{2,18},{18,2},{3,19},{19,3},{4,20},{20... | collective-permute-start | bytes 393224 | tf_op jit(solution)/shard_map/ppermute | solution.py:361
  38.6 5.0 %collective-permute-start.12 = (bf16[2,16,1024]{2,1,0:T(8,128)(2,1)S(1)}, bf16[2,16,1024]{2,1,0:T(8,128)(2,1)S(1)}, u32[]{:S(2)}, u32[]{:S(2)}) collective-permute-start(bf16[2,16,1024]{2,1,0:T(8,128)(2,1)S(1)} %get-tuple-element.37), channel_id=1, source_target_pairs={{0,4},{2,6},{4,0},{6,2},{8,12},{10,14},{12,8},{14,10},{1,5},{3,7},... | collective-permute-start | bytes 196616 | tf_op jit(solution)/shard_map/ppermute | solution.py:367
  41.0 8.1 %collective-permute-start.13 = (bf16[2,16,1024]{2,1,0:T(8,128)(2,1)S(1)}, bf16[2,16,1024]{2,1,0:T(8,128)(2,1)S(1)}, u32[]{:S(2)}, u32[]{:S(2)}) collective-permute-start(bf16[2,16,1024]{2,1,0:T(8,128)(2,1)S(1)} %get-tuple-element.38), channel_id=1, source_target_pairs={{0,8},{2,10},{4,12},{6,14},{8,0},{10,2},{12,4},{14,6},{1,9},{3,11}... | collective-permute-start | bytes 196616 | tf_op jit(solution)/shard_map/ppermute | solution.py:367
  42.2 6.9 %collective-permute-start.14 = (bf16[2,16,1024]{2,1,0:T(8,128)(2,1)S(1)}, bf16[2,16,1024]{2,1,0:T(8,128)(2,1)S(1)}, u32[]{:S(2)}, u32[]{:S(2)}) collective-permute-start(bf16[2,16,1024]{2,1,0:T(8,128)(2,1)S(1)} %get-tuple-element.39), channel_id=1, source_target_pairs={{0,12},{2,14},{4,8},{6,10},{8,4},{10,6},{12,0},{14,2},{1,13},{3,15... | collective-permute-start | bytes 196616 | tf_op jit(solution)/shard_map/ppermute | solution.py:367
  43.6 7.5 %collective-permute-start.15 = (bf16[2,16,1024]{2,1,0:T(8,128)(2,1)S(1)}, bf16[2,16,1024]{2,1,0:T(8,128)(2,1)S(1)}, u32[]{:S(2)}, u32[]{:S(2)}) collective-permute-start(bf16[2,16,1024]{2,1,0:T(8,128)(2,1)S(1)} %get-tuple-element.36.refs_0_), channel_id=1, source_target_pairs={{0,2},{2,0},{4,6},{6,4},{8,10},{10,8},{12,14},{14,12},{1,3},{3,1},... | collective-permute-start | bytes 196616 | tf_op jit(solution)/shard_map/ppermute | solution.py:357
  49.1 3.5 %collective-permute-start.16 = (bf16[2,16,1024]{2,1,0:T(8,128)(2,1)S(1)}, bf16[2,16,1024]{2,1,0:T(8,128)(2,1)S(1)}, u32[]{:S(2)}, u32[]{:S(2)}) collective-permute-start(bf16[2,16,1024]{2,1,0:T(8,128)(2,1)S(1)} %collective-permute-done.12.refs_1_), channel_id=1, source_target_pairs={{0,2},{2,0},{4,6},{6,4},{8,10},{10,8},{12,14},{14,12},{1,3},{3,1},... | collective-permute-start | bytes 196616 | tf_op jit(solution)/shard_map/ppermute | solution.py:357
  49.1 5.1 %collective-permute-start.17 = (bf16[2,16,1024]{2,1,0:T(8,128)(2,1)S(1)}, bf16[2,16,1024]{2,1,0:T(8,128)(2,1)S(1)}, u32[]{:S(2)}, u32[]{:S(2)}) collective-permute-start(bf16[2,16,1024]{2,1,0:T(8,128)(2,1)S(1)} %collective-permute-done.13.refs_2_), channel_id=1, source_target_pairs={{0,2},{2,0},{4,6},{6,4},{8,10},{10,8},{12,14},{14,12},{1,3},{3,1},... | collective-permute-start | bytes 196616 | tf_op jit(solution)/shard_map/ppermute | solution.py:357
  49.7 4.6 %collective-permute-start.18 = (bf16[2,16,1024]{2,1,0:T(8,128)(2,1)S(1)}, bf16[2,16,1024]{2,1,0:T(8,128)(2,1)S(1)}, u32[]{:S(2)}, u32[]{:S(2)}) collective-permute-start(bf16[2,16,1024]{2,1,0:T(8,128)(2,1)S(1)} %collective-permute-done.14.refs_3_), channel_id=1, source_target_pairs={{0,2},{2,0},{4,6},{6,4},{8,10},{10,8},{12,14},{14,12},{1,3},{3,1},... | collective-permute-start | bytes 196616 | tf_op jit(solution)/shard_map/ppermute | solution.py:357
  49.8 5.5 %collective-permute-start.22 = (bf16[2,16,1024]{2,1,0:T(8,128)(2,1)S(1)}, bf16[2,16,1024]{2,1,0:T(8,128)(2,1)S(1)}, u32[]{:S(2)}, u32[]{:S(2)}) collective-permute-start(bf16[2,16,1024]{2,1,0:T(8,128)(2,1)S(1)} %get-tuple-element.43), channel_id=1, source_target_pairs={{0,4},{2,6},{4,0},{6,2},{8,12},{10,14},{12,8},{14,10},{1,5},{3,7},... | collective-permute-start | bytes 196616 | tf_op jit(solution)/shard_map/ppermute | solution.py:367
  51.1 8.4 %collective-permute-start.23 = (bf16[2,16,1024]{2,1,0:T(8,128)(2,1)S(1)}, bf16[2,16,1024]{2,1,0:T(8,128)(2,1)S(1)}, u32[]{:S(2)}, u32[]{:S(2)}) collective-permute-start(bf16[2,16,1024]{2,1,0:T(8,128)(2,1)S(1)} %get-tuple-element.44), channel_id=1, source_target_pairs={{0,8},{2,10},{4,12},{6,14},{8,0},{10,2},{12,4},{14,6},{1,9},{3,11}... | collective-permute-start | bytes 196616 | tf_op jit(solution)/shard_map/ppermute | solution.py:367
  52.7 6.8 %collective-permute-start.24 = (bf16[2,16,1024]{2,1,0:T(8,128)(2,1)S(1)}, bf16[2,16,1024]{2,1,0:T(8,128)(2,1)S(1)}, u32[]{:S(2)}, u32[]{:S(2)}) collective-permute-start(bf16[2,16,1024]{2,1,0:T(8,128)(2,1)S(1)} %get-tuple-element.45), channel_id=1, source_target_pairs={{0,12},{2,14},{4,8},{6,10},{8,4},{10,6},{12,0},{14,2},{1,13},{3,15... | collective-permute-start | bytes 196616 | tf_op jit(solution)/shard_map/ppermute | solution.py:367

commit v2 on v1

--- a/solution.py
+++ b/solution.py
@@ -100,22 +100,23 @@
 
 
 CHUNK = 16
-
-
-def transform(block, first, turn, small, forward, stage, high, low, spectrum, rows):
-    tiles = block.shape[1] // LANES
+GROUP = 32
+
+
+def spread(block, first, stage):
     table = jnp.concatenate([first[0], first[1]], axis=1)
     stage[...] = dot(table, jnp.concatenate([block, block], axis=0))
 
-    def body(index, carry):
-        start = pl.multiple_of(index * CHUNK, CHUNK)
+
+def forward_group(group, turn, small, forward, stage, high, low, rows, tiles):
+    for start in range(group * GROUP, (group + 1) * GROUP, CHUNK):
+        own = slice(start, start + CHUNK)
         res, ims = [], []
         for tile in range(tiles):
-            lanes = pl.ds(tile * LANES, LANES)
-            re = stage[pl.ds(start, CHUNK), lanes]
-            im = stage[pl.ds(rows + start, CHUNK), lanes]
-            c = turn[0, pl.ds(start, CHUNK), lanes]
-            s = turn[1, pl.ds(start, CHUNK), lanes]
+            lanes = slice(tile * LANES, (tile + 1) * LANES)
+            re = stage[own, lanes]
+            im = stage[rows + start : rows + start + CHUNK, lanes]
+            c, s = turn[0, own, lanes], turn[1, own, lanes]
             res.append(re * c + im * s)
             ims.append(im * c - re * s)
         res, ims = butterflies(res, ims, -1.0)
@@ -124,33 +125,45 @@
             if tile > 0:
                 c, s = small[0, tile : tile + 1, :], small[1, tile : tile + 1, :]
                 re, im = re * c + im * s, im * c - re * s
-            at = pl.ds(tile * rows + start, CHUNK)
-            for part, lanes in ((re, pl.ds(0, LANES)), (im, pl.ds(LANES, LANES))):
+            at = group * tiles * GROUP + tile * GROUP + start % GROUP
+            for part, lane in ((re, 0), (im, LANES)):
                 part_high, part_low = split(part)
-                high[at, lanes] = part_high
-                low[at, lanes] = part_low
-        return carry
-
-    lax.fori_loop(0, rows // CHUNK, body, 0)
-    spectrum[...] = dot(
-        jnp.concatenate([high[...], low[...], high[...]], axis=1),
+                high[at : at + CHUNK, lane : lane + LANES] = part_high
+                low[at : at + CHUNK, lane : lane + LANES] = part_low
+    at = slice(group * tiles * GROUP, (group + 1) * tiles * GROUP)
+    return dot(
+        jnp.concatenate([high[at, :], low[at, :], high[at, :]], axis=1),
         jnp.concatenate([forward[0], forward[0], forward[1]], axis=0),
     )
 
 
-def untransform(last, turn, small, inverse, stage, high, back_high, rows, tiles):
-    stage[...] = dot(
-        jnp.concatenate([high[...], high[...]], axis=1),
+def transform(block, first, turn, small, forward, stage, high, low, spectrum, rows):
+    tiles = block.shape[1] // LANES
+    spread(block, first, stage)
+    for group in range(rows // GROUP):
+        at = slice(group * tiles * GROUP, (group + 1) * tiles * GROUP)
+        spectrum[at, :] = forward_group(group, turn, small, forward, stage, high, low, rows, tiles)
+
+
+def correlate(value, other):
+    vr, vi = value[:, :LANES], value[:, LANES:]
+    wr, wi = other[:, :LANES], other[:, LANES:]
+    return jnp.concatenate([(vr * wr + vi * wi).astype(BF16), (vi * wr - vr * wi).astype(BF16)], axis=1)
+
+
+def inverse_group(group, product, turn, small, inverse, back, gathered, rows, tiles):
+    at = slice(group * tiles * GROUP, (group + 1) * tiles * GROUP)
+    back[at, :] = dot(
+        jnp.concatenate([product, product], axis=1),
         jnp.concatenate([inverse[0], inverse[1]], axis=0),
     )
-
-    def body(index, carry):
-        start = pl.multiple_of(index * CHUNK, CHUNK)
+    for start in range(group * GROUP, (group + 1) * GROUP, CHUNK):
+        own = slice(start, start + CHUNK)
         res, ims = [], []
         for tile in range(tiles):
-            at = pl.ds(tile * rows + start, CHUNK)
-            re = stage[at, pl.ds(0, LANES)]
-            im = stage[at, pl.ds(LANES, LANES)]
+            row = group * tiles * GROUP + tile * GROUP + start % GROUP
+            re = back[row : row + CHUNK, :LANES]
+            im = back[row : row + CHUNK, LANES:]
             if tile > 0:
                 c, s = small[0, tile : tile + 1, :], small[1, tile : tile + 1, :]
                 re, im = re * c - im * s, im * c + re * s
@@ -158,16 +171,15 @@
             ims.append(im)
         res, ims = butterflies(res, ims, 1.0)
         for tile in range(tiles):
-            lanes = pl.ds(tile * LANES, LANES)
-            c = turn[0, pl.ds(start, CHUNK), lanes]
-            s = turn[1, pl.ds(start, CHUNK), lanes]
+            lanes = slice(tile * LANES, (tile + 1) * LANES)
+            c, s = turn[0, own, lanes], turn[1, own, lanes]
             re, im = res[tile], ims[tile]
-            back_high[pl.ds(start, CHUNK), lanes] = (re * c - im * s).astype(BF16)
-            back_high[pl.ds(rows + start, CHUNK), lanes] = (im * c + re * s).astype(BF16)
-        return carry
-
-    lax.fori_loop(0, rows // CHUNK, body, 0)
-    right = back_high[...]
+            gathered[own, lanes] = (re * c - im * s).astype(BF16)
+            gathered[rows + start : rows + start + CHUNK, lanes] = (im * c + re * s).astype(BF16)
+
+
+def collapse(last, gathered):
+    right = gathered[...]
     return dot(
         jnp.concatenate([last[0], last[1]], axis=1),
         jnp.concatenate([right, right], axis=0),
@@ -255,37 +267,30 @@
             take(recv, lanes, block)
             transform(block[...], first, turn, small, forward, stage, high, low, spectrum, rows)
 
-    real, imag = pl.ds(0, LANES), pl.ds(LANES, LANES)
-
-    def multiply(grad, other, high):
-        def body(tile, carry):
-            at = pl.ds(pl.multiple_of(tile * rows, rows), rows)
-            gr, gi = grad[at, real], grad[at, imag]
-            kr, ki = other[at, real], other[at, imag]
-            high[at, real] = (gr * kr + gi * ki).astype(BF16)
-            high[at, imag] = (gi * kr - gr * ki).astype(BF16)
-            return carry
-
-        lax.fori_loop(0, tiles, body, 0)
+    count_groups = rows // GROUP
+
+    def span(group):
+        return slice(group * tiles * GROUP, (group + 1) * tiles * GROUP)
 
     def filter_kernel(*refs):
         recv, rest = refs[:count], refs[count:]
         (input_ref, first, last, turn, small, forward, inverse, grad, out_ref,
          block, stage, high, low, back, back_high) = rest
         take(recv, front, block)
-        transform(block[...], first, turn, small, forward, stage, high, low, grad, rows)
-        multiply(grad, input_ref, high)
-        value = untransform(
-            last, turn, small, inverse, back, high, back_high, rows, tiles
-        )
-        out_ref[...] = value.astype(BF16)
+        spread(block[...], first, stage)
+        for group in range(count_groups):
+            value = forward_group(group, turn, small, forward, stage, high, low, rows, tiles)
+            grad[span(group), :] = value
+            product = correlate(value, input_ref[span(group), :])
+            inverse_group(group, product, turn, small, inverse, back, back_high, rows, tiles)
+        out_ref[...] = collapse(last, back_high).astype(BF16)
 
     def input_kernel(grad, taps_ref, last, turn, small, inverse, *refs):
-        *out_refs, high, low, back, back_high, wide = refs
-        multiply(grad, taps_ref, high)
-        wide[...] = untransform(
-            last, turn, small, inverse, back, high, back_high, rows, tiles
-        )
+        *out_refs, back, back_high, wide = refs
+        for group in range(count_groups):
+            product = correlate(grad[span(group), :], taps_ref[span(group), :])
+            inverse_group(group, product, turn, small, inverse, back, back_high, rows, tiles)
+        wide[...] = collapse(last, back_high)
         put(out_refs, wide, front)
 
     def sum_kernel(own_ref, other_ref, *refs):
@@ -318,7 +323,7 @@
     )(*late, input_spec, first, last, turn, small, forward, inverse)
     partial_other = lax.ppermute(partial, "rep", [(k, (k + 1) % groups) for k in range(groups)])
     input_back = exchange(
-        call(input_kernel, pieces(tok_rows), half_pair + [spec_scratch] + back_one + [flat], 6 * 10**6)(
+        call(input_kernel, pieces(tok_rows), [spec_scratch] + back_one + [flat], 6 * 10**6)(
             grad_spec, taps_spec, last, turn, small, inverse
         )
     )
@@ -468,33 +473,31 @@
             block[:, pl.ds(pl.multiple_of(at * part_rows, part_rows), part_rows)] = ref[...]
         transform(block[...], first, turn, small, forward, stage, high, low, spectrum, rows)
 
-    real, imag = pl.ds(0, LANES), pl.ds(LANES, LANES)
-
-    def multiply(grad, other, high):
-        def body(tile, carry):
-            at = pl.ds(pl.multiple_of(tile * rows, rows), rows)
-            gr, gi = grad[at, real], grad[at, imag]
-            kr, ki = other[at, real], other[at, imag]
-            high[at, real] = (gr * kr + gi * ki).astype(BF16)
-            high[at, imag] = (gi * kr - gr * ki).astype(BF16)
-            return carry
-
-        lax.fori_loop(0, tiles, body, 0)
+    count_groups = rows // GROUP
+
+    def span(group):
+        return slice(group * tiles * GROUP, (group + 1) * tiles * GROUP)
 
     def filter_kernel(*refs):
         recv, rest = refs[:chips], refs[chips:]
         (input_ref, first, last, turn, small, forward, inverse, grad, mine_ref, theirs_ref,
          block, stage, high, low, back, back_high, wide) = rest
         take(recv, front, block)
-        transform(block[...], first, turn, small, forward, stage, high, low, grad, rows)
-        multiply(grad, input_ref, high)
-        wide[...] = untransform(last, turn, small, inverse, back, high, back_high, rows, tiles)
+        spread(block[...], first, stage)
+        for group in range(count_groups):
+            value = forward_group(group, turn, small, forward, stage, high, low, rows, tiles)
+            grad[span(group), :] = value
+            product = correlate(value, input_ref[span(group), :])
+            inverse_group(group, product, turn, small, inverse, back, back_high, rows, tiles)
+        wide[...] = collapse(last, back_high)
         cut(wide, mine_ref, theirs_ref)
 
     def input_kernel(grad, taps_ref, last, turn, small, inverse, *refs):
-        *out_refs, high, back, back_high, wide = refs
-        multiply(grad, taps_ref, high)
-        wide[...] = untransform(last, turn, small, inverse, back, high, back_high, rows, tiles)
+        *out_refs, back, back_high, wide = refs
+        for group in range(count_groups):
+            product = correlate(grad[span(group), :], taps_ref[span(group), :])
+            inverse_group(group, product, turn, small, inverse, back, back_high, rows, tiles)
+        wide[...] = collapse(last, back_high)
         chip, _ = place()
         for offset in range(chips):
             at = pl.multiple_of((chip ^ offset) * wide_rows, wide_rows)
@@ -570,7 +573,7 @@
         own_taps, other_taps, first, turn, small, forward
     )
     input_sent = call(
-        input_kernel, pieces(tok_rows), half_pair[:1] + [spec_scratch] + back_one + [flat], 6 * 10**6
+        input_kernel, pieces(tok_rows), [spec_scratch] + back_one + [flat], 6 * 10**6
     )(grad_spec, taps_spec, last, turn, small, inverse)
     input_back = exchange(input_sent)
     input_back += tuple(swap(piece) for piece in input_back)

time: 60.7 us -> 58.7 us (0.967)
  Pallas kernels: 11.4 us -> 9.49 us
    pallas_call x1, Pallas kernels: 3.65 us -> 2.83 us  [per_device_near(): call(filter_kernel, (spec_shape,) + halves, [block_scratch, stage_scratch...]
    pallas_call x1, Pallas kernels: 1.62 us -> 0.99 us  [per_device_near(): call(input_kernel, pieces(tok_rows), [spec_scratch] + back_one + [flat],...]
  transfers between devices with their start and end apart: 25 -> 25, of which waited for: 5 -> 5; matrix products, arithmetic and copies ran while one was open for 2% -> 2% of each run, Pallas kernels for 17% -> 14%
where the time goes in v2:
time: 58.7 us; the launch traced here: 58.6 us
  starting transfers between devices  26.6 us (45%)
  waiting for transfers between devices  20.7 us (35%)
  Pallas kernels  9.49 us (16%)
  local copies, waits for them, and re-layouts  0.96 us (2%)
  between operations  0.82 us (1%)
    ppermute x12, starting transfers between devices, exchange(): got.append(lax.ppermute(sent[offset], 'seq', pairs))  18.7 us
    ppermute x12, waiting for transfers between devices, exchange(): got.append(lax.ppermute(sent[offset], 'seq', pairs))  15.6 us
    ppermute x4, starting transfers between devices, cross(): return lax.ppermute(value, axis, [(k, (k + 1) % size) for k in range(size)])  6.72 us
    ppermute x4, waiting for transfers between devices, cross(): return lax.ppermute(value, axis, [(k, (k + 1) % size) for k in range(size)])  5.1 us
    pallas_call x1, Pallas kernels, per_device_near(): call(filter_kernel, (spec_shape,) + halves, [block_scratch, stage_scratch...  2.83 us
    pallas_call x1, Pallas kernels, per_device_near(): call(taps_spec_kernel, spec_shape, transform_scratch, 6 * 10 ** 6)  1.24 us
    pallas_call x1, Pallas kernels, per_device_near(): call(signal_kernel, spec_shape, transform_scratch, 6 * 10 ** 6)  1.24 us
  transfers between devices with their start and end apart: 25, of which 5 were waited for; matrix products, arithmetic and copies ran while one was open for 2% of the time, Pallas kernels for 14%

profile of v2, /device:TPU:0, one launch (start us, length us, event | category | flops | bytes accessed | tf_op | source)
XLA Modules:
  0.0 58.6 jit_solution(16550463764440445694)
XLA Ops:
  0.6 3.1 %collective-permute-start.1 = (bf16[1024,128]{1,0:T(8,128)(2,1)}, bf16[1024,128]{1,0:T(8,128)(2,1)S(1)}, u32[]{:S(2)}, u32[]{:S(2)}) collective-permute-start(bf16[1024,128]{1,0:T(8,128)(2,1)} %bitcast.3), channel_id=1, source_target_pairs={{0,1},{1,0},{2,3},{3,2},{4,5},{5,4},{6,7},{7,6},{8,9},{9,8},{10,11... | collective-permute-start | bytes 786440 | tf_op jit(solution)/shard_map/ppermute | solution.py:366
  3.7 0.0 collective-permute-start
  3.7 0.5 collective-permute-start.6
  4.2 0.9 %constant_dynamic-slice_fusion = bf16[512,128]{1,0:T(8,128)(2,1)S(1)} fusion(bf16[1024,128]{1,0:T(8,128)(2,1)} %param.12, s32[]{:T(128)S(6)} %select_n.3), kind=kLoop, calls=%fused_computation.1 | loop fusion | bytes 262148 | tf_op jit(solution)/shard_map/dynamic_slice | solution.py:540
  5.1 5.1 %collective-permute-done.1.other_ref = bf16[1024,128]{1,0:T(8,128)(2,1)S(1)} collective-permute-done((bf16[1024,128]{1,0:T(8,128)(2,1)}, bf16[1024,128]{1,0:T(8,128)(2,1)S(1)}, u32[]{:S(2)}, u32[]{:S(2)}) %collective-permute-start.1) | collective-permute-done | bytes 262176 | tf_op jit(solution)/shard_map/ppermute | solution.py:366
  10.2 0.0 collective-permute-start.2
  10.3 0.0 copy-start.5
  10.3 0.0 copy-start.7
  10.3 0.0 collective-permute-done.7.taps_near
  10.3 0.4 shard_map.115
  10.7 1.8 %collective-permute-start.8 = (bf16[2,16,1536]{2,1,0:T(8,128)(2,1)S(1)}, bf16[2,16,1536]{2,1,0:T(8,128)(2,1)S(1)}, u32[]{:S(2)}, u32[]{:S(2)}) collective-permute-start(bf16[2,16,1536]{2,1,0:T(8,128)(2,1)S(1)} %get-tuple-element.32), channel_id=1, source_target_pairs={{0,4},{2,6},{4,0},{6,2},{8,12},{10,14},{12,8},{14,10},{1,5},{3,7},... | collective-permute-start | bytes 294920 | tf_op jit(solution)/shard_map/ppermute | solution.py:372
  12.6 2.6 %collective-permute-start.9 = (bf16[2,16,1536]{2,1,0:T(8,128)(2,1)S(1)}, bf16[2,16,1536]{2,1,0:T(8,128)(2,1)S(1)}, u32[]{:S(2)}, u32[]{:S(2)}) collective-permute-start(bf16[2,16,1536]{2,1,0:T(8,128)(2,1)S(1)} %get-tuple-element.33), channel_id=1, source_target_pairs={{0,8},{2,10},{4,12},{6,14},{8,0},{10,2},{12,4},{14,6},{1,9},{3,11}... | collective-permute-start | bytes 294920 | tf_op jit(solution)/shard_map/ppermute | solution.py:372
  15.2 0.0 collective-permute-start.10
  15.2 0.0 collective-permute-done.near_ref
  15.2 0.3 shard_map.113
  15.5 0.0 copy-start
  15.5 0.0 collective-permute-done.2.other_near
  15.5 0.3 shard_map.114
  15.8 0.9 %collective-permute-start.3 = (bf16[2,16,1024]{2,1,0:T(8,128)(2,1)S(1)}, bf16[2,16,1024]{2,1,0:T(8,128)(2,1)S(1)}, u32[]{:S(2)}, u32[]{:S(2)}) collective-permute-start(bf16[2,16,1024]{2,1,0:T(8,128)(2,1)S(1)} %get-tuple-element.28), channel_id=1, source_target_pairs={{0,4},{2,6},{4,0},{6,2},{8,12},{10,14},{12,8},{14,10},{1,5},{3,7},... | collective-permute-start | bytes 196616 | tf_op jit(solution)/shard_map/ppermute | solution.py:372
  16.8 3.5 %collective-permute-start.4 = (bf16[2,16,1024]{2,1,0:T(8,128)(2,1)S(1)}, bf16[2,16,1024]{2,1,0:T(8,128)(2,1)S(1)}, u32[]{:S(2)}, u32[]{:S(2)}) collective-permute-start(bf16[2,16,1024]{2,1,0:T(8,128)(2,1)S(1)} %get-tuple-element.29), channel_id=1, source_target_pairs={{0,8},{2,10},{4,12},{6,14},{8,0},{10,2},{12,4},{14,6},{1,9},{3,11}... | collective-permute-start | bytes 196616 | tf_op jit(solution)/shard_map/ppermute | solution.py:372
  20.3 0.6 %collective-permute-start.5 = (bf16[2,16,1024]{2,1,0:T(8,128)(2,1)S(1)}, bf16[2,16,1024]{2,1,0:T(8,128)(2,1)S(1)}, u32[]{:S(2)}, u32[]{:S(2)}) collective-permute-start(bf16[2,16,1024]{2,1,0:T(8,128)(2,1)S(1)} %get-tuple-element.30), channel_id=1, source_target_pairs={{0,12},{2,14},{4,8},{6,10},{8,4},{10,6},{12,0},{14,2},{1,13},{3,15... | collective-permute-start | bytes 196616 | tf_op jit(solution)/shard_map/ppermute | solution.py:372
  20.9 2.5 %collective-permute-done.9.refs_2_ = bf16[2,16,1536]{2,1,0:T(8,128)(2,1)S(1)} collective-permute-done((bf16[2,16,1536]{2,1,0:T(8,128)(2,1)S(1)}, bf16[2,16,1536]{2,1,0:T(8,128)(2,1)S(1)}, u32[]{:S(2)}, u32[]{:S(2)}) %collective-permute-start.9) | collective-permute-done | bytes 98336 | tf_op jit(solution)/shard_map/ppermute | solution.py:372
  23.4 0.0 copy-start.3
  23.4 0.0 copy-start.4
  23.4 1.6 %collective-permute-start.11 = (bf16[128,512]{1,0:T(8,128)(2,1)S(1)}, bf16[128,512]{1,0:T(8,128)(2,1)S(1)}, u32[]{:S(2)}, u32[]{:S(2)}) collective-permute-start(bf16[128,512]{1,0:T(8,128)(2,1)S(1)} %shard_map.119.own_ref), channel_id=1, source_target_pairs={{0,16},{16,0},{1,17},{17,1},{2,18},{18,2},{3,19},{19,3},{4,20},{20... | collective-permute-start | bytes 393224 | tf_op jit(solution)/shard_map/ppermute | solution.py:366
  25.0 1.2 %shard_map.116.refs_4_ = f32[1024,256]{1,0:T(8,128)S(1)} custom-call(bf16[2,16,1536]{2,1,0:T(8,128)(2,1)S(1)} %get-tuple-element.31.refs_0_, bf16[2,16,1536]{2,1,0:T(8,128)(2,1)S(1)} %collective-permute-done.8.refs_1_, bf16[2,16,1536]{2,1,0:T(8,128)(2,1)S(1)} %collective-permute-done.9.refs_2_, bf16[2,16,1536]{2,1,0:T(8,128)(2,1)S(1)} %collective-permute-done.10.refs_3_, ...), custom_call_target="tpu_custom_call" | custom-call | flops 100000000 | bytes 6000000 | tf_op jit(solution)/shard_map/pallas_call | solution.py:560
  26.2 3.4 %collective-permute-done.4.refs_2_ = bf16[2,16,1024]{2,1,0:T(8,128)(2,1)S(1)} collective-permute-done((bf16[2,16,1024]{2,1,0:T(8,128)(2,1)S(1)}, bf16[2,16,1024]{2,1,0:T(8,128)(2,1)S(1)}, u32[]{:S(2)}, u32[]{:S(2)}) %collective-permute-start.4) | collective-permute-done | bytes 65568 | tf_op jit(solution)/shard_map/ppermute | solution.py:372
  29.6 2.8 %shard_map.117 = (f32[1024,256]{1,0:T(8,128)S(1)}, bf16[4,16,1024]{2,1,0:T(8,128)(2,1)S(1)}, bf16[4,16,1024]{2,1,0:T(8,128)(2,1)S(1)}) custom-call(bf16[2,16,1024]{2,1,0:T(8,128)(2,1)S(1)} %get-tuple-element.27.refs_0_, bf16[2,16,1024]{2,1,0:T(8,128)(2,1)S(1)} %collective-permute-done.3.refs_1_, bf16[2,16,1024]{2,1,0:T(8,128)(2,1)S(1)} %collective-permute-done.4.refs_2_, ...), custom_call_target="tpu_custom_call" | custom-call | flops 100000000 | bytes 12000000 | tf_op jit(solution)/shard_map/pallas_call | solution.py:563
  32.5 0.1 collective-permute-start.20
  32.6 1.2 %shard_map.120.taps_ref = f32[1024,256]{1,0:T(8,128)S(1)} custom-call(bf16[128,512]{1,0:T(8,128)(2,1)S(1)} %shard_map.119.own_ref, bf16[128,512]{1,0:T(8,128)(2,1)S(1)} %collective-permute-done.11.other_ref, bf16[2,256,128]{2,1,0:T(8,128)(2,1)S(1)} %copy-done.2, f32[2,128,1024]{2,1,0:T(8,128)S(1)} %copy-done, f32[2,8,128]{2,1,0:T(8,128)S(1)} %copy-done.6, ...), custom_call_target="tpu_custom_call" | custom-call | flops 100000000 | bytes 6000000 | tf_op jit(solution)/shard_map/pallas_call | solution.py:572
  33.8 1.6 %collective-permute-start.19 = (bf16[4,16,1024]{2,1,0:T(8,128)(2,1)S(1)}, bf16[4,16,1024]{2,1,0:T(8,128)(2,1)S(1)}, u32[]{:S(2)}, u32[]{:S(2)}) collective-permute-start(bf16[4,16,1024]{2,1,0:T(8,128)(2,1)S(1)} %get-tuple-element.40.mine_ref), channel_id=1, source_target_pairs={{0,16},{16,0},{1,17},{17,1},{2,18},{18,2},{3,19},{19,3},{4,20},{20... | collective-permute-start | bytes 393224 | tf_op jit(solution)/shard_map/ppermute | solution.py:366
  35.4 0.5 collective-permute-start.21
  35.9 1.0 %shard_map.121 = (bf16[2,16,1024]{2,1,0:T(8,128)(2,1)S(1)}, bf16[2,16,1024]{2,1,0:T(8,128)(2,1)S(1)}, bf16[2,16,1024]{2,1,0:T(8,128)(2,1)S(1)}, bf16[2,16,1024]{2,1,0:T(8,128)(2,1)S(1)}) custom-call(f32[1024,256]{1,0:T(8,128)S(1)} %get-tuple-element.35.grad, f32[1024,256]{1,0:T(8,128)S(1)} %shard_map.120.taps_ref, bf16[2,128,256]{2,1,0:T(8,128)(2,1)S(1)} %copy-done.4, ...), custom_call_target="tpu_custom_call" | custom-call | flops 100000000 | bytes 6000000 | tf_op jit(solution)/shard_map/pallas_call | solution.py:575
  36.9 2.2 %collective-permute-start.12 = (bf16[2,16,1024]{2,1,0:T(8,128)(2,1)S(1)}, bf16[2,16,1024]{2,1,0:T(8,128)(2,1)S(1)}, u32[]{:S(2)}, u32[]{:S(2)}) collective-permute-start(bf16[2,16,1024]{2,1,0:T(8,128)(2,1)S(1)} %get-tuple-element.37), channel_id=1, source_target_pairs={{0,4},{2,6},{4,0},{6,2},{8,12},{10,14},{12,8},{14,10},{1,5},{3,7},... | collective-permute-start | bytes 196616 | tf_op jit(solution)/shard_map/ppermute | solution.py:372
  39.1 1.2 %collective-permute-start.13 = (bf16[2,16,1024]{2,1,0:T(8,128)(2,1)S(1)}, bf16[2,16,1024]{2,1,0:T(8,128)(2,1)S(1)}, u32[]{:S(2)}, u32[]{:S(2)}) collective-permute-start(bf16[2,16,1024]{2,1,0:T(8,128)(2,1)S(1)} %get-tuple-element.38), channel_id=1, source_target_pairs={{0,8},{2,10},{4,12},{6,14},{8,0},{10,2},{12,4},{14,6},{1,9},{3,11}... | collective-permute-start | bytes 196616 | tf_op jit(solution)/shard_map/ppermute | solution.py:372
  40.3 1.4 %collective-permute-start.14 = (bf16[2,16,1024]{2,1,0:T(8,128)(2,1)S(1)}, bf16[2,16,1024]{2,1,0:T(8,128)(2,1)S(1)}, u32[]{:S(2)}, u32[]{:S(2)}) collective-permute-start(bf16[2,16,1024]{2,1,0:T(8,128)(2,1)S(1)} %get-tuple-element.39), channel_id=1, source_target_pairs={{0,12},{2,14},{4,8},{6,10},{8,4},{10,6},{12,0},{14,2},{1,13},{3,15... | collective-permute-start | bytes 196616 | tf_op jit(solution)/shard_map/ppermute | solution.py:372
  41.7 5.5 %collective-permute-done.13.refs_2_ = bf16[2,16,1024]{2,1,0:T(8,128)(2,1)S(1)} collective-permute-done((bf16[2,16,1024]{2,1,0:T(8,128)(2,1)S(1)}, bf16[2,16,1024]{2,1,0:T(8,128)(2,1)S(1)}, u32[]{:S(2)}, u32[]{:S(2)}) %collective-permute-start.13) | collective-permute-done | bytes 65568 | tf_op jit(solution)/shard_map/ppermute | solution.py:372
  47.2 0.0 collective-permute-start.16
  47.2 0.0 collective-permute-done.14.refs_3_
  47.2 0.5 collective-permute-start.17
  47.7 0.1 collective-permute-start.18
  47.8 0.1 shard_map.123
  47.9 1.3 %collective-permute-start.22 = (bf16[2,16,1024]{2,1,0:T(8,128)(2,1)S(1)}, bf16[2,16,1024]{2,1,0:T(8,128)(2,1)S(1)}, u32[]{:S(2)}, u32[]{:S(2)}) collective-permute-start(bf16[2,16,1024]{2,1,0:T(8,128)(2,1)S(1)} %get-tuple-element.43), channel_id=1, source_target_pairs={{0,4},{2,6},{4,0},{6,2},{8,12},{10,14},{12,8},{14,10},{1,5},{3,7},... | collective-permute-start | bytes 196616 | tf_op jit(solution)/shard_map/ppermute | solution.py:372
  49.1 1.6 %collective-permute-start.23 = (bf16[2,16,1024]{2,1,0:T(8,128)(2,1)S(1)}, bf16[2,16,1024]{2,1,0:T(8,128)(2,1)S(1)}, u32[]{:S(2)}, u32[]{:S(2)}) collective-permute-start(bf16[2,16,1024]{2,1,0:T(8,128)(2,1)S(1)} %get-tuple-element.44), channel_id=1, source_target_pairs={{0,8},{2,10},{4,12},{6,14},{8,0},{10,2},{12,4},{14,6},{1,9},{3,11}... | collective-permute-start | bytes 196616 | tf_op jit(solution)/shard_map/ppermute | solution.py:372
  50.7 1.6 %collective-permute-start.24 = (bf16[2,16,1024]{2,1,0:T(8,128)(2,1)S(1)}, bf16[2,16,1024]{2,1,0:T(8,128)(2,1)S(1)}, u32[]{:S(2)}, u32[]{:S(2)}) collective-permute-start(bf16[2,16,1024]{2,1,0:T(8,128)(2,1)S(1)} %get-tuple-element.45), channel_id=1, source_target_pairs={{0,12},{2,14},{4,8},{6,10},{8,4},{10,6},{12,0},{14,2},{1,13},{3,15... | collective-permute-start | bytes 196616 | tf_op jit(solution)/shard_map/ppermute | solution.py:372
  52.3 1.0 %shard_map.122 = bf16[1024,128]{1,0:T(8,128)(2,1)} custom-call(bf16[2,16,1024]{2,1,0:T(8,128)(2,1)S(1)} %get-tuple-element.36.refs_0_, bf16[2,16,1024]{2,1,0:T(8,128)(2,1)S(1)} %collective-permute-done.12.refs_1_, bf16[2,16,1024]{2,1,0:T(8,128)(2,1)S(1)} %collective-permute-done.13.refs_2_, bf16[2,16,1024]{2,1,0:T(8,128)(2,1)S(1)} %collective-permute-done.14.refs_3_, ...), custom_call_target="tpu_custom_call" | custom-call | flops 100000000 | bytes 3000000 | tf_op jit(solution)/shard_map/pallas_call | solution.py:581
  53.3 4.2 %collective-permute-done.23.refs_2_ = bf16[2,16,1024]{2,1,0:T(8,128)(2,1)S(1)} collective-permute-done((bf16[2,16,1024]{2,1,0:T(8,128)(2,1)S(1)}, bf16[2,16,1024]{2,1,0:T(8,128)(2,1)S(1)}, u32[]{:S(2)}, u32[]{:S(2)}) %collective-permute-start.23) | collective-permute-done | bytes 65568 | tf_op jit(solution)/shard_map/ppermute | solution.py:372
  57.5 1.1 %shard_map.124 = f32[1024,128]{1,0:T(8,128)} custom-call(bf16[2,16,1024]{2,1,0:T(8,128)(2,1)S(1)} %get-tuple-element.42.refs_0_, bf16[2,16,1024]{2,1,0:T(8,128)(2,1)S(1)} %collective-permute-done.22.refs_1_, bf16[2,16,1024]{2,1,0:T(8,128)(2,1)S(1)} %collective-permute-done.23.refs_2_, bf16[2,16,1024]{2,1,0:T(8,128)(2,1)S(1)} %collective-permute-done.24.refs_3_), custom_call_target="tpu_custom_call" | custom-call | flops 100000000 | bytes 3000000 | tf_op jit(solution)/shard_map/pallas_call | solution.py:582
  (34 shorter events, 0.1 us)
Async XLA Ops:
  0.6 9.6 %copy-start.8 = (bf16[1,1024,128]{2,1,0:T(8,128)(2,1)S(1)}, bf16[1,1024,128]{2,1,0:T(8,128)(2,1)}, u32[]{:S(2)}) copy-start(bf16[1,1024,128]{2,1,0:T(8,128)(2,1)} %param.10) | copy-start | bytes 786436
  0.6 9.6 %collective-permute-start.1 = (bf16[1024,128]{1,0:T(8,128)(2,1)}, bf16[1024,128]{1,0:T(8,128)(2,1)S(1)}, u32[]{:S(2)}, u32[]{:S(2)}) collective-permute-start(bf16[1024,128]{1,0:T(8,128)(2,1)} %bitcast.3), channel_id=1, source_target_pairs={{0,1},{1,0},{2,3},{3,2},{4,5},{5,4},{6,7},{7,6},{8,9},{9,8},{10,11... | collective-permute-start | bytes 786440 | tf_op jit(solution)/shard_map/ppermute | solution.py:366
  3.7 11.5 %collective-permute-start = (bf16[1024,128]{1,0:T(8,128)(2,1)}, bf16[1024,128]{1,0:T(8,128)(2,1)S(1)}, u32[]{:S(2)}, u32[]{:S(2)}) collective-permute-start(bf16[1024,128]{1,0:T(8,128)(2,1)} %bitcast.4), channel_id=1, source_target_pairs={{0,2},{2,0},{4,6},{6,4},{8,10},{10,8},{12,14},{14,12},{1,3},{3,1},... | collective-permute-start | bytes 786440 | tf_op jit(solution)/shard_map/ppermute | solution.py:362
  3.7 6.6 %collective-permute-start.6 = (bf16[1024,128]{1,0:T(8,128)(2,1)}, bf16[1024,128]{1,0:T(8,128)(2,1)S(1)}, u32[]{:S(2)}, u32[]{:S(2)}) collective-permute-start(bf16[1024,128]{1,0:T(8,128)(2,1)} %bitcast.6), channel_id=1, source_target_pairs={{0,2},{2,0},{4,6},{6,4},{8,10},{10,8},{12,14},{14,12},{1,3},{3,1},... | collective-permute-start | bytes 786440 | tf_op jit(solution)/shard_map/ppermute | solution.py:362
  4.2 6.1 %collective-permute-start.7 = (bf16[1024,128]{1,0:T(8,128)(2,1)}, bf16[1024,128]{1,0:T(8,128)(2,1)S(1)}, u32[]{:S(2)}, u32[]{:S(2)}) collective-permute-start(bf16[1024,128]{1,0:T(8,128)(2,1)} %param.12), channel_id=1, source_target_pairs={{0,2},{2,0},{4,6},{6,4},{8,10},{10,8},{12,14},{14,12},{1,3},{3,1},... | collective-permute-start | bytes 786440 | tf_op jit(solution)/shard_map/ppermute | solution.py:362
  10.2 5.3 %collective-permute-start.2 = (bf16[1024,128]{1,0:T(8,128)(2,1)S(1)}, bf16[1024,128]{1,0:T(8,128)(2,1)S(1)}, u32[]{:S(2)}, u32[]{:S(2)}) collective-permute-start(bf16[1024,128]{1,0:T(8,128)(2,1)S(1)} %collective-permute-done.1.other_ref), channel_id=1, source_target_pairs={{0,2},{2,0},{4,6},{6,4},{8,10},{10,8},{12,14},{14,12},{1,3},{3,1},... | collective-permute-start | bytes 786440 | tf_op jit(solution)/shard_map/ppermute | solution.py:362
  10.3 4.9 %copy-start.5 = (bf16[1,1024,128]{2,1,0:T(8,128)(2,1)S(1)}, bf16[1,1024,128]{2,1,0:T(8,128)(2,1)}, u32[]{:S(2)}) copy-start(bf16[1,1024,128]{2,1,0:T(8,128)(2,1)} %param.11) | copy-start | bytes 786436
  10.3 4.9 %copy-start.7 = (bf16[128,256]{1,0:T(8,128)(2,1)S(1)}, bf16[128,256]{1,0:T(8,128)(2,1)}, u32[]{:S(2)}) copy-start(bf16[128,256]{1,0:T(8,128)(2,1)} %proj_ref.1) | copy-start | bytes 196612
  10.7 9.6 %collective-permute-start.8 = (bf16[2,16,1536]{2,1,0:T(8,128)(2,1)S(1)}, bf16[2,16,1536]{2,1,0:T(8,128)(2,1)S(1)}, u32[]{:S(2)}, u32[]{:S(2)}) collective-permute-start(bf16[2,16,1536]{2,1,0:T(8,128)(2,1)S(1)} %get-tuple-element.32), channel_id=1, source_target_pairs={{0,4},{2,6},{4,0},{6,2},{8,12},{10,14},{12,8},{14,10},{1,5},{3,7},... | collective-permute-start | bytes 294920 | tf_op jit(solution)/shard_map/ppermute | solution.py:372
  12.6 10.8 %collective-permute-start.9 = (bf16[2,16,1536]{2,1,0:T(8,128)(2,1)S(1)}, bf16[2,16,1536]{2,1,0:T(8,128)(2,1)S(1)}, u32[]{:S(2)}, u32[]{:S(2)}) collective-permute-start(bf16[2,16,1536]{2,1,0:T(8,128)(2,1)S(1)} %get-tuple-element.33), channel_id=1, source_target_pairs={{0,8},{2,10},{4,12},{6,14},{8,0},{10,2},{12,4},{14,6},{1,9},{3,11}... | collective-permute-start | bytes 294920 | tf_op jit(solution)/shard_map/ppermute | solution.py:372
  15.2 8.2 %collective-permute-start.10 = (bf16[2,16,1536]{2,1,0:T(8,128)(2,1)S(1)}, bf16[2,16,1536]{2,1,0:T(8,128)(2,1)S(1)}, u32[]{:S(2)}, u32[]{:S(2)}) collective-permute-start(bf16[2,16,1536]{2,1,0:T(8,128)(2,1)S(1)} %get-tuple-element.34), channel_id=1, source_target_pairs={{0,12},{2,14},{4,8},{6,10},{8,4},{10,6},{12,0},{14,2},{1,13},{3,15... | collective-permute-start | bytes 294920 | tf_op jit(solution)/shard_map/ppermute | solution.py:372
  15.5 9.5 %copy-start = (f32[2,128,1024]{2,1,0:T(8,128)S(1)}, f32[2,128,1024]{2,1,0:T(8,128)}, u32[]{:S(2)}) copy-start(f32[2,128,1024]{2,1,0:T(8,128)} %constant.26.clone.refs_5_.refs_7_.turn) | copy-start | bytes 3145732
  15.8 10.4 %collective-permute-start.3 = (bf16[2,16,1024]{2,1,0:T(8,128)(2,1)S(1)}, bf16[2,16,1024]{2,1,0:T(8,128)(2,1)S(1)}, u32[]{:S(2)}, u32[]{:S(2)}) collective-permute-start(bf16[2,16,1024]{2,1,0:T(8,128)(2,1)S(1)} %get-tuple-element.28), channel_id=1, source_target_pairs={{0,4},{2,6},{4,0},{6,2},{8,12},{10,14},{12,8},{14,10},{1,5},{3,7},... | collective-permute-start | bytes 196616 | tf_op jit(solution)/shard_map/ppermute | solution.py:372
  16.8 12.8 %collective-permute-start.4 = (bf16[2,16,1024]{2,1,0:T(8,128)(2,1)S(1)}, bf16[2,16,1024]{2,1,0:T(8,128)(2,1)S(1)}, u32[]{:S(2)}, u32[]{:S(2)}) collective-permute-start(bf16[2,16,1024]{2,1,0:T(8,128)(2,1)S(1)} %get-tuple-element.29), channel_id=1, source_target_pairs={{0,8},{2,10},{4,12},{6,14},{8,0},{10,2},{12,4},{14,6},{1,9},{3,11}... | collective-permute-start | bytes 196616 | tf_op jit(solution)/shard_map/ppermute | solution.py:372
  20.3 9.4 %collective-permute-start.5 = (bf16[2,16,1024]{2,1,0:T(8,128)(2,1)S(1)}, bf16[2,16,1024]{2,1,0:T(8,128)(2,1)S(1)}, u32[]{:S(2)}, u32[]{:S(2)}) collective-permute-start(bf16[2,16,1024]{2,1,0:T(8,128)(2,1)S(1)} %get-tuple-element.30), channel_id=1, source_target_pairs={{0,12},{2,14},{4,8},{6,10},{8,4},{10,6},{12,0},{14,2},{1,13},{3,15... | collective-permute-start | bytes 196616 | tf_op jit(solution)/shard_map/ppermute | solution.py:372
  23.3 1.6 %copy-start.1 = (bf16[2,256,256]{2,1,0:T(8,128)(2,1)S(1)}, bf16[2,256,256]{2,1,0:T(8,128)(2,1)}, u32[]{:S(2)}) copy-start(bf16[2,256,256]{2,1,0:T(8,128)(2,1)} %constant.28.clone.refs_7_.refs_9_.forward) | copy-start | bytes 786436
  23.3 1.6 %copy-start.2 = (bf16[2,256,128]{2,1,0:T(8,128)(2,1)S(1)}, bf16[2,256,128]{2,1,0:T(8,128)(2,1)}, u32[]{:S(2)}) copy-start(bf16[2,256,128]{2,1,0:T(8,128)(2,1)} %constant.24.clone.refs_4_.refs_5_.first) | copy-start | bytes 393220
  23.3 1.6 %copy-start.6 = (f32[2,8,128]{2,1,0:T(8,128)S(1)}, f32[2,8,128]{2,1,0:T(8,128)}, u32[]{:S(2)}) copy-start(f32[2,8,128]{2,1,0:T(8,128)} %constant.27.clone.refs_6_.refs_8_.small) | copy-start | bytes 24580
  23.4 6.2 %copy-start.3 = (bf16[2,256,256]{2,1,0:T(8,128)(2,1)S(1)}, bf16[2,256,256]{2,1,0:T(8,128)(2,1)}, u32[]{:S(2)}) copy-start(bf16[2,256,256]{2,1,0:T(8,128)(2,1)} %constant.29.clone.refs_10_.inverse) | copy-start | bytes 786436
  23.4 6.2 %copy-start.4 = (bf16[2,128,256]{2,1,0:T(8,128)(2,1)S(1)}, bf16[2,128,256]{2,1,0:T(8,128)(2,1)}, u32[]{:S(2)}) copy-start(bf16[2,128,256]{2,1,0:T(8,128)(2,1)} %constant.25.clone.refs_6_.last) | copy-start | bytes 393220
  23.4 9.1 %collective-permute-start.11 = (bf16[128,512]{1,0:T(8,128)(2,1)S(1)}, bf16[128,512]{1,0:T(8,128)(2,1)S(1)}, u32[]{:S(2)}, u32[]{:S(2)}) collective-permute-start(bf16[128,512]{1,0:T(8,128)(2,1)S(1)} %shard_map.119.own_ref), channel_id=1, source_target_pairs={{0,16},{16,0},{1,17},{17,1},{2,18},{18,2},{3,19},{19,3},{4,20},{20... | collective-permute-start | bytes 393224 | tf_op jit(solution)/shard_map/ppermute | solution.py:366
  32.5 2.9 %collective-permute-start.20 = (bf16[4,16,1024]{2,1,0:T(8,128)(2,1)S(1)}, bf16[4,16,1024]{2,1,0:T(8,128)(2,1)S(1)}, u32[]{:S(2)}, u32[]{:S(2)}) collective-permute-start(bf16[4,16,1024]{2,1,0:T(8,128)(2,1)S(1)} %get-tuple-element.41), channel_id=1, source_target_pairs={{0,2},{2,0},{4,6},{6,4},{8,10},{10,8},{12,14},{14,12},{1,3},{3,1},... | collective-permute-start | bytes 393224 | tf_op jit(solution)/shard_map/ppermute | solution.py:362
  33.8 13.9 %collective-permute-start.19 = (bf16[4,16,1024]{2,1,0:T(8,128)(2,1)S(1)}, bf16[4,16,1024]{2,1,0:T(8,128)(2,1)S(1)}, u32[]{:S(2)}, u32[]{:S(2)}) collective-permute-start(bf16[4,16,1024]{2,1,0:T(8,128)(2,1)S(1)} %get-tuple-element.40.mine_ref), channel_id=1, source_target_pairs={{0,16},{16,0},{1,17},{17,1},{2,18},{18,2},{3,19},{19,3},{4,20},{20... | collective-permute-start | bytes 393224 | tf_op jit(solution)/shard_map/ppermute | solution.py:366
  35.4 12.4 %collective-permute-start.21 = (bf16[4,16,1024]{2,1,0:T(8,128)(2,1)S(1)}, bf16[4,16,1024]{2,1,0:T(8,128)(2,1)S(1)}, u32[]{:S(2)}, u32[]{:S(2)}) collective-permute-start(bf16[4,16,1024]{2,1,0:T(8,128)(2,1)S(1)} %collective-permute-done.20.near_ref), channel_id=1, source_target_pairs={{0,16},{16,0},{1,17},{17,1},{2,18},{18,2},{3,19},{19,3},{4,20},{20... | collective-permute-start | bytes 393224 | tf_op jit(solution)/shard_map/ppermute | solution.py:366
  36.9 4.8 %collective-permute-start.12 = (bf16[2,16,1024]{2,1,0:T(8,128)(2,1)S(1)}, bf16[2,16,1024]{2,1,0:T(8,128)(2,1)S(1)}, u32[]{:S(2)}, u32[]{:S(2)}) collective-permute-start(bf16[2,16,1024]{2,1,0:T(8,128)(2,1)S(1)} %get-tuple-element.37), channel_id=1, source_target_pairs={{0,4},{2,6},{4,0},{6,2},{8,12},{10,14},{12,8},{14,10},{1,5},{3,7},... | collective-permute-start | bytes 196616 | tf_op jit(solution)/shard_map/ppermute | solution.py:372
  39.1 8.1 %collective-permute-start.13 = (bf16[2,16,1024]{2,1,0:T(8,128)(2,1)S(1)}, bf16[2,16,1024]{2,1,0:T(8,128)(2,1)S(1)}, u32[]{:S(2)}, u32[]{:S(2)}) collective-permute-start(bf16[2,16,1024]{2,1,0:T(8,128)(2,1)S(1)} %get-tuple-element.38), channel_id=1, source_target_pairs={{0,8},{2,10},{4,12},{6,14},{8,0},{10,2},{12,4},{14,6},{1,9},{3,11}... | collective-permute-start | bytes 196616 | tf_op jit(solution)/shard_map/ppermute | solution.py:372
  40.3 6.9 %collective-permute-start.14 = (bf16[2,16,1024]{2,1,0:T(8,128)(2,1)S(1)}, bf16[2,16,1024]{2,1,0:T(8,128)(2,1)S(1)}, u32[]{:S(2)}, u32[]{:S(2)}) collective-permute-start(bf16[2,16,1024]{2,1,0:T(8,128)(2,1)S(1)} %get-tuple-element.39), channel_id=1, source_target_pairs={{0,12},{2,14},{4,8},{6,10},{8,4},{10,6},{12,0},{14,2},{1,13},{3,15... | collective-permute-start | bytes 196616 | tf_op jit(solution)/shard_map/ppermute | solution.py:372
  41.6 7.5 %collective-permute-start.15 = (bf16[2,16,1024]{2,1,0:T(8,128)(2,1)S(1)}, bf16[2,16,1024]{2,1,0:T(8,128)(2,1)S(1)}, u32[]{:S(2)}, u32[]{:S(2)}) collective-permute-start(bf16[2,16,1024]{2,1,0:T(8,128)(2,1)S(1)} %get-tuple-element.36.refs_0_), channel_id=1, source_target_pairs={{0,2},{2,0},{4,6},{6,4},{8,10},{10,8},{12,14},{14,12},{1,3},{3,1},... | collective-permute-start | bytes 196616 | tf_op jit(solution)/shard_map/ppermute | solution.py:362
  47.2 3.5 %collective-permute-start.16 = (bf16[2,16,1024]{2,1,0:T(8,128)(2,1)S(1)}, bf16[2,16,1024]{2,1,0:T(8,128)(2,1)S(1)}, u32[]{:S(2)}, u32[]{:S(2)}) collective-permute-start(bf16[2,16,1024]{2,1,0:T(8,128)(2,1)S(1)} %collective-permute-done.12.refs_1_), channel_id=1, source_target_pairs={{0,2},{2,0},{4,6},{6,4},{8,10},{10,8},{12,14},{14,12},{1,3},{3,1},... | collective-permute-start | bytes 196616 | tf_op jit(solution)/shard_map/ppermute | solution.py:362
  47.2 5.1 %collective-permute-start.17 = (bf16[2,16,1024]{2,1,0:T(8,128)(2,1)S(1)}, bf16[2,16,1024]{2,1,0:T(8,128)(2,1)S(1)}, u32[]{:S(2)}, u32[]{:S(2)}) collective-permute-start(bf16[2,16,1024]{2,1,0:T(8,128)(2,1)S(1)} %collective-permute-done.13.refs_2_), channel_id=1, source_target_pairs={{0,2},{2,0},{4,6},{6,4},{8,10},{10,8},{12,14},{14,12},{1,3},{3,1},... | collective-permute-start | bytes 196616 | tf_op jit(solution)/shard_map/ppermute | solution.py:362
  47.7 4.6 %collective-permute-start.18 = (bf16[2,16,1024]{2,1,0:T(8,128)(2,1)S(1)}, bf16[2,16,1024]{2,1,0:T(8,128)(2,1)S(1)}, u32[]{:S(2)}, u32[]{:S(2)}) collective-permute-start(bf16[2,16,1024]{2,1,0:T(8,128)(2,1)S(1)} %collective-permute-done.14.refs_3_), channel_id=1, source_target_pairs={{0,2},{2,0},{4,6},{6,4},{8,10},{10,8},{12,14},{14,12},{1,3},{3,1},... | collective-permute-start | bytes 196616 | tf_op jit(solution)/shard_map/ppermute | solution.py:362
  47.9 5.5 %collective-permute-start.22 = (bf16[2,16,1024]{2,1,0:T(8,128)(2,1)S(1)}, bf16[2,16,1024]{2,1,0:T(8,128)(2,1)S(1)}, u32[]{:S(2)}, u32[]{:S(2)}) collective-permute-start(bf16[2,16,1024]{2,1,0:T(8,128)(2,1)S(1)} %get-tuple-element.43), channel_id=1, source_target_pairs={{0,4},{2,6},{4,0},{6,2},{8,12},{10,14},{12,8},{14,10},{1,5},{3,7},... | collective-permute-start | bytes 196616 | tf_op jit(solution)/shard_map/ppermute | solution.py:372
  49.1 8.4 %collective-permute-start.23 = (bf16[2,16,1024]{2,1,0:T(8,128)(2,1)S(1)}, bf16[2,16,1024]{2,1,0:T(8,128)(2,1)S(1)}, u32[]{:S(2)}, u32[]{:S(2)}) collective-permute-start(bf16[2,16,1024]{2,1,0:T(8,128)(2,1)S(1)} %get-tuple-element.44), channel_id=1, source_target_pairs={{0,8},{2,10},{4,12},{6,14},{8,0},{10,2},{12,4},{14,6},{1,9},{3,11}... | collective-permute-start | bytes 196616 | tf_op jit(solution)/shard_map/ppermute | solution.py:372
  50.7 6.8 %collective-permute-start.24 = (bf16[2,16,1024]{2,1,0:T(8,128)(2,1)S(1)}, bf16[2,16,1024]{2,1,0:T(8,128)(2,1)S(1)}, u32[]{:S(2)}, u32[]{:S(2)}) collective-permute-start(bf16[2,16,1024]{2,1,0:T(8,128)(2,1)S(1)} %get-tuple-element.45), channel_id=1, source_target_pairs={{0,12},{2,14},{4,8},{6,10},{8,4},{10,6},{12,0},{14,2},{1,13},{3,15... | collective-permute-start | bytes 196616 | tf_op jit(solution)/shard_map/ppermute | solution.py:372

commit v3 on v2

--- a/solution.py
+++ b/solution.py
@@ -99,7 +99,7 @@
     return jnp.dot(lhs, rhs, preferred_element_type=F32)
 
 
-CHUNK = 16
+CHUNK = 8
 GROUP = 32
 
 
@@ -422,20 +422,17 @@
         pick = (row // narrow) * wide_rows + core * narrow + row % narrow
         return (pick == col).astype(F32).astype(BF16)
 
-    def pack_kernel(held_ref, input_near, taps_near, *refs):
+    def pack_kernel(input_ref, taps_ref, input_near, taps_near, *refs):
         *out_refs, wide = refs
         _, core = place()
         pick = chosen(core)
-        start = pl.multiple_of(lax.axis_index("rep") * part_rows, part_rows)
-        wide[...] = flipped(pick, held_ref[:tok_rows, :])
-        put(out_refs, wide, core, front)
-        wide[...] = flipped(pick, input_near[...])
-        put(out_refs, wide, 1 - core, front)
         part = pl.ds(0, part_rows)
-        wide[:, part] = flipped(pick, held_ref[tok_rows:, :])
-        put(out_refs, wide, core, behind, part)
-        wide[:, part] = flipped(pick, taps_near[pl.ds(start, part_rows), :])
-        put(out_refs, wide, 1 - core, behind, part)
+        for own_ref, near_ref, lanes, span_in in (
+            (input_ref, input_near, front, slice(None)), (taps_ref, taps_near, behind, part),
+        ):
+            for ref, side in ((own_ref, core), (near_ref, 1 - core)):
+                wide[:, span_in] = flipped(pick, ref[...])
+                put(out_refs, wide, side, lanes, span_in)
 
     def taps_kernel(gate_ref, *refs):
         *recv, out_ref = refs
@@ -534,17 +531,16 @@
     signal = inputs.reshape(tok_rows, chan_width)
     own = cotangent.reshape(tok_rows, chan_width)
     signal_near = swap(signal)
-    taps_near = swap(filter_taps)
+    taps_part = lax.dynamic_slice_in_dim(filter_taps, lax.axis_index("rep") * part_rows, part_rows, 0)
+    taps_near = swap(taps_part)
     other = cross(own, "chan")
     own_near = swap(own)
-    taps_part = lax.dynamic_slice_in_dim(filter_taps, lax.axis_index("rep") * part_rows, part_rows, 0)
-    held = jnp.concatenate([signal, taps_part], axis=0)
     early = exchange(
         call(
             pack_kernel,
             pieces(tok_rows + part_rows),
             [half_scratch],
-        )(held, signal_near, taps_near),
+        )(signal, taps_part, signal_near, taps_near),
     )
     part_shape = shape((half, tok_rows), F32)
     part, part_near, proj_other = call(

time: 58.7 us -> 60.1 us (1.024)
  waiting for transfers between devices: 20.7 us -> 22.6 us
  local copies, waits for them, and re-layouts: 0.96 us -> 0.07 us
    ppermute x9, waiting for transfers between devices: 0.02 us -> 1.13 us  [swap(): return lax.ppermute(value, 'seq', swap_pairs)]
    ppermute x4, waiting for transfers between devices: 5.1 us -> 6.01 us  [cross(): return lax.ppermute(value, axis, [(k, (k + 1) % size) for k in range(size)])]
    dynamic_slice x1, local copies, waits for them, and re-layouts: 0.91 us -> 0.01 us  [per_device_near(): lax.dynamic_slice_in_dim(filter_taps, lax.axis_index('rep') * part_rows,...]
  transfers between devices with their start and end apart: 25 -> 25, of which waited for: 5 -> 6; matrix products, arithmetic and copies ran while one was open for 2% -> 0% of each run, Pallas kernels for 14% -> 14%
where the time goes in v3:
time: 60.1 us; the launch traced here: 60 us
  starting transfers between devices  27.1 us (45%)
  waiting for transfers between devices  22.6 us (38%)
  Pallas kernels  9.4 us (16%)
  between operations  0.82 us (1%)
    ppermute x12, starting transfers between devices, exchange(): got.append(lax.ppermute(sent[offset], 'seq', pairs))  18.6 us
    ppermute x12, waiting for transfers between devices, exchange(): got.append(lax.ppermute(sent[offset], 'seq', pairs))  15.5 us
    ppermute x4, starting transfers between devices, cross(): return lax.ppermute(value, axis, [(k, (k + 1) % size) for k in range(size)])  6.74 us
    ppermute x4, waiting for transfers between devices, cross(): return lax.ppermute(value, axis, [(k, (k + 1) % size) for k in range(size)])  6.01 us
    pallas_call x1, Pallas kernels, per_device_near(): call(filter_kernel, (spec_shape,) + halves, [block_scratch, stage_scratch...  2.81 us
    ppermute x9, starting transfers between devices, swap(): return lax.ppermute(value, 'seq', swap_pairs)  1.74 us
    pallas_call x1, Pallas kernels, per_device_near(): call(signal_kernel, spec_shape, transform_scratch, 6 * 10 ** 6)  1.22 us
    pallas_call x1, Pallas kernels, per_device_near(): call(taps_spec_kernel, spec_shape, transform_scratch, 6 * 10 ** 6)  1.21 us
  transfers between devices with their start and end apart: 25, of which 6 were waited for; matrix products, arithmetic and copies ran while one was open for 0% of the time, Pallas kernels for 14%

profile of v3, /device:TPU:0, one launch (start us, length us, event | category | flops | bytes accessed | tf_op | source)
XLA Modules:
  0.0 60.0 jit_solution(8651039524542850454)
XLA Ops:
  0.6 0.0 copy-start
  0.7 3.1 %collective-permute-start.1 = (bf16[1024,128]{1,0:T(8,128)(2,1)}, bf16[1024,128]{1,0:T(8,128)(2,1)S(1)}, u32[]{:S(2)}, u32[]{:S(2)}) collective-permute-start(bf16[1024,128]{1,0:T(8,128)(2,1)} %bitcast.5), channel_id=1, source_target_pairs={{0,1},{1,0},{2,3},{3,2},{4,5},{5,4},{6,7},{7,6},{8,9},{9,8},{10,11... | collective-permute-start | bytes 786440 | tf_op jit(solution)/shard_map/ppermute | solution.py:366
  3.7 0.0 collective-permute-start.6
  3.7 0.5 collective-permute-start
  4.2 6.0 %collective-permute-done.1.other_ref = bf16[1024,128]{1,0:T(8,128)(2,1)S(1)} collective-permute-done((bf16[1024,128]{1,0:T(8,128)(2,1)}, bf16[1024,128]{1,0:T(8,128)(2,1)S(1)}, u32[]{:S(2)}, u32[]{:S(2)}) %collective-permute-start.1) | collective-permute-done | bytes 262176 | tf_op jit(solution)/shard_map/ppermute | solution.py:366
  10.2 0.0 collective-permute-start.2
  10.3 0.0 copy-start.7
  10.3 0.0 copy-start.9
  10.3 0.6 collective-permute-start.7
  10.8 1.1 %collective-permute-done.7.taps_near = bf16[512,128]{1,0:T(8,128)(2,1)S(1)} collective-permute-done((bf16[512,128]{1,0:T(8,128)(2,1)S(1)}, bf16[512,128]{1,0:T(8,128)(2,1)S(1)}, u32[]{:S(2)}, u32[]{:S(2)}) %collective-permute-start.7) | collective-permute-done | bytes 131104 | tf_op jit(solution)/shard_map/ppermute | solution.py:362
  12.0 0.4 shard_map.115
  12.4 1.9 %collective-permute-start.8 = (bf16[2,16,1536]{2,1,0:T(8,128)(2,1)S(1)}, bf16[2,16,1536]{2,1,0:T(8,128)(2,1)S(1)}, u32[]{:S(2)}, u32[]{:S(2)}) collective-permute-start(bf16[2,16,1536]{2,1,0:T(8,128)(2,1)S(1)} %get-tuple-element.32), channel_id=1, source_target_pairs={{0,4},{2,6},{4,0},{6,2},{8,12},{10,14},{12,8},{14,10},{1,5},{3,7},... | collective-permute-start | bytes 294920 | tf_op jit(solution)/shard_map/ppermute | solution.py:372
  14.2 2.6 %collective-permute-start.9 = (bf16[2,16,1536]{2,1,0:T(8,128)(2,1)S(1)}, bf16[2,16,1536]{2,1,0:T(8,128)(2,1)S(1)}, u32[]{:S(2)}, u32[]{:S(2)}) collective-permute-start(bf16[2,16,1536]{2,1,0:T(8,128)(2,1)S(1)} %get-tuple-element.33), channel_id=1, source_target_pairs={{0,8},{2,10},{4,12},{6,14},{8,0},{10,2},{12,4},{14,6},{1,9},{3,11}... | collective-permute-start | bytes 294920 | tf_op jit(solution)/shard_map/ppermute | solution.py:372
  16.8 0.3 shard_map.113
  17.1 0.0 copy-start.1
  17.2 0.3 shard_map.114
  17.5 0.9 %collective-permute-start.3 = (bf16[2,16,1024]{2,1,0:T(8,128)(2,1)S(1)}, bf16[2,16,1024]{2,1,0:T(8,128)(2,1)S(1)}, u32[]{:S(2)}, u32[]{:S(2)}) collective-permute-start(bf16[2,16,1024]{2,1,0:T(8,128)(2,1)S(1)} %get-tuple-element.28), channel_id=1, source_target_pairs={{0,4},{2,6},{4,0},{6,2},{8,12},{10,14},{12,8},{14,10},{1,5},{3,7},... | collective-permute-start | bytes 196616 | tf_op jit(solution)/shard_map/ppermute | solution.py:372
  18.4 3.5 %collective-permute-start.4 = (bf16[2,16,1024]{2,1,0:T(8,128)(2,1)S(1)}, bf16[2,16,1024]{2,1,0:T(8,128)(2,1)S(1)}, u32[]{:S(2)}, u32[]{:S(2)}) collective-permute-start(bf16[2,16,1024]{2,1,0:T(8,128)(2,1)S(1)} %get-tuple-element.29), channel_id=1, source_target_pairs={{0,8},{2,10},{4,12},{6,14},{8,0},{10,2},{12,4},{14,6},{1,9},{3,11}... | collective-permute-start | bytes 196616 | tf_op jit(solution)/shard_map/ppermute | solution.py:372
  21.9 0.3 collective-permute-start.5
  22.3 2.8 %collective-permute-done.9.refs_2_ = bf16[2,16,1536]{2,1,0:T(8,128)(2,1)S(1)} collective-permute-done((bf16[2,16,1536]{2,1,0:T(8,128)(2,1)S(1)}, bf16[2,16,1536]{2,1,0:T(8,128)(2,1)S(1)}, u32[]{:S(2)}, u32[]{:S(2)}) %collective-permute-start.9) | collective-permute-done | bytes 98336 | tf_op jit(solution)/shard_map/ppermute | solution.py:372
  25.1 0.0 collective-permute-done.10.refs_3_
  25.2 0.0 copy-start.4
  25.2 0.0 copy-start.5
  25.2 1.6 %collective-permute-start.11 = (bf16[128,512]{1,0:T(8,128)(2,1)S(1)}, bf16[128,512]{1,0:T(8,128)(2,1)S(1)}, u32[]{:S(2)}, u32[]{:S(2)}) collective-permute-start(bf16[128,512]{1,0:T(8,128)(2,1)S(1)} %shard_map.119.own_ref), channel_id=1, source_target_pairs={{0,16},{16,0},{1,17},{17,1},{2,18},{18,2},{3,19},{19,3},{4,20},{20... | collective-permute-start | bytes 393224 | tf_op jit(solution)/shard_map/ppermute | solution.py:366
  26.8 1.2 %shard_map.116.refs_4_ = f32[1024,256]{1,0:T(8,128)S(1)} custom-call(bf16[2,16,1536]{2,1,0:T(8,128)(2,1)S(1)} %get-tuple-element.31.refs_0_, bf16[2,16,1536]{2,1,0:T(8,128)(2,1)S(1)} %collective-permute-done.8.refs_1_, bf16[2,16,1536]{2,1,0:T(8,128)(2,1)S(1)} %collective-permute-done.9.refs_2_, bf16[2,16,1536]{2,1,0:T(8,128)(2,1)S(1)} %collective-permute-done.10.refs_3_, ...), custom_call_target="tpu_custom_call" | custom-call | flops 100000000 | bytes 6000000 | tf_op jit(solution)/shard_map/pallas_call | solution.py:556
  28.0 0.0 collective-permute-done.3.refs_1_
  28.0 3.0 %collective-permute-done.4.refs_2_ = bf16[2,16,1024]{2,1,0:T(8,128)(2,1)S(1)} collective-permute-done((bf16[2,16,1024]{2,1,0:T(8,128)(2,1)S(1)}, bf16[2,16,1024]{2,1,0:T(8,128)(2,1)S(1)}, u32[]{:S(2)}, u32[]{:S(2)}) %collective-permute-start.4) | collective-permute-done | bytes 65568 | tf_op jit(solution)/shard_map/ppermute | solution.py:372
  31.0 0.0 collective-permute-done.5.refs_3_
  31.0 2.8 %shard_map.117 = (f32[1024,256]{1,0:T(8,128)S(1)}, bf16[4,16,1024]{2,1,0:T(8,128)(2,1)S(1)}, bf16[4,16,1024]{2,1,0:T(8,128)(2,1)S(1)}) custom-call(bf16[2,16,1024]{2,1,0:T(8,128)(2,1)S(1)} %get-tuple-element.27.refs_0_, bf16[2,16,1024]{2,1,0:T(8,128)(2,1)S(1)} %collective-permute-done.3.refs_1_, bf16[2,16,1024]{2,1,0:T(8,128)(2,1)S(1)} %collective-permute-done.4.refs_2_, ...), custom_call_target="tpu_custom_call" | custom-call | flops 100000000 | bytes 12000000 | tf_op jit(solution)/shard_map/pallas_call | solution.py:559
  33.8 0.1 collective-permute-start.20
  33.9 1.2 %shard_map.120.taps_ref = f32[1024,256]{1,0:T(8,128)S(1)} custom-call(bf16[128,512]{1,0:T(8,128)(2,1)S(1)} %shard_map.119.own_ref, bf16[128,512]{1,0:T(8,128)(2,1)S(1)} %collective-permute-done.11.other_ref, bf16[2,256,128]{2,1,0:T(8,128)(2,1)S(1)} %copy-done.3, f32[2,128,1024]{2,1,0:T(8,128)S(1)} %copy-done.1, f32[2,8,128]{2,1,0:T(8,128)S(1)} %copy-done.8, ...), custom_call_target="tpu_custom_call" | custom-call | flops 100000000 | bytes 6000000 | tf_op jit(solution)/shard_map/pallas_call | solution.py:568
  35.1 1.6 %collective-permute-start.19 = (bf16[4,16,1024]{2,1,0:T(8,128)(2,1)S(1)}, bf16[4,16,1024]{2,1,0:T(8,128)(2,1)S(1)}, u32[]{:S(2)}, u32[]{:S(2)}) collective-permute-start(bf16[4,16,1024]{2,1,0:T(8,128)(2,1)S(1)} %get-tuple-element.40.mine_ref), channel_id=1, source_target_pairs={{0,16},{16,0},{1,17},{17,1},{2,18},{18,2},{3,19},{19,3},{4,20},{20... | collective-permute-start | bytes 393224 | tf_op jit(solution)/shard_map/ppermute | solution.py:366
  36.7 0.5 collective-permute-start.21
  37.2 1.0 %shard_map.121 = (bf16[2,16,1024]{2,1,0:T(8,128)(2,1)S(1)}, bf16[2,16,1024]{2,1,0:T(8,128)(2,1)S(1)}, bf16[2,16,1024]{2,1,0:T(8,128)(2,1)S(1)}, bf16[2,16,1024]{2,1,0:T(8,128)(2,1)S(1)}) custom-call(f32[1024,256]{1,0:T(8,128)S(1)} %get-tuple-element.35.grad, f32[1024,256]{1,0:T(8,128)S(1)} %shard_map.120.taps_ref, bf16[2,128,256]{2,1,0:T(8,128)(2,1)S(1)} %copy-done.5, ...), custom_call_target="tpu_custom_call" | custom-call | flops 100000000 | bytes 6000000 | tf_op jit(solution)/shard_map/pallas_call | solution.py:571
  38.2 2.3 %collective-permute-start.12 = (bf16[2,16,1024]{2,1,0:T(8,128)(2,1)S(1)}, bf16[2,16,1024]{2,1,0:T(8,128)(2,1)S(1)}, u32[]{:S(2)}, u32[]{:S(2)}) collective-permute-start(bf16[2,16,1024]{2,1,0:T(8,128)(2,1)S(1)} %get-tuple-element.37), channel_id=1, source_target_pairs={{0,4},{2,6},{4,0},{6,2},{8,12},{10,14},{12,8},{14,10},{1,5},{3,7},... | collective-permute-start | bytes 196616 | tf_op jit(solution)/shard_map/ppermute | solution.py:372
  40.5 1.3 %collective-permute-start.13 = (bf16[2,16,1024]{2,1,0:T(8,128)(2,1)S(1)}, bf16[2,16,1024]{2,1,0:T(8,128)(2,1)S(1)}, u32[]{:S(2)}, u32[]{:S(2)}) collective-permute-start(bf16[2,16,1024]{2,1,0:T(8,128)(2,1)S(1)} %get-tuple-element.38), channel_id=1, source_target_pairs={{0,8},{2,10},{4,12},{6,14},{8,0},{10,2},{12,4},{14,6},{1,9},{3,11}... | collective-permute-start | bytes 196616 | tf_op jit(solution)/shard_map/ppermute | solution.py:372
  41.7 1.4 %collective-permute-start.14 = (bf16[2,16,1024]{2,1,0:T(8,128)(2,1)S(1)}, bf16[2,16,1024]{2,1,0:T(8,128)(2,1)S(1)}, u32[]{:S(2)}, u32[]{:S(2)}) collective-permute-start(bf16[2,16,1024]{2,1,0:T(8,128)(2,1)S(1)} %get-tuple-element.39), channel_id=1, source_target_pairs={{0,12},{2,14},{4,8},{6,10},{8,4},{10,6},{12,0},{14,2},{1,13},{3,15... | collective-permute-start | bytes 196616 | tf_op jit(solution)/shard_map/ppermute | solution.py:372
  43.1 0.0 collective-permute-done.12.refs_1_
  43.1 5.5 %collective-permute-done.13.refs_2_ = bf16[2,16,1024]{2,1,0:T(8,128)(2,1)S(1)} collective-permute-done((bf16[2,16,1024]{2,1,0:T(8,128)(2,1)S(1)}, bf16[2,16,1024]{2,1,0:T(8,128)(2,1)S(1)}, u32[]{:S(2)}, u32[]{:S(2)}) %collective-permute-start.13) | collective-permute-done | bytes 65568 | tf_op jit(solution)/shard_map/ppermute | solution.py:372
  48.6 0.5 collective-permute-start.17
  49.1 0.1 collective-permute-start.18
  49.2 0.1 shard_map.123
  49.3 1.3 %collective-permute-start.22 = (bf16[2,16,1024]{2,1,0:T(8,128)(2,1)S(1)}, bf16[2,16,1024]{2,1,0:T(8,128)(2,1)S(1)}, u32[]{:S(2)}, u32[]{:S(2)}) collective-permute-start(bf16[2,16,1024]{2,1,0:T(8,128)(2,1)S(1)} %get-tuple-element.43), channel_id=1, source_target_pairs={{0,4},{2,6},{4,0},{6,2},{8,12},{10,14},{12,8},{14,10},{1,5},{3,7},... | collective-permute-start | bytes 196616 | tf_op jit(solution)/shard_map/ppermute | solution.py:372
  50.6 1.6 %collective-permute-start.23 = (bf16[2,16,1024]{2,1,0:T(8,128)(2,1)S(1)}, bf16[2,16,1024]{2,1,0:T(8,128)(2,1)S(1)}, u32[]{:S(2)}, u32[]{:S(2)}) collective-permute-start(bf16[2,16,1024]{2,1,0:T(8,128)(2,1)S(1)} %get-tuple-element.44), channel_id=1, source_target_pairs={{0,8},{2,10},{4,12},{6,14},{8,0},{10,2},{12,4},{14,6},{1,9},{3,11}... | collective-permute-start | bytes 196616 | tf_op jit(solution)/shard_map/ppermute | solution.py:372
  52.1 1.6 %collective-permute-start.24 = (bf16[2,16,1024]{2,1,0:T(8,128)(2,1)S(1)}, bf16[2,16,1024]{2,1,0:T(8,128)(2,1)S(1)}, u32[]{:S(2)}, u32[]{:S(2)}) collective-permute-start(bf16[2,16,1024]{2,1,0:T(8,128)(2,1)S(1)} %get-tuple-element.45), channel_id=1, source_target_pairs={{0,12},{2,14},{4,8},{6,10},{8,4},{10,6},{12,0},{14,2},{1,13},{3,15... | collective-permute-start | bytes 196616 | tf_op jit(solution)/shard_map/ppermute | solution.py:372
  53.7 1.0 %shard_map.122 = bf16[1024,128]{1,0:T(8,128)(2,1)} custom-call(bf16[2,16,1024]{2,1,0:T(8,128)(2,1)S(1)} %get-tuple-element.36.refs_0_, bf16[2,16,1024]{2,1,0:T(8,128)(2,1)S(1)} %collective-permute-done.12.refs_1_, bf16[2,16,1024]{2,1,0:T(8,128)(2,1)S(1)} %collective-permute-done.13.refs_2_, bf16[2,16,1024]{2,1,0:T(8,128)(2,1)S(1)} %collective-permute-done.14.refs_3_, ...), custom_call_target="tpu_custom_call" | custom-call | flops 100000000 | bytes 3000000 | tf_op jit(solution)/shard_map/pallas_call | solution.py:577
  54.7 4.2 %collective-permute-done.23.refs_2_ = bf16[2,16,1024]{2,1,0:T(8,128)(2,1)S(1)} collective-permute-done((bf16[2,16,1024]{2,1,0:T(8,128)(2,1)S(1)}, bf16[2,16,1024]{2,1,0:T(8,128)(2,1)S(1)}, u32[]{:S(2)}, u32[]{:S(2)}) %collective-permute-start.23) | collective-permute-done | bytes 65568 | tf_op jit(solution)/shard_map/ppermute | solution.py:372
  58.9 1.1 %shard_map.124 = f32[1024,128]{1,0:T(8,128)} custom-call(bf16[2,16,1024]{2,1,0:T(8,128)(2,1)S(1)} %get-tuple-element.42.refs_0_, bf16[2,16,1024]{2,1,0:T(8,128)(2,1)S(1)} %collective-permute-done.22.refs_1_, bf16[2,16,1024]{2,1,0:T(8,128)(2,1)S(1)} %collective-permute-done.23.refs_2_, bf16[2,16,1024]{2,1,0:T(8,128)(2,1)S(1)} %collective-permute-done.24.refs_3_), custom_call_target="tpu_custom_call" | custom-call | flops 100000000 | bytes 3000000 | tf_op jit(solution)/shard_map/pallas_call | solution.py:578
  (35 shorter events, 0.1 us)
Async XLA Ops:
  0.6 9.6 %copy-start = (bf16[1024,128]{1,0:T(8,128)(2,1)S(1)}, bf16[1024,128]{1,0:T(8,128)(2,1)}, u32[]{:S(2)}) copy-start(bf16[1024,128]{1,0:T(8,128)(2,1)} %param.12) | copy-start | bytes 786436
  0.6 11.3 %copy-start.6 = (bf16[1,1024,128]{2,1,0:T(8,128)(2,1)S(1)}, bf16[1,1024,128]{2,1,0:T(8,128)(2,1)}, u32[]{:S(2)}) copy-start(bf16[1,1024,128]{2,1,0:T(8,128)(2,1)} %param.10) | copy-start | bytes 786436
  0.7 9.6 %collective-permute-start.1 = (bf16[1024,128]{1,0:T(8,128)(2,1)}, bf16[1024,128]{1,0:T(8,128)(2,1)S(1)}, u32[]{:S(2)}, u32[]{:S(2)}) collective-permute-start(bf16[1024,128]{1,0:T(8,128)(2,1)} %bitcast.5), channel_id=1, source_target_pairs={{0,1},{1,0},{2,3},{3,2},{4,5},{5,4},{6,7},{7,6},{8,9},{9,8},{10,11... | collective-permute-start | bytes 786440 | tf_op jit(solution)/shard_map/ppermute | solution.py:366
  3.7 8.2 %collective-permute-start.6 = (bf16[1024,128]{1,0:T(8,128)(2,1)}, bf16[1024,128]{1,0:T(8,128)(2,1)S(1)}, u32[]{:S(2)}, u32[]{:S(2)}) collective-permute-start(bf16[1024,128]{1,0:T(8,128)(2,1)} %bitcast.3), channel_id=1, source_target_pairs={{0,2},{2,0},{4,6},{6,4},{8,10},{10,8},{12,14},{14,12},{1,3},{3,1},... | collective-permute-start | bytes 786440 | tf_op jit(solution)/shard_map/ppermute | solution.py:362
  3.7 13.1 %collective-permute-start = (bf16[1024,128]{1,0:T(8,128)(2,1)}, bf16[1024,128]{1,0:T(8,128)(2,1)S(1)}, u32[]{:S(2)}, u32[]{:S(2)}) collective-permute-start(bf16[1024,128]{1,0:T(8,128)(2,1)} %bitcast.6), channel_id=1, source_target_pairs={{0,2},{2,0},{4,6},{6,4},{8,10},{10,8},{12,14},{14,12},{1,3},{3,1},... | collective-permute-start | bytes 786440 | tf_op jit(solution)/shard_map/ppermute | solution.py:362
  10.2 6.9 %collective-permute-start.2 = (bf16[1024,128]{1,0:T(8,128)(2,1)S(1)}, bf16[1024,128]{1,0:T(8,128)(2,1)S(1)}, u32[]{:S(2)}, u32[]{:S(2)}) collective-permute-start(bf16[1024,128]{1,0:T(8,128)(2,1)S(1)} %collective-permute-done.1.other_ref), channel_id=1, source_target_pairs={{0,2},{2,0},{4,6},{6,4},{8,10},{10,8},{12,14},{14,12},{1,3},{3,1},... | collective-permute-start | bytes 786440 | tf_op jit(solution)/shard_map/ppermute | solution.py:362
  10.3 6.6 %copy-start.7 = (bf16[1,1024,128]{2,1,0:T(8,128)(2,1)S(1)}, bf16[1,1024,128]{2,1,0:T(8,128)(2,1)}, u32[]{:S(2)}) copy-start(bf16[1,1024,128]{2,1,0:T(8,128)(2,1)} %param.11) | copy-start | bytes 786436
  10.3 6.6 %copy-start.9 = (bf16[128,256]{1,0:T(8,128)(2,1)S(1)}, bf16[128,256]{1,0:T(8,128)(2,1)}, u32[]{:S(2)}) copy-start(bf16[128,256]{1,0:T(8,128)(2,1)} %proj_ref.1) | copy-start | bytes 196612
  10.3 1.7 %collective-permute-start.7 = (bf16[512,128]{1,0:T(8,128)(2,1)S(1)}, bf16[512,128]{1,0:T(8,128)(2,1)S(1)}, u32[]{:S(2)}, u32[]{:S(2)}) collective-permute-start(bf16[512,128]{1,0:T(8,128)(2,1)S(1)} %constant_dynamic-slice_fusion.taps_ref), channel_id=1, source_target_pairs={{0,2},{2,0},{4,6},{6,4},{8,10},{10,8},{12,14},{14,12},{1,3},{3,1},... | collective-permute-start | bytes 393224 | tf_op jit(solution)/shard_map/ppermute | solution.py:362
  12.4 9.6 %collective-permute-start.8 = (bf16[2,16,1536]{2,1,0:T(8,128)(2,1)S(1)}, bf16[2,16,1536]{2,1,0:T(8,128)(2,1)S(1)}, u32[]{:S(2)}, u32[]{:S(2)}) collective-permute-start(bf16[2,16,1536]{2,1,0:T(8,128)(2,1)S(1)} %get-tuple-element.32), channel_id=1, source_target_pairs={{0,4},{2,6},{4,0},{6,2},{8,12},{10,14},{12,8},{14,10},{1,5},{3,7},... | collective-permute-start | bytes 294920 | tf_op jit(solution)/shard_map/ppermute | solution.py:372
  14.2 10.9 %collective-permute-start.9 = (bf16[2,16,1536]{2,1,0:T(8,128)(2,1)S(1)}, bf16[2,16,1536]{2,1,0:T(8,128)(2,1)S(1)}, u32[]{:S(2)}, u32[]{:S(2)}) collective-permute-start(bf16[2,16,1536]{2,1,0:T(8,128)(2,1)S(1)} %get-tuple-element.33), channel_id=1, source_target_pairs={{0,8},{2,10},{4,12},{6,14},{8,0},{10,2},{12,4},{14,6},{1,9},{3,11}... | collective-permute-start | bytes 294920 | tf_op jit(solution)/shard_map/ppermute | solution.py:372
  16.8 8.3 %collective-permute-start.10 = (bf16[2,16,1536]{2,1,0:T(8,128)(2,1)S(1)}, bf16[2,16,1536]{2,1,0:T(8,128)(2,1)S(1)}, u32[]{:S(2)}, u32[]{:S(2)}) collective-permute-start(bf16[2,16,1536]{2,1,0:T(8,128)(2,1)S(1)} %get-tuple-element.34), channel_id=1, source_target_pairs={{0,12},{2,14},{4,8},{6,10},{8,4},{10,6},{12,0},{14,2},{1,13},{3,15... | collective-permute-start | bytes 294920 | tf_op jit(solution)/shard_map/ppermute | solution.py:372
  17.1 9.6 %copy-start.1 = (f32[2,128,1024]{2,1,0:T(8,128)S(1)}, f32[2,128,1024]{2,1,0:T(8,128)}, u32[]{:S(2)}) copy-start(f32[2,128,1024]{2,1,0:T(8,128)} %constant.26.clone.refs_5_.refs_7_.turn) | copy-start | bytes 3145732
  17.5 10.5 %collective-permute-start.3 = (bf16[2,16,1024]{2,1,0:T(8,128)(2,1)S(1)}, bf16[2,16,1024]{2,1,0:T(8,128)(2,1)S(1)}, u32[]{:S(2)}, u32[]{:S(2)}) collective-permute-start(bf16[2,16,1024]{2,1,0:T(8,128)(2,1)S(1)} %get-tuple-element.28), channel_id=1, source_target_pairs={{0,4},{2,6},{4,0},{6,2},{8,12},{10,14},{12,8},{14,10},{1,5},{3,7},... | collective-permute-start | bytes 196616 | tf_op jit(solution)/shard_map/ppermute | solution.py:372
  18.4 12.6 %collective-permute-start.4 = (bf16[2,16,1024]{2,1,0:T(8,128)(2,1)S(1)}, bf16[2,16,1024]{2,1,0:T(8,128)(2,1)S(1)}, u32[]{:S(2)}, u32[]{:S(2)}) collective-permute-start(bf16[2,16,1024]{2,1,0:T(8,128)(2,1)S(1)} %get-tuple-element.29), channel_id=1, source_target_pairs={{0,8},{2,10},{4,12},{6,14},{8,0},{10,2},{12,4},{14,6},{1,9},{3,11}... | collective-permute-start | bytes 196616 | tf_op jit(solution)/shard_map/ppermute | solution.py:372
  21.9 9.1 %collective-permute-start.5 = (bf16[2,16,1024]{2,1,0:T(8,128)(2,1)S(1)}, bf16[2,16,1024]{2,1,0:T(8,128)(2,1)S(1)}, u32[]{:S(2)}, u32[]{:S(2)}) collective-permute-start(bf16[2,16,1024]{2,1,0:T(8,128)(2,1)S(1)} %get-tuple-element.30), channel_id=1, source_target_pairs={{0,12},{2,14},{4,8},{6,10},{8,4},{10,6},{12,0},{14,2},{1,13},{3,15... | collective-permute-start | bytes 196616 | tf_op jit(solution)/shard_map/ppermute | solution.py:372
  25.1 1.7 %copy-start.2 = (bf16[2,256,256]{2,1,0:T(8,128)(2,1)S(1)}, bf16[2,256,256]{2,1,0:T(8,128)(2,1)}, u32[]{:S(2)}) copy-start(bf16[2,256,256]{2,1,0:T(8,128)(2,1)} %constant.28.clone.refs_7_.refs_9_.forward) | copy-start | bytes 786436
  25.1 1.7 %copy-start.3 = (bf16[2,256,128]{2,1,0:T(8,128)(2,1)S(1)}, bf16[2,256,128]{2,1,0:T(8,128)(2,1)}, u32[]{:S(2)}) copy-start(bf16[2,256,128]{2,1,0:T(8,128)(2,1)} %constant.24.clone.refs_4_.refs_5_.first) | copy-start | bytes 393220
  25.1 1.7 %copy-start.8 = (f32[2,8,128]{2,1,0:T(8,128)S(1)}, f32[2,8,128]{2,1,0:T(8,128)}, u32[]{:S(2)}) copy-start(f32[2,8,128]{2,1,0:T(8,128)} %constant.27.clone.refs_6_.refs_8_.small) | copy-start | bytes 24580
  25.2 5.9 %copy-start.4 = (bf16[2,256,256]{2,1,0:T(8,128)(2,1)S(1)}, bf16[2,256,256]{2,1,0:T(8,128)(2,1)}, u32[]{:S(2)}) copy-start(bf16[2,256,256]{2,1,0:T(8,128)(2,1)} %constant.29.clone.refs_10_.inverse) | copy-start | bytes 786436
  25.2 5.9 %copy-start.5 = (bf16[2,128,256]{2,1,0:T(8,128)(2,1)S(1)}, bf16[2,128,256]{2,1,0:T(8,128)(2,1)}, u32[]{:S(2)}) copy-start(bf16[2,128,256]{2,1,0:T(8,128)(2,1)} %constant.25.clone.refs_6_.last) | copy-start | bytes 393220
  25.2 8.7 %collective-permute-start.11 = (bf16[128,512]{1,0:T(8,128)(2,1)S(1)}, bf16[128,512]{1,0:T(8,128)(2,1)S(1)}, u32[]{:S(2)}, u32[]{:S(2)}) collective-permute-start(bf16[128,512]{1,0:T(8,128)(2,1)S(1)} %shard_map.119.own_ref), channel_id=1, source_target_pairs={{0,16},{16,0},{1,17},{17,1},{2,18},{18,2},{3,19},{19,3},{4,20},{20... | collective-permute-start | bytes 393224 | tf_op jit(solution)/shard_map/ppermute | solution.py:366
  33.8 2.9 %collective-permute-start.20 = (bf16[4,16,1024]{2,1,0:T(8,128)(2,1)S(1)}, bf16[4,16,1024]{2,1,0:T(8,128)(2,1)S(1)}, u32[]{:S(2)}, u32[]{:S(2)}) collective-permute-start(bf16[4,16,1024]{2,1,0:T(8,128)(2,1)S(1)} %get-tuple-element.41), channel_id=1, source_target_pairs={{0,2},{2,0},{4,6},{6,4},{8,10},{10,8},{12,14},{14,12},{1,3},{3,1},... | collective-permute-start | bytes 393224 | tf_op jit(solution)/shard_map/ppermute | solution.py:362
  35.1 14.0 %collective-permute-start.19 = (bf16[4,16,1024]{2,1,0:T(8,128)(2,1)S(1)}, bf16[4,16,1024]{2,1,0:T(8,128)(2,1)S(1)}, u32[]{:S(2)}, u32[]{:S(2)}) collective-permute-start(bf16[4,16,1024]{2,1,0:T(8,128)(2,1)S(1)} %get-tuple-element.40.mine_ref), channel_id=1, source_target_pairs={{0,16},{16,0},{1,17},{17,1},{2,18},{18,2},{3,19},{19,3},{4,20},{20... | collective-permute-start | bytes 393224 | tf_op jit(solution)/shard_map/ppermute | solution.py:366
  36.7 12.5 %collective-permute-start.21 = (bf16[4,16,1024]{2,1,0:T(8,128)(2,1)S(1)}, bf16[4,16,1024]{2,1,0:T(8,128)(2,1)S(1)}, u32[]{:S(2)}, u32[]{:S(2)}) collective-permute-start(bf16[4,16,1024]{2,1,0:T(8,128)(2,1)S(1)} %collective-permute-done.20.near_ref), channel_id=1, source_target_pairs={{0,16},{16,0},{1,17},{17,1},{2,18},{18,2},{3,19},{19,3},{4,20},{20... | collective-permute-start | bytes 393224 | tf_op jit(solution)/shard_map/ppermute | solution.py:366
  38.2 4.9 %collective-permute-start.12 = (bf16[2,16,1024]{2,1,0:T(8,128)(2,1)S(1)}, bf16[2,16,1024]{2,1,0:T(8,128)(2,1)S(1)}, u32[]{:S(2)}, u32[]{:S(2)}) collective-permute-start(bf16[2,16,1024]{2,1,0:T(8,128)(2,1)S(1)} %get-tuple-element.37), channel_id=1, source_target_pairs={{0,4},{2,6},{4,0},{6,2},{8,12},{10,14},{12,8},{14,10},{1,5},{3,7},... | collective-permute-start | bytes 196616 | tf_op jit(solution)/shard_map/ppermute | solution.py:372
  40.5 8.1 %collective-permute-start.13 = (bf16[2,16,1024]{2,1,0:T(8,128)(2,1)S(1)}, bf16[2,16,1024]{2,1,0:T(8,128)(2,1)S(1)}, u32[]{:S(2)}, u32[]{:S(2)}) collective-permute-start(bf16[2,16,1024]{2,1,0:T(8,128)(2,1)S(1)} %get-tuple-element.38), channel_id=1, source_target_pairs={{0,8},{2,10},{4,12},{6,14},{8,0},{10,2},{12,4},{14,6},{1,9},{3,11}... | collective-permute-start | bytes 196616 | tf_op jit(solution)/shard_map/ppermute | solution.py:372
  41.7 6.9 %collective-permute-start.14 = (bf16[2,16,1024]{2,1,0:T(8,128)(2,1)S(1)}, bf16[2,16,1024]{2,1,0:T(8,128)(2,1)S(1)}, u32[]{:S(2)}, u32[]{:S(2)}) collective-permute-start(bf16[2,16,1024]{2,1,0:T(8,128)(2,1)S(1)} %get-tuple-element.39), channel_id=1, source_target_pairs={{0,12},{2,14},{4,8},{6,10},{8,4},{10,6},{12,0},{14,2},{1,13},{3,15... | collective-permute-start | bytes 196616 | tf_op jit(solution)/shard_map/ppermute | solution.py:372
  43.1 7.4 %collective-permute-start.15 = (bf16[2,16,1024]{2,1,0:T(8,128)(2,1)S(1)}, bf16[2,16,1024]{2,1,0:T(8,128)(2,1)S(1)}, u32[]{:S(2)}, u32[]{:S(2)}) collective-permute-start(bf16[2,16,1024]{2,1,0:T(8,128)(2,1)S(1)} %get-tuple-element.36.refs_0_), channel_id=1, source_target_pairs={{0,2},{2,0},{4,6},{6,4},{8,10},{10,8},{12,14},{14,12},{1,3},{3,1},... | collective-permute-start | bytes 196616 | tf_op jit(solution)/shard_map/ppermute | solution.py:362
  48.6 3.5 %collective-permute-start.16 = (bf16[2,16,1024]{2,1,0:T(8,128)(2,1)S(1)}, bf16[2,16,1024]{2,1,0:T(8,128)(2,1)S(1)}, u32[]{:S(2)}, u32[]{:S(2)}) collective-permute-start(bf16[2,16,1024]{2,1,0:T(8,128)(2,1)S(1)} %collective-permute-done.12.refs_1_), channel_id=1, source_target_pairs={{0,2},{2,0},{4,6},{6,4},{8,10},{10,8},{12,14},{14,12},{1,3},{3,1},... | collective-permute-start | bytes 196616 | tf_op jit(solution)/shard_map/ppermute | solution.py:362
  48.6 5.1 %collective-permute-start.17 = (bf16[2,16,1024]{2,1,0:T(8,128)(2,1)S(1)}, bf16[2,16,1024]{2,1,0:T(8,128)(2,1)S(1)}, u32[]{:S(2)}, u32[]{:S(2)}) collective-permute-start(bf16[2,16,1024]{2,1,0:T(8,128)(2,1)S(1)} %collective-permute-done.13.refs_2_), channel_id=1, source_target_pairs={{0,2},{2,0},{4,6},{6,4},{8,10},{10,8},{12,14},{14,12},{1,3},{3,1},... | collective-permute-start | bytes 196616 | tf_op jit(solution)/shard_map/ppermute | solution.py:362
  49.1 4.6 %collective-permute-start.18 = (bf16[2,16,1024]{2,1,0:T(8,128)(2,1)S(1)}, bf16[2,16,1024]{2,1,0:T(8,128)(2,1)S(1)}, u32[]{:S(2)}, u32[]{:S(2)}) collective-permute-start(bf16[2,16,1024]{2,1,0:T(8,128)(2,1)S(1)} %collective-permute-done.14.refs_3_), channel_id=1, source_target_pairs={{0,2},{2,0},{4,6},{6,4},{8,10},{10,8},{12,14},{14,12},{1,3},{3,1},... | collective-permute-start | bytes 196616 | tf_op jit(solution)/shard_map/ppermute | solution.py:362
  49.3 5.5 %collective-permute-start.22 = (bf16[2,16,1024]{2,1,0:T(8,128)(2,1)S(1)}, bf16[2,16,1024]{2,1,0:T(8,128)(2,1)S(1)}, u32[]{:S(2)}, u32[]{:S(2)}) collective-permute-start(bf16[2,16,1024]{2,1,0:T(8,128)(2,1)S(1)} %get-tuple-element.43), channel_id=1, source_target_pairs={{0,4},{2,6},{4,0},{6,2},{8,12},{10,14},{12,8},{14,10},{1,5},{3,7},... | collective-permute-start | bytes 196616 | tf_op jit(solution)/shard_map/ppermute | solution.py:372
  50.6 8.3 %collective-permute-start.23 = (bf16[2,16,1024]{2,1,0:T(8,128)(2,1)S(1)}, bf16[2,16,1024]{2,1,0:T(8,128)(2,1)S(1)}, u32[]{:S(2)}, u32[]{:S(2)}) collective-permute-start(bf16[2,16,1024]{2,1,0:T(8,128)(2,1)S(1)} %get-tuple-element.44), channel_id=1, source_target_pairs={{0,8},{2,10},{4,12},{6,14},{8,0},{10,2},{12,4},{14,6},{1,9},{3,11}... | collective-permute-start | bytes 196616 | tf_op jit(solution)/shard_map/ppermute | solution.py:372
  52.1 6.8 %collective-permute-start.24 = (bf16[2,16,1024]{2,1,0:T(8,128)(2,1)S(1)}, bf16[2,16,1024]{2,1,0:T(8,128)(2,1)S(1)}, u32[]{:S(2)}, u32[]{:S(2)}) collective-permute-start(bf16[2,16,1024]{2,1,0:T(8,128)(2,1)S(1)} %get-tuple-element.45), channel_id=1, source_target_pairs={{0,12},{2,14},{4,8},{6,10},{8,4},{10,6},{12,0},{14,2},{1,13},{3,15... | collective-permute-start | bytes 196616 | tf_op jit(solution)/shard_map/ppermute | solution.py:372

commit v4 on v3

--- a/solution.py
+++ b/solution.py
@@ -179,11 +179,9 @@
 
 
 def collapse(last, gathered):
-    right = gathered[...]
-    return dot(
-        jnp.concatenate([last[0], last[1]], axis=1),
-        jnp.concatenate([right, right], axis=0),
-    )
+    rows = last.shape[1]
+    both = dot(jnp.concatenate([last[0], last[1]], axis=0), gathered[...])
+    return both[:rows] + both[rows:]
 
 
 def identity(size, dtype):
@@ -475,16 +473,9 @@
     def span(group):
         return slice(group * tiles * GROUP, (group + 1) * tiles * GROUP)
 
-    def filter_kernel(*refs):
-        recv, rest = refs[:chips], refs[chips:]
-        (input_ref, first, last, turn, small, forward, inverse, grad, mine_ref, theirs_ref,
-         block, stage, high, low, back, back_high, wide) = rest
-        take(recv, front, block)
-        spread(block[...], first, stage)
+    def filter_kernel(grad, input_ref, last, turn, small, inverse, mine_ref, theirs_ref, back, back_high, wide):
         for group in range(count_groups):
-            value = forward_group(group, turn, small, forward, stage, high, low, rows, tiles)
-            grad[span(group), :] = value
-            product = correlate(value, input_ref[span(group), :])
+            product = correlate(grad[span(group), :], input_ref[span(group), :])
             inverse_group(group, product, turn, small, inverse, back, back_high, rows, tiles)
         wide[...] = collapse(last, back_high)
         cut(wide, mine_ref, theirs_ref)
@@ -556,12 +547,12 @@
     input_spec = call(signal_kernel, spec_shape, transform_scratch, 6 * 10**6)(
         *early, first, turn, small, forward
     )
-    grad_spec, mine, theirs = call(
-        filter_kernel,
-        (spec_shape,) + halves,
-        [block_scratch, stage_scratch] + half_pair + [spec_scratch] + back_one + [flat],
-        12 * 10**6,
-    )(*late, input_spec, first, last, turn, small, forward, inverse)
+    grad_spec = call(signal_kernel, spec_shape, transform_scratch, 6 * 10**6)(
+        *late, first, turn, small, forward
+    )
+    mine, theirs = call(
+        filter_kernel, halves, [spec_scratch] + back_one + [flat], 6 * 10**6
+    )(grad_spec, input_spec, last, turn, small, inverse)
     mine_other = cross(mine, "rep")
     near = swap(theirs)
     near_other = cross(near, "rep")

time: 60.1 us -> 59.6 us (level)
    pallas_call x1, Pallas kernels: 2.81 us -> 1.02 us  [per_device_near(): call(filter_kernel, halves, [spec_scratch] + back_one + [flat], 6 * 10 ** 6)]
    pallas_call x1 -> x2, Pallas kernels: 1.22 us -> 2.42 us  [per_device_near(): call(signal_kernel, spec_shape, transform_scratch, 6 * 10 ** 6)]
  transfers between devices with their start and end apart: 25 -> 25, of which waited for: 6 -> 6; matrix products, arithmetic and copies ran while one was open for 0% -> 0% of each run, Pallas kernels for 14% -> 13%
where the time goes in v4:
time: 59.6 us; the launch traced here: 59.4 us
  starting transfers between devices  27.1 us (45%)
  waiting for transfers between devices  22.7 us (38%)
  Pallas kernels  8.81 us (15%)
  between operations  0.82 us (1%)
    ppermute x12, starting transfers between devices, exchange(): got.append(lax.ppermute(sent[offset], 'seq', pairs))  18.6 us
    ppermute x12, waiting for transfers between devices, exchange(): got.append(lax.ppermute(sent[offset], 'seq', pairs))  15.5 us
    ppermute x4, starting transfers between devices, cross(): return lax.ppermute(value, axis, [(k, (k + 1) % size) for k in range(size)])  6.74 us
    ppermute x4, waiting for transfers between devices, cross(): return lax.ppermute(value, axis, [(k, (k + 1) % size) for k in range(size)])  6.01 us
    pallas_call x2, Pallas kernels, per_device_near(): call(signal_kernel, spec_shape, transform_scratch, 6 * 10 ** 6)  2.42 us
    ppermute x9, starting transfers between devices, swap(): return lax.ppermute(value, 'seq', swap_pairs)  1.74 us
    pallas_call x1, Pallas kernels, per_device_near(): call(taps_spec_kernel, spec_shape, transform_scratch, 6 * 10 ** 6)  1.2 us
  transfers between devices with their start and end apart: 25, of which 6 were waited for; matrix products, arithmetic and copies ran while one was open for 0% of the time, Pallas kernels for 13%

profile of v4, /device:TPU:0, one launch (start us, length us, event | category | flops | bytes accessed | tf_op | source)
XLA Modules:
  0.0 59.4 jit_solution(13212815321878495420)
XLA Ops:
  0.6 0.0 copy-start
  0.7 3.1 %collective-permute-start.1 = (bf16[1024,128]{1,0:T(8,128)(2,1)}, bf16[1024,128]{1,0:T(8,128)(2,1)S(1)}, u32[]{:S(2)}, u32[]{:S(2)}) collective-permute-start(bf16[1024,128]{1,0:T(8,128)(2,1)} %bitcast.5), channel_id=1, source_target_pairs={{0,1},{1,0},{2,3},{3,2},{4,5},{5,4},{6,7},{7,6},{8,9},{9,8},{10,11... | collective-permute-start | bytes 786440 | tf_op jit(solution)/shard_map/ppermute | solution.py:364
  3.7 0.0 collective-permute-start.6
  3.7 0.5 collective-permute-start
  4.2 6.0 %collective-permute-done.1.other_ref = bf16[1024,128]{1,0:T(8,128)(2,1)S(1)} collective-permute-done((bf16[1024,128]{1,0:T(8,128)(2,1)}, bf16[1024,128]{1,0:T(8,128)(2,1)S(1)}, u32[]{:S(2)}, u32[]{:S(2)}) %collective-permute-start.1) | collective-permute-done | bytes 262176 | tf_op jit(solution)/shard_map/ppermute | solution.py:364
  10.2 0.0 collective-permute-start.2
  10.3 0.0 copy-start.7
  10.3 0.0 copy-start.9
  10.3 0.6 collective-permute-start.7
  10.8 1.1 %collective-permute-done.7.taps_near = bf16[512,128]{1,0:T(8,128)(2,1)S(1)} collective-permute-done((bf16[512,128]{1,0:T(8,128)(2,1)S(1)}, bf16[512,128]{1,0:T(8,128)(2,1)S(1)}, u32[]{:S(2)}, u32[]{:S(2)}) %collective-permute-start.7) | collective-permute-done | bytes 131104 | tf_op jit(solution)/shard_map/ppermute | solution.py:360
  12.0 0.4 shard_map.117
  12.4 1.9 %collective-permute-start.8 = (bf16[2,16,1536]{2,1,0:T(8,128)(2,1)S(1)}, bf16[2,16,1536]{2,1,0:T(8,128)(2,1)S(1)}, u32[]{:S(2)}, u32[]{:S(2)}) collective-permute-start(bf16[2,16,1536]{2,1,0:T(8,128)(2,1)S(1)} %get-tuple-element.31), channel_id=1, source_target_pairs={{0,4},{2,6},{4,0},{6,2},{8,12},{10,14},{12,8},{14,10},{1,5},{3,7},... | collective-permute-start | bytes 294920 | tf_op jit(solution)/shard_map/ppermute | solution.py:370
  14.2 2.6 %collective-permute-start.9 = (bf16[2,16,1536]{2,1,0:T(8,128)(2,1)S(1)}, bf16[2,16,1536]{2,1,0:T(8,128)(2,1)S(1)}, u32[]{:S(2)}, u32[]{:S(2)}) collective-permute-start(bf16[2,16,1536]{2,1,0:T(8,128)(2,1)S(1)} %get-tuple-element.32), channel_id=1, source_target_pairs={{0,8},{2,10},{4,12},{6,14},{8,0},{10,2},{12,4},{14,6},{1,9},{3,11}... | collective-permute-start | bytes 294920 | tf_op jit(solution)/shard_map/ppermute | solution.py:370
  16.8 0.3 shard_map.113
  17.1 0.0 copy-start.1
  17.2 0.3 shard_map.114
  17.5 0.9 %collective-permute-start.3 = (bf16[2,16,1024]{2,1,0:T(8,128)(2,1)S(1)}, bf16[2,16,1024]{2,1,0:T(8,128)(2,1)S(1)}, u32[]{:S(2)}, u32[]{:S(2)}) collective-permute-start(bf16[2,16,1024]{2,1,0:T(8,128)(2,1)S(1)} %get-tuple-element.27), channel_id=1, source_target_pairs={{0,4},{2,6},{4,0},{6,2},{8,12},{10,14},{12,8},{14,10},{1,5},{3,7},... | collective-permute-start | bytes 196616 | tf_op jit(solution)/shard_map/ppermute | solution.py:370
  18.4 3.5 %collective-permute-start.4 = (bf16[2,16,1024]{2,1,0:T(8,128)(2,1)S(1)}, bf16[2,16,1024]{2,1,0:T(8,128)(2,1)S(1)}, u32[]{:S(2)}, u32[]{:S(2)}) collective-permute-start(bf16[2,16,1024]{2,1,0:T(8,128)(2,1)S(1)} %get-tuple-element.28), channel_id=1, source_target_pairs={{0,8},{2,10},{4,12},{6,14},{8,0},{10,2},{12,4},{14,6},{1,9},{3,11}... | collective-permute-start | bytes 196616 | tf_op jit(solution)/shard_map/ppermute | solution.py:370
  21.9 0.0 collective-permute-done.8.refs_1_
  21.9 0.3 collective-permute-start.5
  22.3 2.8 %collective-permute-done.9.refs_2_ = bf16[2,16,1536]{2,1,0:T(8,128)(2,1)S(1)} collective-permute-done((bf16[2,16,1536]{2,1,0:T(8,128)(2,1)S(1)}, bf16[2,16,1536]{2,1,0:T(8,128)(2,1)S(1)}, u32[]{:S(2)}, u32[]{:S(2)}) %collective-permute-start.9) | collective-permute-done | bytes 98336 | tf_op jit(solution)/shard_map/ppermute | solution.py:370
  25.1 0.0 collective-permute-done.10.refs_3_
  25.2 1.6 %collective-permute-start.11 = (bf16[128,512]{1,0:T(8,128)(2,1)S(1)}, bf16[128,512]{1,0:T(8,128)(2,1)S(1)}, u32[]{:S(2)}, u32[]{:S(2)}) collective-permute-start(bf16[128,512]{1,0:T(8,128)(2,1)S(1)} %shard_map.118.own_ref), channel_id=1, source_target_pairs={{0,16},{16,0},{1,17},{17,1},{2,18},{18,2},{3,19},{19,3},{4,20},{20... | collective-permute-start | bytes 393224 | tf_op jit(solution)/shard_map/ppermute | solution.py:364
  26.8 1.2 %shard_map.122.input_ref = f32[1024,256]{1,0:T(8,128)S(1)} custom-call(bf16[2,16,1536]{2,1,0:T(8,128)(2,1)S(1)} %get-tuple-element.30.refs_0_, bf16[2,16,1536]{2,1,0:T(8,128)(2,1)S(1)} %collective-permute-done.8.refs_1_, bf16[2,16,1536]{2,1,0:T(8,128)(2,1)S(1)} %collective-permute-done.9.refs_2_, bf16[2,16,1536]{2,1,0:T(8,128)(2,1)S(1)} %collective-permute-done.10.refs_3_, ...), custom_call_target="tpu_custom_call" | custom-call | flops 100000000 | bytes 6000000 | tf_op jit(solution)/shard_map/pallas_call | solution.py:547
  28.0 0.0 collective-permute-done.3.refs_1_
  28.0 3.0 %collective-permute-done.4.refs_2_ = bf16[2,16,1024]{2,1,0:T(8,128)(2,1)S(1)} collective-permute-done((bf16[2,16,1024]{2,1,0:T(8,128)(2,1)S(1)}, bf16[2,16,1024]{2,1,0:T(8,128)(2,1)S(1)}, u32[]{:S(2)}, u32[]{:S(2)}) %collective-permute-start.4) | collective-permute-done | bytes 65568 | tf_op jit(solution)/shard_map/ppermute | solution.py:370
  31.0 0.0 collective-permute-done.5.refs_3_
  31.0 1.2 %shard_map.115.grad = f32[1024,256]{1,0:T(8,128)S(1)} custom-call(bf16[2,16,1024]{2,1,0:T(8,128)(2,1)S(1)} %get-tuple-element.26.refs_0_, bf16[2,16,1024]{2,1,0:T(8,128)(2,1)S(1)} %collective-permute-done.3.refs_1_, bf16[2,16,1024]{2,1,0:T(8,128)(2,1)S(1)} %collective-permute-done.4.refs_2_, bf16[2,16,1024]{2,1,0:T(8,128)(2,1)S(1)} %collective-permute-done.5.refs_3_, ...), custom_call_target="tpu_custom_call" | custom-call | flops 100000000 | bytes 6000000 | tf_op jit(solution)/shard_map/pallas_call | solution.py:550
  32.3 1.0 %shard_map.123 = (bf16[4,16,1024]{2,1,0:T(8,128)(2,1)S(1)}, bf16[4,16,1024]{2,1,0:T(8,128)(2,1)S(1)}) custom-call(f32[1024,256]{1,0:T(8,128)S(1)} %shard_map.115.grad, f32[1024,256]{1,0:T(8,128)S(1)} %shard_map.122.input_ref, bf16[2,128,256]{2,1,0:T(8,128)(2,1)S(1)} %copy-done.5, f32[2,128,1024]{2,1,0:T(8,128)S(1)} %copy-done.1, f32[2,8,128]{2,1,0:T(8,128)S(1)} %copy-done.8, ...), custom_call_target="tpu_custom_call" | custom-call | flops 100000000 | bytes 6000000 | tf_op jit(solution)/shard_map/pallas_call | solution.py:553
  33.3 0.1 collective-permute-start.20
  33.4 1.2 %shard_map.119.taps_ref = f32[1024,256]{1,0:T(8,128)S(1)} custom-call(bf16[128,512]{1,0:T(8,128)(2,1)S(1)} %shard_map.118.own_ref, bf16[128,512]{1,0:T(8,128)(2,1)S(1)} %collective-permute-done.11.other_ref, bf16[2,256,128]{2,1,0:T(8,128)(2,1)S(1)} %copy-done.3, f32[2,128,1024]{2,1,0:T(8,128)S(1)} %copy-done.1, f32[2,8,128]{2,1,0:T(8,128)S(1)} %copy-done.8, ...), custom_call_target="tpu_custom_call" | custom-call | flops 100000000 | bytes 6000000 | tf_op jit(solution)/shard_map/pallas_call | solution.py:559
  34.6 1.6 %collective-permute-start.19 = (bf16[4,16,1024]{2,1,0:T(8,128)(2,1)S(1)}, bf16[4,16,1024]{2,1,0:T(8,128)(2,1)S(1)}, u32[]{:S(2)}, u32[]{:S(2)}) collective-permute-start(bf16[4,16,1024]{2,1,0:T(8,128)(2,1)S(1)} %get-tuple-element.38.mine_ref), channel_id=1, source_target_pairs={{0,16},{16,0},{1,17},{17,1},{2,18},{18,2},{3,19},{19,3},{4,20},{20... | collective-permute-start | bytes 393224 | tf_op jit(solution)/shard_map/ppermute | solution.py:364
  36.1 0.5 collective-permute-start.21
  36.7 1.0 %shard_map.120 = (bf16[2,16,1024]{2,1,0:T(8,128)(2,1)S(1)}, bf16[2,16,1024]{2,1,0:T(8,128)(2,1)S(1)}, bf16[2,16,1024]{2,1,0:T(8,128)(2,1)S(1)}, bf16[2,16,1024]{2,1,0:T(8,128)(2,1)S(1)}) custom-call(f32[1024,256]{1,0:T(8,128)S(1)} %shard_map.115.grad, f32[1024,256]{1,0:T(8,128)S(1)} %shard_map.119.taps_ref, bf16[2,128,256]{2,1,0:T(8,128)(2,1)S(1)} %copy-done.5, ...), custom_call_target="tpu_custom_call" | custom-call | flops 100000000 | bytes 6000000 | tf_op jit(solution)/shard_map/pallas_call | solution.py:562
  37.7 2.2 %collective-permute-start.12 = (bf16[2,16,1024]{2,1,0:T(8,128)(2,1)S(1)}, bf16[2,16,1024]{2,1,0:T(8,128)(2,1)S(1)}, u32[]{:S(2)}, u32[]{:S(2)}) collective-permute-start(bf16[2,16,1024]{2,1,0:T(8,128)(2,1)S(1)} %get-tuple-element.35), channel_id=1, source_target_pairs={{0,4},{2,6},{4,0},{6,2},{8,12},{10,14},{12,8},{14,10},{1,5},{3,7},... | collective-permute-start | bytes 196616 | tf_op jit(solution)/shard_map/ppermute | solution.py:370
  39.9 1.3 %collective-permute-start.13 = (bf16[2,16,1024]{2,1,0:T(8,128)(2,1)S(1)}, bf16[2,16,1024]{2,1,0:T(8,128)(2,1)S(1)}, u32[]{:S(2)}, u32[]{:S(2)}) collective-permute-start(bf16[2,16,1024]{2,1,0:T(8,128)(2,1)S(1)} %get-tuple-element.36), channel_id=1, source_target_pairs={{0,8},{2,10},{4,12},{6,14},{8,0},{10,2},{12,4},{14,6},{1,9},{3,11}... | collective-permute-start | bytes 196616 | tf_op jit(solution)/shard_map/ppermute | solution.py:370
  41.2 1.4 %collective-permute-start.14 = (bf16[2,16,1024]{2,1,0:T(8,128)(2,1)S(1)}, bf16[2,16,1024]{2,1,0:T(8,128)(2,1)S(1)}, u32[]{:S(2)}, u32[]{:S(2)}) collective-permute-start(bf16[2,16,1024]{2,1,0:T(8,128)(2,1)S(1)} %get-tuple-element.37), channel_id=1, source_target_pairs={{0,12},{2,14},{4,8},{6,10},{8,4},{10,6},{12,0},{14,2},{1,13},{3,15... | collective-permute-start | bytes 196616 | tf_op jit(solution)/shard_map/ppermute | solution.py:370
  42.6 0.0 collective-permute-done.12.refs_1_
  42.6 5.5 %collective-permute-done.13.refs_2_ = bf16[2,16,1024]{2,1,0:T(8,128)(2,1)S(1)} collective-permute-done((bf16[2,16,1024]{2,1,0:T(8,128)(2,1)S(1)}, bf16[2,16,1024]{2,1,0:T(8,128)(2,1)S(1)}, u32[]{:S(2)}, u32[]{:S(2)}) %collective-permute-start.13) | collective-permute-done | bytes 65568 | tf_op jit(solution)/shard_map/ppermute | solution.py:370
  48.0 0.5 collective-permute-start.17
  48.5 0.1 collective-permute-start.18
  48.6 0.1 shard_map.124
  48.7 1.3 %collective-permute-start.22 = (bf16[2,16,1024]{2,1,0:T(8,128)(2,1)S(1)}, bf16[2,16,1024]{2,1,0:T(8,128)(2,1)S(1)}, u32[]{:S(2)}, u32[]{:S(2)}) collective-permute-start(bf16[2,16,1024]{2,1,0:T(8,128)(2,1)S(1)} %get-tuple-element.41), channel_id=1, source_target_pairs={{0,4},{2,6},{4,0},{6,2},{8,12},{10,14},{12,8},{14,10},{1,5},{3,7},... | collective-permute-start | bytes 196616 | tf_op jit(solution)/shard_map/ppermute | solution.py:370
  50.0 1.6 %collective-permute-start.23 = (bf16[2,16,1024]{2,1,0:T(8,128)(2,1)S(1)}, bf16[2,16,1024]{2,1,0:T(8,128)(2,1)S(1)}, u32[]{:S(2)}, u32[]{:S(2)}) collective-permute-start(bf16[2,16,1024]{2,1,0:T(8,128)(2,1)S(1)} %get-tuple-element.42), channel_id=1, source_target_pairs={{0,8},{2,10},{4,12},{6,14},{8,0},{10,2},{12,4},{14,6},{1,9},{3,11}... | collective-permute-start | bytes 196616 | tf_op jit(solution)/shard_map/ppermute | solution.py:370
  51.6 1.6 %collective-permute-start.24 = (bf16[2,16,1024]{2,1,0:T(8,128)(2,1)S(1)}, bf16[2,16,1024]{2,1,0:T(8,128)(2,1)S(1)}, u32[]{:S(2)}, u32[]{:S(2)}) collective-permute-start(bf16[2,16,1024]{2,1,0:T(8,128)(2,1)S(1)} %get-tuple-element.43), channel_id=1, source_target_pairs={{0,12},{2,14},{4,8},{6,10},{8,4},{10,6},{12,0},{14,2},{1,13},{3,15... | collective-permute-start | bytes 196616 | tf_op jit(solution)/shard_map/ppermute | solution.py:370
  53.1 1.0 %shard_map.121 = bf16[1024,128]{1,0:T(8,128)(2,1)} custom-call(bf16[2,16,1024]{2,1,0:T(8,128)(2,1)S(1)} %get-tuple-element.34.refs_0_, bf16[2,16,1024]{2,1,0:T(8,128)(2,1)S(1)} %collective-permute-done.12.refs_1_, bf16[2,16,1024]{2,1,0:T(8,128)(2,1)S(1)} %collective-permute-done.13.refs_2_, bf16[2,16,1024]{2,1,0:T(8,128)(2,1)S(1)} %collective-permute-done.14.refs_3_, ...), custom_call_target="tpu_custom_call" | custom-call | flops 100000000 | bytes 3000000 | tf_op jit(solution)/shard_map/pallas_call | solution.py:568
  54.1 4.2 %collective-permute-done.23.refs_2_ = bf16[2,16,1024]{2,1,0:T(8,128)(2,1)S(1)} collective-permute-done((bf16[2,16,1024]{2,1,0:T(8,128)(2,1)S(1)}, bf16[2,16,1024]{2,1,0:T(8,128)(2,1)S(1)}, u32[]{:S(2)}, u32[]{:S(2)}) %collective-permute-start.23) | collective-permute-done | bytes 65568 | tf_op jit(solution)/shard_map/ppermute | solution.py:370
  58.3 1.1 %shard_map.125 = f32[1024,128]{1,0:T(8,128)} custom-call(bf16[2,16,1024]{2,1,0:T(8,128)(2,1)S(1)} %get-tuple-element.40.refs_0_, bf16[2,16,1024]{2,1,0:T(8,128)(2,1)S(1)} %collective-permute-done.22.refs_1_, bf16[2,16,1024]{2,1,0:T(8,128)(2,1)S(1)} %collective-permute-done.23.refs_2_, bf16[2,16,1024]{2,1,0:T(8,128)(2,1)S(1)} %collective-permute-done.24.refs_3_), custom_call_target="tpu_custom_call" | custom-call | flops 100000000 | bytes 3000000 | tf_op jit(solution)/shard_map/pallas_call | solution.py:569
  (36 shorter events, 0.1 us)
Async XLA Ops:
  0.6 9.6 %copy-start = (bf16[1024,128]{1,0:T(8,128)(2,1)S(1)}, bf16[1024,128]{1,0:T(8,128)(2,1)}, u32[]{:S(2)}) copy-start(bf16[1024,128]{1,0:T(8,128)(2,1)} %param.12) | copy-start | bytes 786436
  0.6 11.3 %copy-start.6 = (bf16[1,1024,128]{2,1,0:T(8,128)(2,1)S(1)}, bf16[1,1024,128]{2,1,0:T(8,128)(2,1)}, u32[]{:S(2)}) copy-start(bf16[1,1024,128]{2,1,0:T(8,128)(2,1)} %param.10) | copy-start | bytes 786436
  0.7 9.6 %collective-permute-start.1 = (bf16[1024,128]{1,0:T(8,128)(2,1)}, bf16[1024,128]{1,0:T(8,128)(2,1)S(1)}, u32[]{:S(2)}, u32[]{:S(2)}) collective-permute-start(bf16[1024,128]{1,0:T(8,128)(2,1)} %bitcast.5), channel_id=1, source_target_pairs={{0,1},{1,0},{2,3},{3,2},{4,5},{5,4},{6,7},{7,6},{8,9},{9,8},{10,11... | collective-permute-start | bytes 786440 | tf_op jit(solution)/shard_map/ppermute | solution.py:364
  3.7 8.2 %collective-permute-start.6 = (bf16[1024,128]{1,0:T(8,128)(2,1)}, bf16[1024,128]{1,0:T(8,128)(2,1)S(1)}, u32[]{:S(2)}, u32[]{:S(2)}) collective-permute-start(bf16[1024,128]{1,0:T(8,128)(2,1)} %bitcast.3), channel_id=1, source_target_pairs={{0,2},{2,0},{4,6},{6,4},{8,10},{10,8},{12,14},{14,12},{1,3},{3,1},... | collective-permute-start | bytes 786440 | tf_op jit(solution)/shard_map/ppermute | solution.py:360
  3.7 13.1 %collective-permute-start = (bf16[1024,128]{1,0:T(8,128)(2,1)}, bf16[1024,128]{1,0:T(8,128)(2,1)S(1)}, u32[]{:S(2)}, u32[]{:S(2)}) collective-permute-start(bf16[1024,128]{1,0:T(8,128)(2,1)} %bitcast.6), channel_id=1, source_target_pairs={{0,2},{2,0},{4,6},{6,4},{8,10},{10,8},{12,14},{14,12},{1,3},{3,1},... | collective-permute-start | bytes 786440 | tf_op jit(solution)/shard_map/ppermute | solution.py:360
  10.2 6.9 %collective-permute-start.2 = (bf16[1024,128]{1,0:T(8,128)(2,1)S(1)}, bf16[1024,128]{1,0:T(8,128)(2,1)S(1)}, u32[]{:S(2)}, u32[]{:S(2)}) collective-permute-start(bf16[1024,128]{1,0:T(8,128)(2,1)S(1)} %collective-permute-done.1.other_ref), channel_id=1, source_target_pairs={{0,2},{2,0},{4,6},{6,4},{8,10},{10,8},{12,14},{14,12},{1,3},{3,1},... | collective-permute-start | bytes 786440 | tf_op jit(solution)/shard_map/ppermute | solution.py:360
  10.3 6.6 %copy-start.7 = (bf16[1,1024,128]{2,1,0:T(8,128)(2,1)S(1)}, bf16[1,1024,128]{2,1,0:T(8,128)(2,1)}, u32[]{:S(2)}) copy-start(bf16[1,1024,128]{2,1,0:T(8,128)(2,1)} %param.11) | copy-start | bytes 786436
  10.3 6.6 %copy-start.9 = (bf16[128,256]{1,0:T(8,128)(2,1)S(1)}, bf16[128,256]{1,0:T(8,128)(2,1)}, u32[]{:S(2)}) copy-start(bf16[128,256]{1,0:T(8,128)(2,1)} %proj_ref.1) | copy-start | bytes 196612
  10.3 1.7 %collective-permute-start.7 = (bf16[512,128]{1,0:T(8,128)(2,1)S(1)}, bf16[512,128]{1,0:T(8,128)(2,1)S(1)}, u32[]{:S(2)}, u32[]{:S(2)}) collective-permute-start(bf16[512,128]{1,0:T(8,128)(2,1)S(1)} %constant_dynamic-slice_fusion.taps_ref), channel_id=1, source_target_pairs={{0,2},{2,0},{4,6},{6,4},{8,10},{10,8},{12,14},{14,12},{1,3},{3,1},... | collective-permute-start | bytes 393224 | tf_op jit(solution)/shard_map/ppermute | solution.py:360
  12.4 9.6 %collective-permute-start.8 = (bf16[2,16,1536]{2,1,0:T(8,128)(2,1)S(1)}, bf16[2,16,1536]{2,1,0:T(8,128)(2,1)S(1)}, u32[]{:S(2)}, u32[]{:S(2)}) collective-permute-start(bf16[2,16,1536]{2,1,0:T(8,128)(2,1)S(1)} %get-tuple-element.31), channel_id=1, source_target_pairs={{0,4},{2,6},{4,0},{6,2},{8,12},{10,14},{12,8},{14,10},{1,5},{3,7},... | collective-permute-start | bytes 294920 | tf_op jit(solution)/shard_map/ppermute | solution.py:370
  14.2 10.9 %collective-permute-start.9 = (bf16[2,16,1536]{2,1,0:T(8,128)(2,1)S(1)}, bf16[2,16,1536]{2,1,0:T(8,128)(2,1)S(1)}, u32[]{:S(2)}, u32[]{:S(2)}) collective-permute-start(bf16[2,16,1536]{2,1,0:T(8,128)(2,1)S(1)} %get-tuple-element.32), channel_id=1, source_target_pairs={{0,8},{2,10},{4,12},{6,14},{8,0},{10,2},{12,4},{14,6},{1,9},{3,11}... | collective-permute-start | bytes 294920 | tf_op jit(solution)/shard_map/ppermute | solution.py:370
  16.8 8.3 %collective-permute-start.10 = (bf16[2,16,1536]{2,1,0:T(8,128)(2,1)S(1)}, bf16[2,16,1536]{2,1,0:T(8,128)(2,1)S(1)}, u32[]{:S(2)}, u32[]{:S(2)}) collective-permute-start(bf16[2,16,1536]{2,1,0:T(8,128)(2,1)S(1)} %get-tuple-element.33), channel_id=1, source_target_pairs={{0,12},{2,14},{4,8},{6,10},{8,4},{10,6},{12,0},{14,2},{1,13},{3,15... | collective-permute-start | bytes 294920 | tf_op jit(solution)/shard_map/ppermute | solution.py:370
  17.1 9.6 %copy-start.1 = (f32[2,128,1024]{2,1,0:T(8,128)S(1)}, f32[2,128,1024]{2,1,0:T(8,128)}, u32[]{:S(2)}) copy-start(f32[2,128,1024]{2,1,0:T(8,128)} %constant.26.clone.refs_5_.turn) | copy-start | bytes 3145732
  17.5 10.5 %collective-permute-start.3 = (bf16[2,16,1024]{2,1,0:T(8,128)(2,1)S(1)}, bf16[2,16,1024]{2,1,0:T(8,128)(2,1)S(1)}, u32[]{:S(2)}, u32[]{:S(2)}) collective-permute-start(bf16[2,16,1024]{2,1,0:T(8,128)(2,1)S(1)} %get-tuple-element.27), channel_id=1, source_target_pairs={{0,4},{2,6},{4,0},{6,2},{8,12},{10,14},{12,8},{14,10},{1,5},{3,7},... | collective-permute-start | bytes 196616 | tf_op jit(solution)/shard_map/ppermute | solution.py:370
  18.4 12.6 %collective-permute-start.4 = (bf16[2,16,1024]{2,1,0:T(8,128)(2,1)S(1)}, bf16[2,16,1024]{2,1,0:T(8,128)(2,1)S(1)}, u32[]{:S(2)}, u32[]{:S(2)}) collective-permute-start(bf16[2,16,1024]{2,1,0:T(8,128)(2,1)S(1)} %get-tuple-element.28), channel_id=1, source_target_pairs={{0,8},{2,10},{4,12},{6,14},{8,0},{10,2},{12,4},{14,6},{1,9},{3,11}... | collective-permute-start | bytes 196616 | tf_op jit(solution)/shard_map/ppermute | solution.py:370
  21.9 9.1 %collective-permute-start.5 = (bf16[2,16,1024]{2,1,0:T(8,128)(2,1)S(1)}, bf16[2,16,1024]{2,1,0:T(8,128)(2,1)S(1)}, u32[]{:S(2)}, u32[]{:S(2)}) collective-permute-start(bf16[2,16,1024]{2,1,0:T(8,128)(2,1)S(1)} %get-tuple-element.29), channel_id=1, source_target_pairs={{0,12},{2,14},{4,8},{6,10},{8,4},{10,6},{12,0},{14,2},{1,13},{3,15... | collective-permute-start | bytes 196616 | tf_op jit(solution)/shard_map/ppermute | solution.py:370
  25.1 1.6 %copy-start.2 = (bf16[2,256,256]{2,1,0:T(8,128)(2,1)S(1)}, bf16[2,256,256]{2,1,0:T(8,128)(2,1)}, u32[]{:S(2)}) copy-start(bf16[2,256,256]{2,1,0:T(8,128)(2,1)} %constant.28.clone.refs_7_.forward) | copy-start | bytes 786436
  25.1 1.6 %copy-start.3 = (bf16[2,256,128]{2,1,0:T(8,128)(2,1)S(1)}, bf16[2,256,128]{2,1,0:T(8,128)(2,1)}, u32[]{:S(2)}) copy-start(bf16[2,256,128]{2,1,0:T(8,128)(2,1)} %constant.24.clone.refs_4_.first) | copy-start | bytes 393220
  25.1 1.6 %copy-start.8 = (f32[2,8,128]{2,1,0:T(8,128)S(1)}, f32[2,8,128]{2,1,0:T(8,128)}, u32[]{:S(2)}) copy-start(f32[2,8,128]{2,1,0:T(8,128)} %constant.27.clone.refs_6_.small) | copy-start | bytes 24580
  25.2 8.2 %collective-permute-start.11 = (bf16[128,512]{1,0:T(8,128)(2,1)S(1)}, bf16[128,512]{1,0:T(8,128)(2,1)S(1)}, u32[]{:S(2)}, u32[]{:S(2)}) collective-permute-start(bf16[128,512]{1,0:T(8,128)(2,1)S(1)} %shard_map.118.own_ref), channel_id=1, source_target_pairs={{0,16},{16,0},{1,17},{17,1},{2,18},{18,2},{3,19},{19,3},{4,20},{20... | collective-permute-start | bytes 393224 | tf_op jit(solution)/shard_map/ppermute | solution.py:364
  31.0 1.2 %copy-start.4 = (bf16[2,256,256]{2,1,0:T(8,128)(2,1)S(1)}, bf16[2,256,256]{2,1,0:T(8,128)(2,1)}, u32[]{:S(2)}) copy-start(bf16[2,256,256]{2,1,0:T(8,128)(2,1)} %constant.29.clone.inverse) | copy-start | bytes 786436
  31.0 1.2 %copy-start.5 = (bf16[2,128,256]{2,1,0:T(8,128)(2,1)S(1)}, bf16[2,128,256]{2,1,0:T(8,128)(2,1)}, u32[]{:S(2)}) copy-start(bf16[2,128,256]{2,1,0:T(8,128)(2,1)} %constant.25.clone.last) | copy-start | bytes 393220
  33.3 2.9 %collective-permute-start.20 = (bf16[4,16,1024]{2,1,0:T(8,128)(2,1)S(1)}, bf16[4,16,1024]{2,1,0:T(8,128)(2,1)S(1)}, u32[]{:S(2)}, u32[]{:S(2)}) collective-permute-start(bf16[4,16,1024]{2,1,0:T(8,128)(2,1)S(1)} %get-tuple-element.39), channel_id=1, source_target_pairs={{0,2},{2,0},{4,6},{6,4},{8,10},{10,8},{12,14},{14,12},{1,3},{3,1},... | collective-permute-start | bytes 393224 | tf_op jit(solution)/shard_map/ppermute | solution.py:360
  34.6 14.0 %collective-permute-start.19 = (bf16[4,16,1024]{2,1,0:T(8,128)(2,1)S(1)}, bf16[4,16,1024]{2,1,0:T(8,128)(2,1)S(1)}, u32[]{:S(2)}, u32[]{:S(2)}) collective-permute-start(bf16[4,16,1024]{2,1,0:T(8,128)(2,1)S(1)} %get-tuple-element.38.mine_ref), channel_id=1, source_target_pairs={{0,16},{16,0},{1,17},{17,1},{2,18},{18,2},{3,19},{19,3},{4,20},{20... | collective-permute-start | bytes 393224 | tf_op jit(solution)/shard_map/ppermute | solution.py:364
  36.1 12.5 %collective-permute-start.21 = (bf16[4,16,1024]{2,1,0:T(8,128)(2,1)S(1)}, bf16[4,16,1024]{2,1,0:T(8,128)(2,1)S(1)}, u32[]{:S(2)}, u32[]{:S(2)}) collective-permute-start(bf16[4,16,1024]{2,1,0:T(8,128)(2,1)S(1)} %collective-permute-done.20.near_ref), channel_id=1, source_target_pairs={{0,16},{16,0},{1,17},{17,1},{2,18},{18,2},{3,19},{19,3},{4,20},{20... | collective-permute-start | bytes 393224 | tf_op jit(solution)/shard_map/ppermute | solution.py:364
  37.7 4.9 %collective-permute-start.12 = (bf16[2,16,1024]{2,1,0:T(8,128)(2,1)S(1)}, bf16[2,16,1024]{2,1,0:T(8,128)(2,1)S(1)}, u32[]{:S(2)}, u32[]{:S(2)}) collective-permute-start(bf16[2,16,1024]{2,1,0:T(8,128)(2,1)S(1)} %get-tuple-element.35), channel_id=1, source_target_pairs={{0,4},{2,6},{4,0},{6,2},{8,12},{10,14},{12,8},{14,10},{1,5},{3,7},... | collective-permute-start | bytes 196616 | tf_op jit(solution)/shard_map/ppermute | solution.py:370
  39.9 8.1 %collective-permute-start.13 = (bf16[2,16,1024]{2,1,0:T(8,128)(2,1)S(1)}, bf16[2,16,1024]{2,1,0:T(8,128)(2,1)S(1)}, u32[]{:S(2)}, u32[]{:S(2)}) collective-permute-start(bf16[2,16,1024]{2,1,0:T(8,128)(2,1)S(1)} %get-tuple-element.36), channel_id=1, source_target_pairs={{0,8},{2,10},{4,12},{6,14},{8,0},{10,2},{12,4},{14,6},{1,9},{3,11}... | collective-permute-start | bytes 196616 | tf_op jit(solution)/shard_map/ppermute | solution.py:370
  41.2 6.9 %collective-permute-start.14 = (bf16[2,16,1024]{2,1,0:T(8,128)(2,1)S(1)}, bf16[2,16,1024]{2,1,0:T(8,128)(2,1)S(1)}, u32[]{:S(2)}, u32[]{:S(2)}) collective-permute-start(bf16[2,16,1024]{2,1,0:T(8,128)(2,1)S(1)} %get-tuple-element.37), channel_id=1, source_target_pairs={{0,12},{2,14},{4,8},{6,10},{8,4},{10,6},{12,0},{14,2},{1,13},{3,15... | collective-permute-start | bytes 196616 | tf_op jit(solution)/shard_map/ppermute | solution.py:370
  42.6 7.5 %collective-permute-start.15 = (bf16[2,16,1024]{2,1,0:T(8,128)(2,1)S(1)}, bf16[2,16,1024]{2,1,0:T(8,128)(2,1)S(1)}, u32[]{:S(2)}, u32[]{:S(2)}) collective-permute-start(bf16[2,16,1024]{2,1,0:T(8,128)(2,1)S(1)} %get-tuple-element.34.refs_0_), channel_id=1, source_target_pairs={{0,2},{2,0},{4,6},{6,4},{8,10},{10,8},{12,14},{14,12},{1,3},{3,1},... | collective-permute-start | bytes 196616 | tf_op jit(solution)/shard_map/ppermute | solution.py:360
  48.0 3.5 %collective-permute-start.16 = (bf16[2,16,1024]{2,1,0:T(8,128)(2,1)S(1)}, bf16[2,16,1024]{2,1,0:T(8,128)(2,1)S(1)}, u32[]{:S(2)}, u32[]{:S(2)}) collective-permute-start(bf16[2,16,1024]{2,1,0:T(8,128)(2,1)S(1)} %collective-permute-done.12.refs_1_), channel_id=1, source_target_pairs={{0,2},{2,0},{4,6},{6,4},{8,10},{10,8},{12,14},{14,12},{1,3},{3,1},... | collective-permute-start | bytes 196616 | tf_op jit(solution)/shard_map/ppermute | solution.py:360
  48.0 5.1 %collective-permute-start.17 = (bf16[2,16,1024]{2,1,0:T(8,128)(2,1)S(1)}, bf16[2,16,1024]{2,1,0:T(8,128)(2,1)S(1)}, u32[]{:S(2)}, u32[]{:S(2)}) collective-permute-start(bf16[2,16,1024]{2,1,0:T(8,128)(2,1)S(1)} %collective-permute-done.13.refs_2_), channel_id=1, source_target_pairs={{0,2},{2,0},{4,6},{6,4},{8,10},{10,8},{12,14},{14,12},{1,3},{3,1},... | collective-permute-start | bytes 196616 | tf_op jit(solution)/shard_map/ppermute | solution.py:360
  48.5 4.6 %collective-permute-start.18 = (bf16[2,16,1024]{2,1,0:T(8,128)(2,1)S(1)}, bf16[2,16,1024]{2,1,0:T(8,128)(2,1)S(1)}, u32[]{:S(2)}, u32[]{:S(2)}) collective-permute-start(bf16[2,16,1024]{2,1,0:T(8,128)(2,1)S(1)} %collective-permute-done.14.refs_3_), channel_id=1, source_target_pairs={{0,2},{2,0},{4,6},{6,4},{8,10},{10,8},{12,14},{14,12},{1,3},{3,1},... | collective-permute-start | bytes 196616 | tf_op jit(solution)/shard_map/ppermute | solution.py:360
  48.7 5.5 %collective-permute-start.22 = (bf16[2,16,1024]{2,1,0:T(8,128)(2,1)S(1)}, bf16[2,16,1024]{2,1,0:T(8,128)(2,1)S(1)}, u32[]{:S(2)}, u32[]{:S(2)}) collective-permute-start(bf16[2,16,1024]{2,1,0:T(8,128)(2,1)S(1)} %get-tuple-element.41), channel_id=1, source_target_pairs={{0,4},{2,6},{4,0},{6,2},{8,12},{10,14},{12,8},{14,10},{1,5},{3,7},... | collective-permute-start | bytes 196616 | tf_op jit(solution)/shard_map/ppermute | solution.py:370
  50.0 8.3 %collective-permute-start.23 = (bf16[2,16,1024]{2,1,0:T(8,128)(2,1)S(1)}, bf16[2,16,1024]{2,1,0:T(8,128)(2,1)S(1)}, u32[]{:S(2)}, u32[]{:S(2)}) collective-permute-start(bf16[2,16,1024]{2,1,0:T(8,128)(2,1)S(1)} %get-tuple-element.42), channel_id=1, source_target_pairs={{0,8},{2,10},{4,12},{6,14},{8,0},{10,2},{12,4},{14,6},{1,9},{3,11}... | collective-permute-start | bytes 196616 | tf_op jit(solution)/shard_map/ppermute | solution.py:370
  51.6 6.8 %collective-permute-start.24 = (bf16[2,16,1024]{2,1,0:T(8,128)(2,1)S(1)}, bf16[2,16,1024]{2,1,0:T(8,128)(2,1)S(1)}, u32[]{:S(2)}, u32[]{:S(2)}) collective-permute-start(bf16[2,16,1024]{2,1,0:T(8,128)(2,1)S(1)} %get-tuple-element.43), channel_id=1, source_target_pairs={{0,12},{2,14},{4,8},{6,10},{8,4},{10,6},{12,0},{14,2},{1,13},{3,15... | collective-permute-start | bytes 196616 | tf_op jit(solution)/shard_map/ppermute | solution.py:370
